TPU v7x, 32 devices: a whole 2x2x4 slice. The times are simulated.
32 devices in a mesh: parts: 2 (over x), space: 16 (over z, y, core).
Axes of the slice: x: 2, y: 2, z: 4, core: 2. Of those that a mesh axis runs over, the one named last changes fastest.
Arguments:
- coefficients: bfloat16 [64, 4096], P('parts'), parts along dimension 0, may hold values from -6 to 6
- kl_modes: bfloat16 [8192, 2048], P('parts', 'space'), parts along dimension 0, may hold values from -0.09375 to 0.09375
- green: bfloat16 [4096, 256, 128], P(('parts', 'space')), parts along dimension 0, may hold values from -0.1875 to 0.1875
- sub_index: int32 [4096], P('parts'), parts along dimension 0, may hold values from 0 to 2047, each once
- kernel: float32 [33, 33], replicated, may hold values from 0.2 to 5
- wet_mask: int32 [512, 128], P(('parts', 'space')), parts along dimension 0, may hold values 0 or 1
Outputs:
- surface: float32 [64, 256, 128], P('parts', 'space'), parts along dimension 0
There are 2 independent parts, one for each index of `parts`. A program takes and returns all parts, laid end to end along the dimension named above; an argument that names none is the same for every part. Nothing has to cross between parts.
Inputs may be any that keep to these rules, and one draw needn't show every extreme that they name: `sub_index`: each subfault appears once.
All inputs are finite; a program needn't handle non-finite values. No bound on the sum of `wet_mask` on one device may be relied on, other than what follows from the above.
Results may differ from a plain program's by a relative error of at most 0.005.
Values may be sent and summed in bfloat16 or wider, within the bound.
No kernel may reach another device: no remote copies, remote signals or barrier semaphores. Data moves between devices by JAX's collectives and lax.ppermute only.
A program may use at most 128 MiB of HBM per device.

v0:
```python
import jax
import jax.numpy as jnp
from jax import lax
from jax.sharding import PartitionSpec as P


def with_halo(block, sides, width):
    for axis, dim in sides:
        count = lax.axis_size(axis)
        forward = [(i, i + 1) for i in range(count - 1)]
        backward = [(target, source) for source, target in forward]
        low = lax.ppermute(
            lax.slice_in_dim(block, block.shape[dim] - width, None, axis=dim), axis, forward
        )
        high = lax.ppermute(lax.slice_in_dim(block, 0, width, axis=dim), axis, backward)
        block = jnp.concatenate([low, block, high], axis=dim)
    return block


def make_bands(weights, width):
    half = weights.shape[1] // 2
    source = lax.broadcasted_iota(jnp.int32, (width, width), 0)
    target = lax.broadcasted_iota(jnp.int32, (width, width), 1)
    offset = source - target + half
    inside = (offset >= 0) & (offset <= 2 * half)
    picked = jnp.take(weights, jnp.clip(offset, 0, 2 * half), axis=1)
    return jnp.where(inside[None], picked, jnp.zeros_like(picked))


def on_device(coefficients, kl_modes, green, sub_index, kernel, wet_mask):
    realizations = coefficients.shape[0]
    group = green.shape[0]
    width = green.shape[2]
    rows_here = wet_mask.shape[0]
    field = jnp.dot(coefficients, kl_modes, preferred_element_type=jnp.float32)
    slip = jnp.exp(0.5 * field).astype(jnp.bfloat16)
    slip_all = lax.all_gather(slip, "space", axis=1, tiled=True)
    row_ids = lax.dynamic_slice_in_dim(sub_index, lax.axis_index("space") * group, group)
    slip_rows = jnp.take(slip_all, row_ids, axis=1)
    partial_value = jnp.dot(slip_rows, green.reshape(group, -1), preferred_element_type=jnp.float32)
    partial_value = partial_value.reshape(realizations, green.shape[1], width)
    uplift = lax.psum_scatter(partial_value, "space", scatter_dimension=1, tiled=True)
    seafloor = uplift.astype(jnp.bfloat16)
    taps = kernel.shape[0]
    half = taps // 2
    weights = (kernel / jnp.sum(kernel)).astype(jnp.bfloat16).astype(jnp.float32)
    bands = make_bands(weights, width).astype(jnp.bfloat16).reshape(taps * width, width)
    padded = with_halo(seafloor, (("space", 1),), half)
    windows = jnp.concatenate(
        [padded[:, shift_row : shift_row + rows_here, :] for shift_row in range(taps)], axis=2
    )
    smooth = jnp.dot(
        windows.reshape(realizations * rows_here, taps * width),
        bands,
        preferred_element_type=jnp.float32,
    )
    smooth = smooth.reshape(realizations, rows_here, width)
    return smooth * wet_mask.astype(jnp.float32)[None]


def solution(mesh):
    placed = (
        P("parts", None),
        P("parts", "space"),
        P(("parts", "space"), None, None),
        P("parts"),
        P(),
        P(("parts", "space"), None),
    )
    return jax.shard_map(
        on_device, mesh=mesh, in_specs=placed, out_specs=P("parts", "space", None), check_vma=False
    )
```

profile of v0, /device:TPU:1, one launch (start us, length us, event | category | flops | bytes accessed | tf_op | source)
XLA Modules:
  0.0 168.3 jit_solution(8644153561037456515)
XLA Ops:
  6.5 0.0 copy-start
  6.5 0.0 reduce-scatter.2.cloned.1.call-start
  6.5 13.8 %copy.24 = bf16[16,8,256,128]{3,1,2,0:T(8,128)(2,1)} copy(bf16[16,8,256,128]{3,2,1,0:T(8,128)(2,1)} %bitcast.28) | data formatting | bytes 16777216
  20.3 0.0 copy-start.2
  20.3 12.0 %copy.12 = bf16[32768,128]{1,0:T(8,128)(2,1)} copy(bf16[32768,128]{0,1:T(8,128)(2,1)} %bitcast.27) | data formatting | bytes 16777216 | tf_op jit(solution)/shard_map/dot_general | solution.py:40
  32.3 0.0 copy-done
  32.3 0.0 copy-done.2
  32.3 0.5 fusion.2
  32.9 24.5 %all_gather.3 = bf16[32,2048]{0,1:T(8,128)(2,1)S(1)} all-gather(bf16[32,128]{0,1:T(8,128)(2,1)S(1)} %fusion.2), channel_id=1, replica_groups=mesh['parts'=2,'space'=16] {'space'}, dimensions={1}, use_global_device_ids=true | all-gather | bytes 139264 | tf_op jit(solution)/shard_map/all_gather | solution.py:37
  57.3 0.8 compare_and_fusion
  58.1 0.7 gather_fusion
  58.8 0.0 copy-start.3
  58.8 8.4 %fusion.69 = f32[32,256,128]{2,0,1:T(8,128)} fusion(bf16[256,128,128]{2,1,0:T(8,128)(2,1)} %bitcast.26, bf16[128,32]{1,0:T(8,128)(2,1)S(1)} %gather_fusion, pred[128]{0:T(512)(128)(4,1)S(1)} %get-tuple-element.5), kind=kOutput, calls=%fused_computation.139 | convolution fusion | flops 268439552 | bytes 12591232 | tf_op jit(solution)/shard_map/dot_general | solution.py:40
  67.2 0.0 reduce-scatter.2.cloned.1.call-update
  67.2 0.0 copy-done.3
  67.3 0.1 copy.14
  67.4 0.6 reduce_sum.9
  68.0 0.7 fusion.74
  68.7 57.8 %gather_fusion.1 = bf16[16384,33]{1,0:T(8,128)(2,1)} fusion(bf16[33,33]{0,1:T(8,128)(2,1)S(1)} %fusion.74, s32[16384]{0:T(1024)S(1)} %fusion.62), kind=kCustom, calls=%fused_computation.1 | custom fusion | bytes 2228224 | tf_op jit(solution)/shard_map/jit(_take)/gather | solution.py:26
  126.5 0.1 fusion.67
  126.5 8.9 %reduce-scatter.2.cloned.1.call-done = f32[32,16,128]{2,0,1:T(8,128)} async-done(((f32[32,256,128]{2,0,1:T(8,128)}), f32[32,16,128]{2,0,1:T(8,128)}) %reduce-scatter.2.cloned.1.call-update) | async-done | bytes 262160 | tf_op jit(solution)/shard_map/reduce_scatter | solution.py:42
  135.4 1.0 convert_element_type.25
  136.4 4.2 %collective-permute-start = (bf16[32,16,128]{2,0,1:T(8,128)(2,1)S(1)}, bf16[32,16,128]{2,0,1:T(8,128)(2,1)S(1)}, u32[]{:S(2)}, u32[]{:S(2)}) collective-permute-start(bf16[32,16,128]{2,0,1:T(8,128)(2,1)S(1)} %convert_element_type.25), channel_id=1, source_target_pairs={{0,1},{1,2},{2,3},{3,4},{4,5},{5,6},{6,7},{7,8},{8,9},{9,10},{10,1... | collective-permute-start | bytes 393224 | tf_op jit(solution)/shard_map/ppermute | solution.py:12
  140.5 7.5 %fusion = bf16[33,128,128]{0,2,1:T(8,128)(2,1)} fusion(bf16[128,128,33]{2,1,0:T(8,128)(2,1)} %bitcast.29, pred[128,128]{1,0:T(8,128)(4,1)S(1)} %get-tuple-element.8, pred[128,128]{1,0:T(8,128)(4,1)S(1)} %get-tuple-element.7), kind=kLoop, calls=%fused_computation.4 | loop fusion | flops 1081344 | bytes 2195456 | tf_op jit(solution)/shard_map/convert_element_type | solution.py:47
  148.0 0.0 copy-start.4
  148.0 4.2 %copy.15 = bf16[33,128,128]{2,1,0:T(8,128)(2,1)S(1)} copy(bf16[33,128,128]{0,2,1:T(8,128)(2,1)} %fusion) | data formatting | bytes 2162688 | tf_op jit(solution)/shard_map/convert_element_type | solution.py:47
  152.2 0.0 copy-done.4
  152.2 0.0 copy-start.1
  152.2 2.1 %collective-permute-start.1 = (bf16[32,16,128]{2,0,1:T(8,128)(2,1)S(1)}, bf16[32,16,128]{2,0,1:T(8,128)(2,1)S(1)}, u32[]{:S(2)}, u32[]{:S(2)}) collective-permute-start(bf16[32,16,128]{2,0,1:T(8,128)(2,1)S(1)} %convert_element_type.25), channel_id=1, source_target_pairs={{1,0},{2,1},{3,2},{4,3},{5,4},{6,5},{7,6},{8,7},{9,8},{10,9},{11,1... | collective-permute-start | bytes 393224 | tf_op jit(solution)/shard_map/ppermute | solution.py:15
  154.3 0.0 collective-permute-done
  154.9 0.0 copy-done.1
  155.0 3.6 %collective-permute-done.1 = bf16[32,16,128]{2,0,1:T(8,128)(2,1)S(1)} collective-permute-done((bf16[32,16,128]{2,0,1:T(8,128)(2,1)S(1)}, bf16[32,16,128]{2,0,1:T(8,128)(2,1)S(1)}, u32[]{:S(2)}, u32[]{:S(2)}) %collective-permute-start.1) | collective-permute-done | bytes 131104 | tf_op jit(solution)/shard_map/ppermute | solution.py:15
  159.3 1.3 fusion.76
  160.6 0.9 copy_multiply_fusion
  (36 shorter events, 1.1 us)
Async XLA Ops:
  6.5 25.8 %copy-start = (bf16[4096,128]{1,0:T(8,128)(2,1)S(1)}, bf16[4096,128]{1,0:T(8,128)(2,1)}, u32[]{:S(2)}) copy-start(bf16[4096,128]{1,0:T(8,128)(2,1)} %param.7) | copy-start | bytes 3145732
  6.5 128.8 %reduce-scatter.2.cloned.1.call-start = ((), (), s32[]{:S(2)}) async-start(), calls=%async_computation.1 | async-start | bytes 4456448 | tf_op jit(solution)/shard_map/reduce_scatter | solution.py:42
  20.3 12.0 %copy-start.2 = (bf16[32,4096]{1,0:T(8,128)(2,1)S(1)}, bf16[32,4096]{1,0:T(8,128)(2,1)}, u32[]{:S(2)}) copy-start(bf16[32,4096]{1,0:T(8,128)(2,1)} %param.6) | copy-start | bytes 786436
  58.8 8.4 %copy-start.3 = (f32[33,33]{1,0:T(8,128)S(1)}, f32[33,33]{1,0:T(8,128)}, u32[]{:S(2)}) copy-start(f32[33,33]{1,0:T(8,128)} %param.10) | copy-start | bytes 13072
  136.4 17.9 %collective-permute-start = (bf16[32,16,128]{2,0,1:T(8,128)(2,1)S(1)}, bf16[32,16,128]{2,0,1:T(8,128)(2,1)S(1)}, u32[]{:S(2)}, u32[]{:S(2)}) collective-permute-start(bf16[32,16,128]{2,0,1:T(8,128)(2,1)S(1)} %convert_element_type.25), channel_id=1, source_target_pairs={{0,1},{1,2},{2,3},{3,4},{4,5},{5,6},{6,7},{7,8},{8,9},{9,10},{10,1... | collective-permute-start | bytes 393224 | tf_op jit(solution)/shard_map/ppermute | solution.py:12
  148.0 4.2 %copy-start.4 = (s32[16,128]{1,0:T(8,128)S(1)}, s32[16,128]{1,0:T(8,128)}, u32[]{:S(2)}) copy-start(s32[16,128]{1,0:T(8,128)} %param.11) | copy-start | bytes 24580
  152.2 2.7 %copy-start.1 = (f32[32,16,128]{2,0,1:T(8,128)S(1)}, f32[32,16,128]{2,0,1:T(8,128)}, u32[]{:S(2)}) copy-start(f32[32,16,128]{2,0,1:T(8,128)} %reduce-scatter.2.cloned.1.call-done) | copy-start | bytes 786436
  152.2 6.4 %collective-permute-start.1 = (bf16[32,16,128]{2,0,1:T(8,128)(2,1)S(1)}, bf16[32,16,128]{2,0,1:T(8,128)(2,1)S(1)}, u32[]{:S(2)}, u32[]{:S(2)}) collective-permute-start(bf16[32,16,128]{2,0,1:T(8,128)(2,1)S(1)} %convert_element_type.25), channel_id=1, source_target_pairs={{1,0},{2,1},{3,2},{4,3},{5,4},{6,5},{7,6},{8,7},{9,8},{10,9},{11,1... | collective-permute-start | bytes 393224 | tf_op jit(solution)/shard_map/ppermute | solution.py:15
Sparse Core Ops, SparseCore 0:
  67.4 67.9 reduce-scatter.1
where the time goes:
time: 169 us; the launch traced here: 168 us
  local copies, waits for them, and re-layouts  88.6 us (52%)
  blocking collectives  24.5 us (14%)
  between operations  13.8 us (8%)
  other arithmetic  12.5 us (7%)
  waiting for transfers between devices  12.5 us (7%)
  matrix products  10.2 us (6%)
  starting transfers between devices  6.22 us (4%)
    gather x1, local copies, waits for them, and re-layouts, make_bands(): picked = jnp.take(weights, jnp.clip(offset, 0, 2 * half), axis=1)  57.8 us
    all_gather x1, blocking collectives, on_device(): slip_all = lax.all_gather(slip, 'space', axis=1, tiled=True)  24.5 us
    unnamed x13, local copies, waits for them, and re-layouts  13.9 us
    dot_general x1, local copies, waits for them, and re-layouts, on_device(): jnp.dot(slip_rows, green.reshape(group, -1), preferred_element_type=jnp.f...  12 us
    reduce_scatter x1, waiting for transfers between devices, on_device(): lax.psum_scatter(partial_value, 'space', scatter_dimension=1, tiled=True)  8.86 us
    dot_general x1, matrix products, on_device(): jnp.dot(slip_rows, green.reshape(group, -1), preferred_element_type=jnp.f...  8.41 us
    convert_element_type x1, other arithmetic, on_device(): make_bands(weights, width).astype(jnp.bfloat16).reshape(taps * width, width)  7.48 us
    ppermute x1, starting transfers between devices, with_halo(): lax.ppermute(lax.slice_in_dim(block, block.shape[dim] - width, None, axis...  4.17 us
  transfers between devices with their start and end apart: 3, of which 2 were waited for; matrix products, arithmetic and copies ran while one was open for 42% of the time, Pallas kernels for 0%

commit v1 on v0

v1 whole, which is shorter than its diff:
```python
import functools

import jax
import jax.numpy as jnp
from jax import lax
from jax.experimental import pallas as pl
from jax.experimental.pallas import tpu as pltpu
from jax.sharding import PartitionSpec as P

VMEM = pl.BlockSpec(memory_space=pltpu.VMEM)


def swap(block, bit):
    count = lax.axis_size("space")
    return lax.ppermute(block, "space", [(i, i ^ bit) for i in range(count)])


def select_kernel(position_ref, slip_ref, spread_ref):
    owners, realizations, columns = slip_ref.shape
    group = position_ref.shape[1]
    rows = spread_ref.shape[0] // realizations
    picked = jnp.zeros((realizations, group), jnp.float32)
    for owner in range(owners):
        column = lax.broadcasted_iota(jnp.int32, (columns, group), 0) + owner * columns
        chosen = jnp.where(column == position_ref[...], 1.0, 0.0).astype(jnp.bfloat16)
        picked += jnp.dot(slip_ref[owner], chosen, preferred_element_type=jnp.float32)
    source = lax.broadcasted_iota(jnp.int32, (group, group * rows), 0)
    target = lax.broadcasted_iota(jnp.int32, (group, group * rows), 1)
    repeat = jnp.where(target // rows == source, 1.0, 0.0).astype(jnp.bfloat16)
    wide = jnp.dot(picked.astype(jnp.bfloat16), repeat, preferred_element_type=jnp.float32)
    row_of = lax.broadcasted_iota(jnp.int32, wide.shape, 1) % rows
    for row in range(rows):
        spread_ref[row * realizations : (row + 1) * realizations, :] = jnp.where(
            row_of == row, wide, 0.0
        ).astype(jnp.bfloat16)


def uplift_kernel(table_ref, spread_ref, first_ref, second_ref, out_ref):
    depth = spread_ref.shape[1]
    width = first_ref.shape[2]
    both = jnp.concatenate(
        [first_ref[...].reshape(depth, width), second_ref[...].reshape(depth, width)], axis=1
    )
    value = jnp.dot(spread_ref[...], both, preferred_element_type=jnp.float32)
    for side in range(2):
        part = value[:, side * width : (side + 1) * width]
        out_ref[side] = part.reshape(out_ref.shape[1:]).astype(out_ref.dtype)


def partial_uplift(table, spread, green, rows, realizations, dtype):
    group, _, width = green.shape
    count = table.shape[0]
    return pl.pallas_call(
        uplift_kernel,
        out_shape=jax.ShapeDtypeStruct((count, rows, realizations, width), dtype),
        grid_spec=pltpu.PrefetchScalarGridSpec(
            num_scalar_prefetch=1,
            grid=(count // 2,),
            in_specs=[
                VMEM,
                pl.BlockSpec((group, rows, width), lambda i, table: (0, table[2 * i], 0)),
                pl.BlockSpec((group, rows, width), lambda i, table: (0, table[2 * i + 1], 0)),
            ],
            out_specs=pl.BlockSpec((2, rows, realizations, width), lambda i, table: (i, 0, 0, 0)),
        ),
        cost_estimate=pl.CostEstimate(
            flops=2 * count * rows * rows * realizations * group * width,
            bytes_accessed=count * rows * width * (2 * group + 4 * realizations),
            transcendentals=0,
        ),
    )(table, spread, green, green)


def bands_kernel(taps, weights_ref, bands_ref):
    half = taps // 2
    width = weights_ref.shape[1]
    source = lax.broadcasted_iota(jnp.int32, (width, width), 0)
    target = lax.broadcasted_iota(jnp.int32, (width, width), 1)
    inside = jnp.abs(source - target) <= half
    for tap in range(-1, taps + 1):
        if 0 <= tap < taps:
            line = jnp.broadcast_to(weights_ref[tap : tap + 1, :], (width, width))
            rolled = pltpu.roll(line, width - half, 1, stride=1, stride_axis=0)
            band = jnp.where(inside, rolled, 0.0).astype(jnp.bfloat16)
        else:
            band = jnp.zeros((width, width), jnp.bfloat16)
        if tap >= 0:
            bands_ref[tap * width : (tap + 1) * width, :width] = band
        if tap < taps:
            bands_ref[(tap + 1) * width : (tap + 2) * width, width:] = band


def smooth_kernel(low_ref, own_ref, high_ref, bands_ref, mask_ref, out_ref, lines_ref):
    half = low_ref.shape[0]
    rows, realizations, width = own_ref.shape

    def row_at(index):
        if index < half:
            return low_ref[index]
        if index < half + rows:
            return own_ref[index - half]
        return high_ref[index - half - rows]

    for shift in range(2 * half + 2):
        for pair in range(rows // 2):
            lines_ref[
                pair * realizations : (pair + 1) * realizations,
                shift * width : (shift + 1) * width,
            ] = row_at(2 * pair + shift)
    value = jnp.dot(lines_ref[...], bands_ref[...], preferred_element_type=jnp.float32)
    value = value.reshape(rows // 2, realizations, 2 * width)
    both = jnp.stack([value[:, :, :width], value[:, :, width:]], axis=1)
    both = both.reshape(rows, realizations, width)
    mask = mask_ref[...].astype(jnp.float32)
    out_ref[...] = jnp.transpose(both, (1, 0, 2)) * mask[None]


def reduce_halves(block, axes):
    bits = {axis: 1 << (block.ndim - 3 - axis) for axis in range(block.ndim - 3)}
    done = []
    for axis in axes:
        place = axis - sum(1 for earlier in done if earlier < axis)
        away = lax.index_in_dim(block, 1, place, keepdims=False).astype(jnp.bfloat16)
        kept = lax.index_in_dim(block, 0, place, keepdims=False)
        block = kept + swap(away, bits[axis]).astype(jnp.float32)
        done.append(axis)
    return block


def on_device(coefficients, kl_modes, green, sub_index, kernel, wet_mask):
    realizations = coefficients.shape[0]
    columns = kl_modes.shape[1]
    group, _, width = green.shape
    rows = wet_mask.shape[0]
    taps = kernel.shape[0]
    half = taps // 2
    count = lax.axis_size("space")
    me = lax.axis_index("space")
    levels = count.bit_length() - 1
    assert 1 << levels == count and half <= rows and levels >= 3

    field = jnp.dot(coefficients, kl_modes, preferred_element_type=jnp.float32)
    slip = jnp.exp(0.5 * field).astype(jnp.bfloat16)[None]
    for level in range(levels):
        slip = jnp.concatenate([slip, swap(slip, 1 << level)], axis=0)

    row_ids = lax.dynamic_slice_in_dim(sub_index, me * group, group)
    position = ((row_ids // columns) ^ me) * columns + row_ids % columns
    spread = pl.pallas_call(
        select_kernel,
        out_shape=jax.ShapeDtypeStruct((rows * realizations, group * rows), jnp.bfloat16),
        in_specs=[VMEM, VMEM],
        out_specs=VMEM,
    )(position[None], slip)

    order = 2 * jnp.arange(count // 2, dtype=jnp.int32)
    away = partial_uplift((order + 1) ^ me, spread, green, rows, realizations, jnp.bfloat16)
    kept = partial_uplift(order ^ me, spread, green, rows, realizations, jnp.float32)
    summed = kept + swap(away, 1).astype(jnp.float32)
    summed = summed.reshape((2,) * (levels - 1) + summed.shape[1:])
    below = levels - 2
    axes = list(range(below - 1, -1, -1))
    other = axes[1::-1] + axes[2:] if below >= 2 else axes
    first = reduce_halves(summed[0], axes)
    second = reduce_halves(summed[1], other)
    uplift = first + swap(second.astype(jnp.bfloat16), count // 2).astype(jnp.float32)
    seafloor = uplift.astype(jnp.bfloat16)

    low = lax.ppermute(seafloor[rows - half :], "space", [(i, i + 1) for i in range(count - 1)])
    high = lax.ppermute(seafloor[:half], "space", [(i + 1, i) for i in range(count - 1)])

    weights = (kernel / jnp.sum(kernel)).astype(jnp.bfloat16).astype(jnp.float32)
    lines = jnp.pad(weights[:, ::-1], ((0, -taps % 8), (0, width - taps)))
    bands = pl.pallas_call(
        functools.partial(bands_kernel, taps),
        out_shape=jax.ShapeDtypeStruct(((taps + 1) * width, 2 * width), jnp.bfloat16),
        in_specs=[VMEM],
        out_specs=VMEM,
    )(lines)
    return pl.pallas_call(
        smooth_kernel,
        out_shape=jax.ShapeDtypeStruct((realizations, rows, width), jnp.float32),
        in_specs=[VMEM] * 5,
        out_specs=VMEM,
        scratch_shapes=[
            pltpu.VMEM((rows // 2 * realizations, (taps + 1) * width), jnp.bfloat16)
        ],
    )(low, seafloor, high, bands, wet_mask)


def solution(mesh):
    placed = (
        P("parts", None),
        P("parts", "space"),
        P(("parts", "space"), None, None),
        P("parts"),
        P(),
        P(("parts", "space"), None),
    )
    return jax.shard_map(
        on_device, mesh=mesh, in_specs=placed, out_specs=P("parts", "space", None), check_vma=False
    )
```

time: 169 us -> 76.1 us (0.45)
  local copies, waits for them, and re-layouts: 88.6 us -> 3.57 us
  blocking collectives: 24.5 us -> 0 us
  Pallas kernels: 0 us -> 22.9 us
  starting transfers between devices: 6.22 us -> 25.2 us
  between operations: 13.8 us -> 0.15 us
  matrix products: 10.2 us -> 1.23 us
  other arithmetic: 12.5 us -> 5.82 us
  waiting for transfers between devices: 12.5 us -> 16.7 us
    gather x2 -> x0, local copies, waits for them, and re-layouts: 58.5 us -> none  [the longest x1 57.8 us: make_bands(): picked = jnp.take(weights, jnp.clip(offset, 0, 2 * half), axis=1)]
    all_gather x1 -> x0, blocking collectives: 24.5 us -> none  [on_device(): slip_all = lax.all_gather(slip, 'space', axis=1, tiled=True)]
    pallas_call x0 -> x5, Pallas kernels: none -> 22.9 us  [the longest x2 14.1 us: partial_uplift(): pl.pallas_call(uplift_kernel, out_shape=jax.ShapeDtypeStruct((count, rows...]
    ppermute x2 -> x12, starting transfers between devices: 6.22 us -> 25.2 us  [the longest x10 18.9 us: swap(): return lax.ppermute(block, 'space', [(i, i ^ bit) for i in range(count)])]
    ppermute x2 -> x12, waiting for transfers between devices: 3.64 us -> 16.7 us  [the longest x10 16.1 us: swap(): return lax.ppermute(block, 'space', [(i, i ^ bit) for i in range(count)])]
    dot_general x1 -> x0, local copies, waits for them, and re-layouts: 12 us -> none  [on_device(): jnp.dot(slip_rows, green.reshape(group, -1), preferred_element_type=jnp.f...]
    unnamed x13 -> x15, local copies, waits for them, and re-layouts: 13.9 us -> 2.68 us
    dot_general x2 -> x0, matrix products: 9.71 us -> none  [the longest x1 8.41 us: on_device(): jnp.dot(slip_rows, green.reshape(group, -1), preferred_element_type=jnp.f...]
  transfers between devices with their start and end apart: 3 -> 12, of which waited for: 2 -> 7; matrix products, arithmetic and copies ran while one was open for 42% -> 6% of each run, Pallas kernels for 0% -> 13%
where the time goes in v1:
time: 76.1 us; the launch traced here: 75.5 us
  starting transfers between devices  25.2 us (33%)
  Pallas kernels  22.9 us (30%)
  waiting for transfers between devices  16.7 us (22%)
  other arithmetic  5.82 us (8%)
  local copies, waits for them, and re-layouts  3.57 us (5%)
  matrix products  1.23 us (2%)
    ppermute x10, starting transfers between devices, swap(): return lax.ppermute(block, 'space', [(i, i ^ bit) for i in range(count)])  18.9 us
    ppermute x10, waiting for transfers between devices, swap(): return lax.ppermute(block, 'space', [(i, i ^ bit) for i in range(count)])  16.1 us
    pallas_call x2, Pallas kernels, partial_uplift(): pl.pallas_call(uplift_kernel, out_shape=jax.ShapeDtypeStruct((count, rows...  14.1 us
    ppermute x1, starting transfers between devices, on_device(): lax.ppermute(seafloor[rows - half:], 'space', [(i, i + 1) for i in range(...  4.35 us
    pallas_call x1, Pallas kernels, on_device(): pl.pallas_call(smooth_kernel, out_shape=jax.ShapeDtypeStruct((realization...  3.28 us
    pallas_call x1, Pallas kernels, on_device(): pl.pallas_call(select_kernel, out_shape=jax.ShapeDtypeStruct((rows * real...  3.01 us
    unnamed x15, local copies, waits for them, and re-layouts  2.68 us
    pallas_call x1, Pallas kernels, on_device(): pl.pallas_call(functools.partial(bands_kernel, taps), out_shape=jax.Shape...  2.46 us
  transfers between devices with their start and end apart: 12, of which 7 were waited for; matrix products, arithmetic and copies ran while one was open for 6% of the time, Pallas kernels for 13%

profile of v1, /device:TPU:1, one launch (start us, length us, event | category | flops | bytes accessed | tf_op | source)
XLA Modules:
  0.0 75.5 jit_solution(3730623383557889133)
XLA Ops:
  0.0 0.0 copy-start
  0.0 1.2 %copy-done = bf16[4096,128]{1,0:T(8,128)(2,1)S(1)} copy-done((bf16[4096,128]{1,0:T(8,128)(2,1)S(1)}, bf16[4096,128]{1,0:T(8,128)(2,1)}, u32[]{:S(2)}) %copy-start) | copy-done | bytes 1048600
  1.2 1.2 %constant_dynamic-update-slice_fusion.4 = (bf16[16,32,128]{2,1,0:T(8,128)(2,1)S(1)}, bf16[1,32,128]{2,1,0:T(8,128)(2,1)S(1)}) fusion(bf16[32,4096]{1,0:T(8,128)(2,1)} %param.6, bf16[4096,128]{1,0:T(8,128)(2,1)S(1)} %copy-done), kind=kOutput, calls=%fused_computation.30 | convolution fusion | flops 33562624 | bytes 1327104 | tf_op jit(solution)/shard_map/dot_general | solution.py:142
  2.5 0.1 collective-permute-start
  2.6 0.5 add_xor_fusion.table_ref
  3.1 1.4 %fusion.14.position_ref = s32[1,128]{1,0:T(1,128)} fusion(s32[2048]{0:T(1024)} %param.9, s32[]{:T(128)S(6)} %select_n.15, s32[]{:T(128)S(6)} %axis_index.12), kind=kLoop, calls=%fused_computation.39 | loop fusion | flops 2816 | bytes 1032 | tf_op jit(solution)/shard_map/broadcast_in_dim | solution.py:154
  4.4 0.0 collective-permute-done
  4.4 2.7 %collective-permute-start.1 = (bf16[2,32,128]{2,1,0:T(8,128)(2,1)S(1)}, bf16[2,32,128]{2,1,0:T(8,128)(2,1)S(1)}, u32[]{:S(2)}, u32[]{:S(2)}) collective-permute-start(bf16[2,32,128]{2,1,0:T(8,128)(2,1)S(1)} %pad_maximum_fusion.2), channel_id=1, source_target_pairs={{0,2},{1,3},{2,0},{3,1},{4,6},{5,7},{6,4},{7,5},{8,10},{9,11},{10,... | collective-permute-start | bytes 49160 | tf_op jit(solution)/shard_map/ppermute | solution.py:15
  7.2 1.1 %collective-permute-done.1 = bf16[2,32,128]{2,1,0:T(8,128)(2,1)S(1)} collective-permute-done((bf16[2,32,128]{2,1,0:T(8,128)(2,1)S(1)}, bf16[2,32,128]{2,1,0:T(8,128)(2,1)S(1)}, u32[]{:S(2)}, u32[]{:S(2)}) %collective-permute-start.1) | collective-permute-done | bytes 16416 | tf_op jit(solution)/shard_map/ppermute | solution.py:15
  8.3 1.5 %collective-permute-start.2 = (bf16[4,32,128]{2,1,0:T(8,128)(2,1)S(1)}, bf16[4,32,128]{2,1,0:T(8,128)(2,1)S(1)}, u32[]{:S(2)}, u32[]{:S(2)}) collective-permute-start(bf16[4,32,128]{2,1,0:T(8,128)(2,1)S(1)} %pad_maximum_fusion.1), channel_id=1, source_target_pairs={{0,4},{1,5},{2,6},{3,7},{4,0},{5,1},{6,2},{7,3},{8,12},{9,13},{10,... | collective-permute-start | bytes 98312 | tf_op jit(solution)/shard_map/ppermute | solution.py:15
  9.8 1.3 %collective-permute-done.2 = bf16[4,32,128]{2,1,0:T(8,128)(2,1)S(1)} collective-permute-done((bf16[4,32,128]{2,1,0:T(8,128)(2,1)S(1)}, bf16[4,32,128]{2,1,0:T(8,128)(2,1)S(1)}, u32[]{:S(2)}, u32[]{:S(2)}) %collective-permute-start.2) | collective-permute-done | bytes 32800 | tf_op jit(solution)/shard_map/ppermute | solution.py:15
  11.1 2.5 %collective-permute-start.3 = (bf16[8,32,128]{2,1,0:T(8,128)(2,1)S(1)}, bf16[8,32,128]{2,1,0:T(8,128)(2,1)S(1)}, u32[]{:S(2)}, u32[]{:S(2)}) collective-permute-start(bf16[8,32,128]{2,1,0:T(8,128)(2,1)S(1)} %pad_maximum_fusion), channel_id=1, source_target_pairs={{0,8},{1,9},{2,10},{3,11},{4,12},{5,13},{6,14},{7,15},{8,0},{9,1},... | collective-permute-start | bytes 196616 | tf_op jit(solution)/shard_map/ppermute | solution.py:15
  13.7 1.6 %collective-permute-done.3 = bf16[8,32,128]{2,1,0:T(8,128)(2,1)S(1)} collective-permute-done((bf16[8,32,128]{2,1,0:T(8,128)(2,1)S(1)}, bf16[8,32,128]{2,1,0:T(8,128)(2,1)S(1)}, u32[]{:S(2)}, u32[]{:S(2)}) %collective-permute-start.3) | collective-permute-done | bytes 65568 | tf_op jit(solution)/shard_map/ppermute | solution.py:15
  15.3 0.0 copy-start.2
  15.4 0.6 copy-done.2
  16.0 3.0 %shard_map.64.spread_ref = bf16[512,2048]{1,0:T(8,128)(2,1)} custom-call(s32[1,128]{1,0:T(1,128)} %fusion.14.position_ref, bf16[16,32,128]{2,1,0:T(8,128)(2,1)} %copy-done.2), custom_call_target="tpu_custom_call" | custom-call | tf_op jit(solution)/shard_map/pallas_call | solution.py:149
  19.0 7.0 %shard_map.66 = bf16[8,16,32,128]{3,2,1,0:T(8,128)(2,1)} custom-call(s32[8]{0:T(128)} %add_xor_fusion.table_ref, bf16[512,2048]{1,0:T(8,128)(2,1)} %shard_map.64.spread_ref, bf16[128,256,128]{2,1,0:T(8,128)(2,1)} %second_ref.3, bf16[128,256,128]{2,1,0:T(8,128)(2,1)} %second_ref.3), custom_call_target="tpu_custom_call" | custom-call | flops 2147483648 | bytes 6291456 | tf_op jit(solution)/shard_map/pallas_call | solution.py:53
  26.0 3.2 %collective-permute-start.4 = (bf16[8,16,32,128]{3,2,1,0:T(8,128)(2,1)}, bf16[8,16,32,128]{3,2,1,0:T(8,128)(2,1)S(1)}, u32[]{:S(2)}, u32[]{:S(2)}) collective-permute-start(bf16[8,16,32,128]{3,2,1,0:T(8,128)(2,1)} %shard_map.66), channel_id=1, source_target_pairs={{0,1},{1,0},{2,3},{3,2},{4,5},{5,4},{6,7},{7,6},{8,9},{9,8},{10,11... | collective-permute-start | bytes 3145736 | tf_op jit(solution)/shard_map/ppermute | solution.py:15
  29.2 0.5 fusion.15.table_ref
  29.7 7.2 %shard_map.65 = f32[8,16,32,128]{3,2,1,0:T(8,128)} custom-call(s32[8]{0:T(128)} %fusion.15.table_ref, bf16[512,2048]{1,0:T(8,128)(2,1)} %shard_map.64.spread_ref, bf16[128,256,128]{2,1,0:T(8,128)(2,1)} %second_ref.3, bf16[128,256,128]{2,1,0:T(8,128)(2,1)} %second_ref.3), custom_call_target="tpu_custom_call" | custom-call | flops 2147483648 | bytes 6291456 | tf_op jit(solution)/shard_map/pallas_call | solution.py:53
  36.8 0.0 collective-permute-done.4
  36.9 1.9 %convert_add_fusion = f32[8,16,32,128]{3,2,1,0:T(8,128)S(1)} fusion(f32[8,16,32,128]{3,2,1,0:T(8,128)} %shard_map.65, bf16[8,16,32,128]{3,2,1,0:T(8,128)(2,1)S(1)} %collective-permute-done.4), kind=kLoop, calls=%fused_computation | loop fusion | flops 1048576 | bytes 5242880 | tf_op jit(solution)/shard_map/add | solution.py:159
  38.8 1.7 %collective-permute-start.7 = (bf16[2,16,32,128]{3,2,1,0:T(8,128)(2,1)S(1)}, bf16[2,16,32,128]{3,2,1,0:T(8,128)(2,1)S(1)}, u32[]{:S(2)}, u32[]{:S(2)}) collective-permute-start(bf16[2,16,32,128]{3,2,1,0:T(8,128)(2,1)S(1)} %slice.76), channel_id=1, source_target_pairs={{0,4},{1,5},{2,6},{3,7},{4,0},{5,1},{6,2},{7,3},{8,12},{9,13},{10,... | collective-permute-start | bytes 786440 | tf_op jit(solution)/shard_map/ppermute | solution.py:15
  40.5 0.1 slice.47
  40.6 0.0 copy-start.5
  40.6 1.3 %collective-permute-start.5 = (bf16[2,16,32,128]{3,2,1,0:T(8,128)(2,1)S(1)}, bf16[2,16,32,128]{3,2,1,0:T(8,128)(2,1)S(1)}, u32[]{:S(2)}, u32[]{:S(2)}) collective-permute-start(bf16[2,16,32,128]{3,2,1,0:T(8,128)(2,1)S(1)} %fusion.4), channel_id=1, source_target_pairs={{0,2},{1,3},{2,0},{3,1},{4,6},{5,7},{6,4},{7,5},{8,10},{9,11},{10,... | collective-permute-start | bytes 786440 | tf_op jit(solution)/shard_map/ppermute | solution.py:15
  41.9 5.1 %collective-permute-done.7 = bf16[2,16,32,128]{3,2,1,0:T(8,128)(2,1)S(1)} collective-permute-done((bf16[2,16,32,128]{3,2,1,0:T(8,128)(2,1)S(1)}, bf16[2,16,32,128]{3,2,1,0:T(8,128)(2,1)S(1)}, u32[]{:S(2)}, u32[]{:S(2)}) %collective-permute-start.7) | collective-permute-done | bytes 262176 | tf_op jit(solution)/shard_map/ppermute | solution.py:15
  47.1 0.1 slice_add_fusion
  47.2 1.3 %collective-permute-start.8 = (bf16[16,32,128]{2,1,0:T(8,128)(2,1)S(1)}, bf16[16,32,128]{2,1,0:T(8,128)(2,1)S(1)}, u32[]{:S(2)}, u32[]{:S(2)}) collective-permute-start(bf16[16,32,128]{2,1,0:T(8,128)(2,1)S(1)} %fusion.11), channel_id=1, source_target_pairs={{0,2},{1,3},{2,0},{3,1},{4,6},{5,7},{6,4},{7,5},{8,10},{9,11},{10,... | collective-permute-start | bytes 393224 | tf_op jit(solution)/shard_map/ppermute | solution.py:15
  48.5 0.0 collective-permute-done.5
  48.5 0.1 fusion.3
  48.6 1.4 %collective-permute-start.6 = (bf16[16,32,128]{2,1,0:T(8,128)(2,1)S(1)}, bf16[16,32,128]{2,1,0:T(8,128)(2,1)S(1)}, u32[]{:S(2)}, u32[]{:S(2)}) collective-permute-start(bf16[16,32,128]{2,1,0:T(8,128)(2,1)S(1)} %fusion.10), channel_id=1, source_target_pairs={{0,4},{1,5},{2,6},{3,7},{4,0},{5,1},{6,2},{7,3},{8,12},{9,13},{10,... | collective-permute-start | bytes 393224 | tf_op jit(solution)/shard_map/ppermute | solution.py:15
  50.0 1.6 %collective-permute-done.8 = bf16[16,32,128]{2,1,0:T(8,128)(2,1)S(1)} collective-permute-done((bf16[16,32,128]{2,1,0:T(8,128)(2,1)S(1)}, bf16[16,32,128]{2,1,0:T(8,128)(2,1)S(1)}, u32[]{:S(2)}, u32[]{:S(2)}) %collective-permute-start.8) | collective-permute-done | bytes 131104 | tf_op jit(solution)/shard_map/ppermute | solution.py:15
  51.6 3.2 %collective-permute-start.9 = (bf16[16,32,128]{2,1,0:T(8,128)(2,1)S(1)}, bf16[16,32,128]{2,1,0:T(8,128)(2,1)S(1)}, u32[]{:S(2)}, u32[]{:S(2)}) collective-permute-start(bf16[16,32,128]{2,1,0:T(8,128)(2,1)S(1)} %fusion.6), channel_id=1, source_target_pairs={{0,8},{1,9},{2,10},{3,11},{4,12},{5,13},{6,14},{7,15},{8,0},{9,1},... | collective-permute-start | bytes 393224 | tf_op jit(solution)/shard_map/ppermute | solution.py:15
  54.8 0.6 reduce_sum.9
  55.5 0.0 collective-permute-done.6
  55.5 5.3 %collective-permute-done.9 = bf16[16,32,128]{2,1,0:T(8,128)(2,1)S(1)} collective-permute-done((bf16[16,32,128]{2,1,0:T(8,128)(2,1)S(1)}, bf16[16,32,128]{2,1,0:T(8,128)(2,1)S(1)}, u32[]{:S(2)}, u32[]{:S(2)}) %collective-permute-start.9) | collective-permute-done | bytes 131104 | tf_op jit(solution)/shard_map/ppermute | solution.py:15
  60.8 4.4 %collective-permute-start.10 = (bf16[16,32,128]{2,1,0:T(8,128)(2,1)S(1)}, bf16[16,32,128]{2,1,0:T(8,128)(2,1)S(1)}, u32[]{:S(2)}, u32[]{:S(2)}) collective-permute-start(bf16[16,32,128]{2,1,0:T(8,128)(2,1)S(1)} %fusion.9.own_ref), channel_id=1, source_target_pairs={{0,1},{1,2},{2,3},{3,4},{4,5},{5,6},{6,7},{7,8},{8,9},{9,10},{10,1... | collective-permute-start | bytes 393224 | tf_op jit(solution)/shard_map/ppermute | solution.py:169
  65.2 1.9 %collective-permute-start.11 = (bf16[16,32,128]{2,1,0:T(8,128)(2,1)S(1)}, bf16[16,32,128]{2,1,0:T(8,128)(2,1)S(1)}, u32[]{:S(2)}, u32[]{:S(2)}) collective-permute-start(bf16[16,32,128]{2,1,0:T(8,128)(2,1)S(1)} %fusion.9.own_ref), channel_id=1, source_target_pairs={{1,0},{2,1},{3,2},{4,3},{5,4},{6,5},{7,6},{8,7},{9,8},{10,9},{11,1... | collective-permute-start | bytes 393224 | tf_op jit(solution)/shard_map/ppermute | solution.py:170
  67.1 0.7 fusion.12
  67.8 0.1 rev.3
  67.9 0.6 pad.4.weights_ref
  68.5 2.5 %shard_map.67.bands_ref = bf16[4352,256]{1,0:T(8,128)(2,1)} custom-call(f32[40,128]{1,0:T(8,128)} %pad.4.weights_ref), custom_call_target="tpu_custom_call" | custom-call | tf_op jit(solution)/shard_map/pallas_call | solution.py:174
  71.0 0.0 collective-permute-done.10.low_ref
  71.0 0.5 collective-permute-done.11.high_ref
  71.5 0.1 copy-done.3
  71.6 0.6 copy-done.4
  72.3 3.3 %shard_map.68 = f32[32,16,128]{2,1,0:T(8,128)} custom-call(bf16[16,32,128]{2,1,0:T(8,128)(2,1)} %copy-done.3, bf16[16,32,128]{2,1,0:T(8,128)(2,1)} %copy-done.1, bf16[16,32,128]{2,1,0:T(8,128)(2,1)} %copy-done.4, bf16[4352,256]{1,0:T(8,128)(2,1)} %shard_map.67.bands_ref, s32[16,128]{1,0:T(8,128)} %mask_ref.1), custom_call_target="tpu_custom_call" | custom-call | tf_op jit(solution)/shard_map/pallas_call | solution.py:180
  (18 shorter events, 0.3 us)
Async XLA Ops:
  0.0 1.2 %copy-start = (bf16[4096,128]{1,0:T(8,128)(2,1)S(1)}, bf16[4096,128]{1,0:T(8,128)(2,1)}, u32[]{:S(2)}) copy-start(bf16[4096,128]{1,0:T(8,128)(2,1)} %param.7) | copy-start | bytes 3145732
  2.5 2.0 %collective-permute-start = (bf16[1,32,128]{2,1,0:T(8,128)(2,1)S(1)}, bf16[1,32,128]{2,1,0:T(8,128)(2,1)S(1)}, u32[]{:S(2)}, u32[]{:S(2)}) collective-permute-start(bf16[1,32,128]{2,1,0:T(8,128)(2,1)S(1)} %get-tuple-element.6), channel_id=1, source_target_pairs={{0,1},{1,0},{2,3},{3,2},{4,5},{5,4},{6,7},{7,6},{8,9},{9,8},{10,11... | collective-permute-start | bytes 24584 | tf_op jit(solution)/shard_map/ppermute | solution.py:15
  4.4 3.8 %collective-permute-start.1 = (bf16[2,32,128]{2,1,0:T(8,128)(2,1)S(1)}, bf16[2,32,128]{2,1,0:T(8,128)(2,1)S(1)}, u32[]{:S(2)}, u32[]{:S(2)}) collective-permute-start(bf16[2,32,128]{2,1,0:T(8,128)(2,1)S(1)} %pad_maximum_fusion.2), channel_id=1, source_target_pairs={{0,2},{1,3},{2,0},{3,1},{4,6},{5,7},{6,4},{7,5},{8,10},{9,11},{10,... | collective-permute-start | bytes 49160 | tf_op jit(solution)/shard_map/ppermute | solution.py:15
  8.3 2.8 %collective-permute-start.2 = (bf16[4,32,128]{2,1,0:T(8,128)(2,1)S(1)}, bf16[4,32,128]{2,1,0:T(8,128)(2,1)S(1)}, u32[]{:S(2)}, u32[]{:S(2)}) collective-permute-start(bf16[4,32,128]{2,1,0:T(8,128)(2,1)S(1)} %pad_maximum_fusion.1), channel_id=1, source_target_pairs={{0,4},{1,5},{2,6},{3,7},{4,0},{5,1},{6,2},{7,3},{8,12},{9,13},{10,... | collective-permute-start | bytes 98312 | tf_op jit(solution)/shard_map/ppermute | solution.py:15
  11.1 4.2 %collective-permute-start.3 = (bf16[8,32,128]{2,1,0:T(8,128)(2,1)S(1)}, bf16[8,32,128]{2,1,0:T(8,128)(2,1)S(1)}, u32[]{:S(2)}, u32[]{:S(2)}) collective-permute-start(bf16[8,32,128]{2,1,0:T(8,128)(2,1)S(1)} %pad_maximum_fusion), channel_id=1, source_target_pairs={{0,8},{1,9},{2,10},{3,11},{4,12},{5,13},{6,14},{7,15},{8,0},{9,1},... | collective-permute-start | bytes 196616 | tf_op jit(solution)/shard_map/ppermute | solution.py:15
  15.3 0.7 copy-start.2
  26.0 10.9 %collective-permute-start.4 = (bf16[8,16,32,128]{3,2,1,0:T(8,128)(2,1)}, bf16[8,16,32,128]{3,2,1,0:T(8,128)(2,1)S(1)}, u32[]{:S(2)}, u32[]{:S(2)}) collective-permute-start(bf16[8,16,32,128]{3,2,1,0:T(8,128)(2,1)} %shard_map.66), channel_id=1, source_target_pairs={{0,1},{1,0},{2,3},{3,2},{4,5},{5,4},{6,7},{7,6},{8,9},{9,8},{10,11... | collective-permute-start | bytes 3145736 | tf_op jit(solution)/shard_map/ppermute | solution.py:15
  38.8 8.2 %collective-permute-start.7 = (bf16[2,16,32,128]{3,2,1,0:T(8,128)(2,1)S(1)}, bf16[2,16,32,128]{3,2,1,0:T(8,128)(2,1)S(1)}, u32[]{:S(2)}, u32[]{:S(2)}) collective-permute-start(bf16[2,16,32,128]{3,2,1,0:T(8,128)(2,1)S(1)} %slice.76), channel_id=1, source_target_pairs={{0,4},{1,5},{2,6},{3,7},{4,0},{5,1},{6,2},{7,3},{8,12},{9,13},{10,... | collective-permute-start | bytes 786440 | tf_op jit(solution)/shard_map/ppermute | solution.py:15
  40.6 14.3 %copy-start.5 = (f32[33,33]{1,0:T(8,128)S(1)}, f32[33,33]{1,0:T(8,128)}, u32[]{:S(2)}) copy-start(f32[33,33]{1,0:T(8,128)} %param.10) | copy-start | bytes 13072
  40.6 7.9 %collective-permute-start.5 = (bf16[2,16,32,128]{3,2,1,0:T(8,128)(2,1)S(1)}, bf16[2,16,32,128]{3,2,1,0:T(8,128)(2,1)S(1)}, u32[]{:S(2)}, u32[]{:S(2)}) collective-permute-start(bf16[2,16,32,128]{3,2,1,0:T(8,128)(2,1)S(1)} %fusion.4), channel_id=1, source_target_pairs={{0,2},{1,3},{2,0},{3,1},{4,6},{5,7},{6,4},{7,5},{8,10},{9,11},{10,... | collective-permute-start | bytes 786440 | tf_op jit(solution)/shard_map/ppermute | solution.py:15
  47.2 4.4 %collective-permute-start.8 = (bf16[16,32,128]{2,1,0:T(8,128)(2,1)S(1)}, bf16[16,32,128]{2,1,0:T(8,128)(2,1)S(1)}, u32[]{:S(2)}, u32[]{:S(2)}) collective-permute-start(bf16[16,32,128]{2,1,0:T(8,128)(2,1)S(1)} %fusion.11), channel_id=1, source_target_pairs={{0,2},{1,3},{2,0},{3,1},{4,6},{5,7},{6,4},{7,5},{8,10},{9,11},{10,... | collective-permute-start | bytes 393224 | tf_op jit(solution)/shard_map/ppermute | solution.py:15
  48.6 6.8 %collective-permute-start.6 = (bf16[16,32,128]{2,1,0:T(8,128)(2,1)S(1)}, bf16[16,32,128]{2,1,0:T(8,128)(2,1)S(1)}, u32[]{:S(2)}, u32[]{:S(2)}) collective-permute-start(bf16[16,32,128]{2,1,0:T(8,128)(2,1)S(1)} %fusion.10), channel_id=1, source_target_pairs={{0,4},{1,5},{2,6},{3,7},{4,0},{5,1},{6,2},{7,3},{8,12},{9,13},{10,... | collective-permute-start | bytes 393224 | tf_op jit(solution)/shard_map/ppermute | solution.py:15
  51.6 9.1 %collective-permute-start.9 = (bf16[16,32,128]{2,1,0:T(8,128)(2,1)S(1)}, bf16[16,32,128]{2,1,0:T(8,128)(2,1)S(1)}, u32[]{:S(2)}, u32[]{:S(2)}) collective-permute-start(bf16[16,32,128]{2,1,0:T(8,128)(2,1)S(1)} %fusion.6), channel_id=1, source_target_pairs={{0,8},{1,9},{2,10},{3,11},{4,12},{5,13},{6,14},{7,15},{8,0},{9,1},... | collective-permute-start | bytes 393224 | tf_op jit(solution)/shard_map/ppermute | solution.py:15
  60.8 10.7 %copy-start.1 = (bf16[16,32,128]{2,1,0:T(8,128)(2,1)}, bf16[16,32,128]{2,1,0:T(8,128)(2,1)S(1)}, u32[]{:S(2)}) copy-start(bf16[16,32,128]{2,1,0:T(8,128)(2,1)S(1)} %fusion.9.own_ref) | copy-start | bytes 393220
  60.8 10.1 %collective-permute-start.10 = (bf16[16,32,128]{2,1,0:T(8,128)(2,1)S(1)}, bf16[16,32,128]{2,1,0:T(8,128)(2,1)S(1)}, u32[]{:S(2)}, u32[]{:S(2)}) collective-permute-start(bf16[16,32,128]{2,1,0:T(8,128)(2,1)S(1)} %fusion.9.own_ref), channel_id=1, source_target_pairs={{0,1},{1,2},{2,3},{3,4},{4,5},{5,6},{6,7},{7,8},{8,9},{9,10},{10,1... | collective-permute-start | bytes 393224 | tf_op jit(solution)/shard_map/ppermute | solution.py:169
  65.2 6.3 %collective-permute-start.11 = (bf16[16,32,128]{2,1,0:T(8,128)(2,1)S(1)}, bf16[16,32,128]{2,1,0:T(8,128)(2,1)S(1)}, u32[]{:S(2)}, u32[]{:S(2)}) collective-permute-start(bf16[16,32,128]{2,1,0:T(8,128)(2,1)S(1)} %fusion.9.own_ref), channel_id=1, source_target_pairs={{1,0},{2,1},{3,2},{4,3},{5,4},{6,5},{7,6},{8,7},{9,8},{10,9},{11,1... | collective-permute-start | bytes 393224 | tf_op jit(solution)/shard_map/ppermute | solution.py:170
  71.0 0.7 copy-start.3
  71.6 0.6 copy-start.4

commit v2 on v1

v2 whole, which is shorter than its diff:
```python
import functools

import jax
import jax.numpy as jnp
from jax import lax
from jax.experimental import pallas as pl
from jax.experimental.pallas import tpu as pltpu
from jax.sharding import PartitionSpec as P


VMEM = pl.BlockSpec(memory_space=pltpu.VMEM)
HBM = pl.BlockSpec(memory_space=pltpu.HBM)
PARAMS = pltpu.CompilerParams(vmem_limit_bytes=20 << 20)


def swap(block, bit):
    count = lax.axis_size("space")
    return lax.ppermute(block, "space", [(i, i ^ bit) for i in range(count)])


def slip_kernel(coefficients_ref, modes_ref, slip_ref, field_ref):
    step = pl.program_id(0)
    part = jnp.dot(coefficients_ref[...], modes_ref[...], preferred_element_type=jnp.float32)

    @pl.when(step == 0)
    def _():
        field_ref[...] = part

    @pl.when(step > 0)
    def _():
        field_ref[...] += part

    @pl.when(step == pl.num_programs(0) - 1)
    def _():
        slip_ref[0] = jnp.exp(0.5 * field_ref[...]).astype(slip_ref.dtype)


def load(green_ref, part_ref, semaphore, start):
    copy = pltpu.make_async_copy(
        green_ref.at[pl.ds(start, part_ref.shape[0])], part_ref, semaphore
    )
    copy.start()
    return copy


def choose_kernel(columns, index_ref, green_ref, part_ref, chosen_ref, semaphore):
    copy = load(green_ref, part_ref, semaphore, 0)
    me = lax.axis_index("space")
    group = index_ref.shape[1]
    row_ids = index_ref[pl.ds(me, 1), :]
    position = ((row_ids // columns) ^ me) * columns + row_ids % columns
    for start in range(0, chosen_ref.shape[0], group):
        row = lax.broadcasted_iota(jnp.int32, (group, group), 0) + start
        chosen_ref[start : start + group, :] = jnp.where(row == position, 1.0, 0.0).astype(
            jnp.bfloat16
        )
    copy.wait()


def repeat_kernel(rows, green_ref, part_ref, repeat_ref, semaphore):
    copy = load(green_ref, part_ref, semaphore, green_ref.shape[0] - part_ref.shape[0])
    source = lax.broadcasted_iota(jnp.int32, repeat_ref.shape, 0)
    target = lax.broadcasted_iota(jnp.int32, repeat_ref.shape, 1)
    near = (target >= source * rows) & (target < (source + 1) * rows)
    repeat_ref[...] = jnp.where(near, 1.0, 0.0).astype(jnp.bfloat16)
    copy.wait()


def select_kernel(chosen_ref, repeat_ref, slip_ref, spread_ref):
    owners, realizations, _ = slip_ref.shape
    rows = spread_ref.shape[0] // realizations
    slip = jnp.concatenate([slip_ref[owner] for owner in range(owners)], axis=1)
    picked = jnp.dot(slip, chosen_ref[...], preferred_element_type=jnp.float32)
    wide = jnp.dot(
        picked.astype(jnp.bfloat16), repeat_ref[...], preferred_element_type=jnp.float32
    )
    row_of = lax.broadcasted_iota(jnp.int32, wide.shape, 1) % rows
    for row in range(rows):
        spread_ref[row * realizations : (row + 1) * realizations, :] = jnp.where(
            row_of == row, wide, 0.0
        ).astype(jnp.bfloat16)


def uplift_kernel(groups, rows, spread_ref, low_ref, high_ref, *rest):
    arrived, outs = rest[: -len(groups)], rest[-len(groups) :]
    depth = low_ref.shape[0] * rows
    width = low_ref.shape[2]
    me = lax.axis_index("space")

    def block(place):
        first = pl.multiple_of((me ^ place) * rows, rows)
        parts = [
            ref[:, pl.ds(first, rows), :].reshape(depth, width) for ref in (low_ref, high_ref)
        ]
        return jnp.concatenate(parts, axis=0)

    columns = jnp.concatenate([block(place) for group in groups for place in group], axis=1)
    value = jnp.dot(spread_ref[...], columns, preferred_element_type=jnp.float32)
    side = 0
    for group, out_ref in zip(groups, outs):
        for slot in range(len(group)):
            part = value[:, side * width : (side + 1) * width].reshape(out_ref.shape[1:])
            if arrived:
                part += arrived[0][side].astype(jnp.float32)
            out_ref[slot] = part.astype(out_ref.dtype)
            side += 1


def uplift_blocks(groups, rows, realizations, dtype, spread, parts, *arrived):
    width = parts[0].shape[2]
    return pl.pallas_call(
        functools.partial(uplift_kernel, groups, rows),
        out_shape=[
            jax.ShapeDtypeStruct((len(group), rows, realizations, width), dtype)
            for group in groups
        ],
        in_specs=[VMEM] * (3 + len(arrived)),
        out_specs=[VMEM] * len(groups),
        compiler_params=PARAMS,
    )(spread, *parts, *arrived)


def bands_kernel(kernel_ref, bands_ref):
    taps = kernel_ref.shape[0]
    half = taps // 2
    width = bands_ref.shape[1] // 2
    weights = (kernel_ref[...] / jnp.sum(kernel_ref[...])).astype(jnp.bfloat16)
    first = lax.broadcasted_iota(jnp.int32, (taps, width), 0)
    second = lax.broadcasted_iota(jnp.int32, (taps, width), 1)
    mirror = jnp.where(first + second == taps - 1, 1.0, 0.0).astype(jnp.bfloat16)
    lines = jnp.dot(weights, mirror, preferred_element_type=jnp.float32)
    source = lax.broadcasted_iota(jnp.int32, (width, width), 0)
    target = lax.broadcasted_iota(jnp.int32, (width, width), 1)
    inside = jnp.abs(source - target) <= half
    for tap in range(-1, taps + 1):
        if 0 <= tap < taps:
            line = jnp.broadcast_to(lines[tap : tap + 1, :], (width, width))
            rolled = pltpu.roll(line, width - half, 1, stride=1, stride_axis=0)
            band = jnp.where(inside, rolled, 0.0).astype(jnp.bfloat16)
        else:
            band = jnp.zeros((width, width), jnp.bfloat16)
        if tap >= 0:
            bands_ref[tap * width : (tap + 1) * width, :width] = band
        if tap < taps:
            bands_ref[(tap + 1) * width : (tap + 2) * width, width:] = band


def smooth_kernel(low_ref, own_ref, high_ref, bands_ref, mask_ref, out_ref, lines_ref):
    half = low_ref.shape[0]
    rows, realizations, width = own_ref.shape

    def row_at(index):
        if index < half:
            return low_ref[index]
        if index < half + rows:
            return own_ref[index - half]
        return high_ref[index - half - rows]

    for shift in range(2 * half + 2):
        for pair in range(rows // 2):
            lines_ref[
                pair * realizations : (pair + 1) * realizations,
                shift * width : (shift + 1) * width,
            ] = row_at(2 * pair + shift)
    value = jnp.dot(lines_ref[...], bands_ref[...], preferred_element_type=jnp.float32)
    value = value.reshape(rows // 2, realizations, 2 * width)
    both = jnp.stack([value[:, :, :width], value[:, :, width:]], axis=1)
    both = both.reshape(rows, realizations, width)
    mask = mask_ref[...].astype(jnp.float32)
    out_ref[...] = jnp.transpose(both, (1, 0, 2)) * mask[None]


def reduce_halves(block, places, bits):
    for bit in bits:
        kept = [slot for slot, place in enumerate(places) if not place & bit]
        away = [slot for slot, place in enumerate(places) if place & bit]
        step = away[0] - kept[0]
        shape = (len(places) // (2 * step), 2, step)
        pairs = block.reshape(shape + block.shape[1:])
        sent = pairs[:, 1].reshape((-1,) + block.shape[1:]).astype(jnp.bfloat16)
        block = pairs[:, 0].reshape(sent.shape) + swap(sent, bit).astype(jnp.float32)
        places = [places[slot] for slot in kept]
    return block


def body(coefficients, kl_modes, green, sub_index, kernel, wet_mask):
    realizations, modes = coefficients.shape
    columns = kl_modes.shape[1]
    group, _, width = green.shape
    rows = wet_mask.shape[0]
    taps = kernel.shape[0]
    half = taps // 2
    count = lax.axis_size("space")
    levels = count.bit_length() - 1
    assert 1 << levels == count and half <= rows and levels >= 4
    green = pltpu.with_memory_space_constraint(green, pltpu.HBM)

    slip = pl.pallas_call(
        slip_kernel,
        out_shape=jax.ShapeDtypeStruct((1, realizations, columns), jnp.bfloat16),
        grid=(4,),
        in_specs=[
            pl.BlockSpec((realizations, modes // 4), lambda i: (0, i)),
            pl.BlockSpec((modes // 4, columns), lambda i: (i, 0)),
        ],
        out_specs=pl.BlockSpec((1, realizations, columns), lambda i: (0, 0, 0)),
        scratch_shapes=[pltpu.VMEM((realizations, columns), jnp.float32)],
        compiler_params=PARAMS,
    )(
        pltpu.with_memory_space_constraint(coefficients, pltpu.HBM),
        pltpu.with_memory_space_constraint(kl_modes, pltpu.HBM),
    )
    for level in range(levels):
        arrived = swap(slip, 1 << level)
        slip = jnp.concatenate([slip, arrived], axis=0)

    part = jax.ShapeDtypeStruct((group // 2,) + green.shape[1:], green.dtype)
    low, chosen = pl.pallas_call(
        functools.partial(choose_kernel, columns),
        out_shape=(part, jax.ShapeDtypeStruct((sub_index.shape[0], group), jnp.bfloat16)),
        in_specs=[VMEM, HBM],
        out_specs=(VMEM, VMEM),
        scratch_shapes=[pltpu.SemaphoreType.DMA],
        compiler_params=PARAMS,
    )(sub_index.reshape(-1, group), green)
    high, repeat = pl.pallas_call(
        functools.partial(repeat_kernel, rows),
        out_shape=(part, jax.ShapeDtypeStruct((group, group * rows), jnp.bfloat16)),
        in_specs=[HBM],
        out_specs=(VMEM, VMEM),
        scratch_shapes=[pltpu.SemaphoreType.DMA],
        compiler_params=PARAMS,
    )(green)
    bands = pl.pallas_call(
        bands_kernel,
        out_shape=jax.ShapeDtypeStruct(((taps + 1) * width, 2 * width), jnp.bfloat16),
        in_specs=[VMEM],
        out_specs=VMEM,
        compiler_params=PARAMS,
    )(kernel)

    spread = pl.pallas_call(
        select_kernel,
        out_shape=jax.ShapeDtypeStruct((rows * realizations, group * rows), jnp.bfloat16),
        in_specs=[VMEM] * 3,
        out_specs=VMEM,
        compiler_params=PARAMS,
    )(chosen, repeat, slip)

    top = count // 2
    even = list(range(0, count, 2))
    away_first = [p for p in even if p < top and p & 2]
    away_second = [p for p in even if p >= top and p & 4]
    keep_first = [p for p in even if p < top and not p & 2]
    keep_second = [p for p in even if p >= top and not p & 4]
    away = away_first + away_second
    keep = keep_first + keep_second

    def blocks(places, dtype, *arrived):
        return uplift_blocks(places, rows, realizations, dtype, spread, (low, high), *arrived)

    (to_send,) = blocks([[place | 1 for place in away]], jnp.bfloat16)
    arrived_away = swap(to_send, 1)
    (to_keep,) = blocks([[place | 1 for place in keep]], jnp.bfloat16)
    arrived_keep = swap(to_keep, 1)
    sent = blocks([away_first, away_second], jnp.bfloat16, arrived_away)
    arrived_first = swap(sent[0], 2)
    arrived_second = swap(sent[1], 4)
    kept = blocks([keep_first, keep_second], jnp.float32, arrived_keep)
    later = [8 << level for level in range(levels - 4)]
    first = reduce_halves(
        kept[0] + arrived_first.astype(jnp.float32), keep_first, [4] + later
    )
    second = reduce_halves(
        kept[1] + arrived_second.astype(jnp.float32), keep_second, [2] + later
    )
    arrived = swap(second.astype(jnp.bfloat16), top)
    seafloor = (first + arrived.astype(jnp.float32))[0].astype(jnp.bfloat16)

    low_rows = lax.ppermute(seafloor[rows - half :], "space", [(i, i + 1) for i in range(count - 1)])
    high_rows = lax.ppermute(seafloor[:half], "space", [(i + 1, i) for i in range(count - 1)])
    return pl.pallas_call(
        smooth_kernel,
        out_shape=jax.ShapeDtypeStruct((realizations, rows, width), jnp.float32),
        in_specs=[VMEM] * 5,
        out_specs=VMEM,
        scratch_shapes=[
            pltpu.VMEM((rows // 2 * realizations, (taps + 1) * width), jnp.bfloat16)
        ],
        compiler_params=PARAMS,
    )(low_rows, seafloor, high_rows, bands, wet_mask)


def solution(mesh):
    placed = (
        P("parts", None),
        P("parts", "space"),
        P(("parts", "space"), None, None),
        P("parts"),
        P(),
        P(("parts", "space"), None),
    )
    return jax.shard_map(
        body, mesh=mesh, in_specs=placed, out_specs=P("parts", "space", None), check_vma=False
    )
```

time: 76.1 us -> 59.8 us (0.79)
  Pallas kernels: 22.9 us -> 14.9 us
  other arithmetic: 5.82 us -> 0.24 us
  local copies, waits for them, and re-layouts: 3.57 us -> 0.1 us
  starting transfers between devices: 25.2 us -> 28.5 us
  matrix products: 1.23 us -> 0 us
  waiting for transfers between devices: 16.7 us -> 15.6 us
    pallas_call x5 -> x10, Pallas kernels: 22.9 us -> 14.9 us  [the longest x4 5.07 us: uplift_blocks(): pl.pallas_call(functools.partial(uplift_kernel, groups, rows), out_shape=...]
    ppermute x10 -> x11, waiting for transfers between devices: 16.1 us -> 11.8 us  [swap(): return lax.ppermute(block, 'space', [(i, i ^ bit) for i in range(count)])]
    ppermute x2, starting transfers between devices: 6.27 us -> 9.51 us  [the longest x1 7.59 us: body(): lax.ppermute(seafloor[rows - half:], 'space', [(i, i + 1) for i in range(...]
    ppermute x2, waiting for transfers between devices: 0.54 us -> 3.73 us  [the longest x1 3.73 us: body(): lax.ppermute(seafloor[:half], 'space', [(i + 1, i) for i in range(count -...]
    unnamed x15 -> x10, local copies, waits for them, and re-layouts: 2.68 us -> 0.04 us
    add x3 -> x0, other arithmetic: 2.07 us -> none  [the longest x1 1.91 us: on_device(): summed = kept + swap(away, 1).astype(jnp.float32)]
    broadcast_in_dim x1 -> x0, other arithmetic: 1.36 us -> none  [on_device(): position[None]]
    dot_general x1 -> x0, matrix products: 1.23 us -> none  [on_device(): field = jnp.dot(coefficients, kl_modes, preferred_element_type=jnp.float32)]
  transfers between devices with their start and end apart: 12 -> 13, of which waited for: 7 -> 8; matrix products, arithmetic and copies ran while one was open for 6% -> 0% of each run, Pallas kernels for 13% -> 15%
where the time goes in v2:
time: 59.8 us; the launch traced here: 59.5 us
  starting transfers between devices  28.5 us (48%)
  waiting for transfers between devices  15.6 us (26%)
  Pallas kernels  14.9 us (25%)
    ppermute x11, starting transfers between devices, swap(): return lax.ppermute(block, 'space', [(i, i ^ bit) for i in range(count)])  19 us
    ppermute x11, waiting for transfers between devices, swap(): return lax.ppermute(block, 'space', [(i, i ^ bit) for i in range(count)])  11.8 us
    ppermute x1, starting transfers between devices, body(): lax.ppermute(seafloor[rows - half:], 'space', [(i, i + 1) for i in range(...  7.59 us
    pallas_call x4, Pallas kernels, uplift_blocks(): pl.pallas_call(functools.partial(uplift_kernel, groups, rows), out_shape=...  5.07 us
    ppermute x1, waiting for transfers between devices, body(): lax.ppermute(seafloor[:half], 'space', [(i + 1, i) for i in range(count -...  3.73 us
    pallas_call x1, Pallas kernels, body(): pl.pallas_call(slip_kernel, out_shape=jax.ShapeDtypeStruct((1, realizatio...  2.56 us
    pallas_call x1, Pallas kernels, body(): pl.pallas_call(functools.partial(repeat_kernel, rows), out_shape=(part, j...  2.2 us
    pallas_call x1, Pallas kernels, body(): pl.pallas_call(functools.partial(choose_kernel, columns), out_shape=(part...  2.2 us
  transfers between devices with their start and end apart: 13, of which 8 were waited for; matrix products, arithmetic and copies ran while one was open for 0% of the time, Pallas kernels for 15%

profile of v2, /device:TPU:1, one launch (start us, length us, event | category | flops | bytes accessed | tf_op | source)
XLA Modules:
  0.0 59.5 jit_solution(12243175070346014600)
XLA Ops:
  0.0 2.6 %shard_map.66 = bf16[1,32,128]{2,1,0:T(8,128)(2,1)S(1)} custom-call(bf16[32,4096]{1,0:T(8,128)(2,1)} %coefficients_ref.1, bf16[4096,128]{1,0:T(8,128)(2,1)} %modes_ref.1), custom_call_target="tpu_custom_call" | custom-call | tf_op jit(solution)/shard_map/pallas_call | solution.py:198
  2.6 0.1 collective-permute-start
  2.7 0.0 copy-start.1
  2.7 2.2 %shard_map.65 = (bf16[64,256,128]{2,1,0:T(8,128)(2,1)S(1)}, bf16[128,2048]{1,0:T(8,128)(2,1)S(1)}) custom-call(bf16[128,256,128]{2,1,0:T(8,128)(2,1)} %green_ref.3), custom_call_target="tpu_custom_call" | custom-call | tf_op jit(solution)/shard_map/pallas_call | solution.py:226
  4.9 0.0 copy-done.1
  4.9 2.2 %shard_map.64 = (bf16[64,256,128]{2,1,0:T(8,128)(2,1)S(1)}, bf16[2048,128]{1,0:T(8,128)(2,1)S(1)}) custom-call(s32[16,128]{1,0:T(8,128)S(1)} %bitcast.27, bf16[128,256,128]{2,1,0:T(8,128)(2,1)} %green_ref.3), custom_call_target="tpu_custom_call" | custom-call | tf_op jit(solution)/shard_map/pallas_call | solution.py:218
  7.1 0.0 collective-permute-done
  7.1 2.8 %collective-permute-start.1 = (bf16[2,32,128]{2,1,0:T(8,128)(2,1)S(1)}, bf16[2,32,128]{2,1,0:T(8,128)(2,1)S(1)}, u32[]{:S(2)}, u32[]{:S(2)}) collective-permute-start(bf16[2,32,128]{2,1,0:T(8,128)(2,1)S(1)} %pad_maximum_fusion.2), channel_id=1, source_target_pairs={{0,2},{1,3},{2,0},{3,1},{4,6},{5,7},{6,4},{7,5},{8,10},{9,11},{10,... | collective-permute-start | bytes 49160 | tf_op jit(solution)/shard_map/ppermute | solution.py:18
  9.9 1.1 %collective-permute-done.1 = bf16[2,32,128]{2,1,0:T(8,128)(2,1)S(1)} collective-permute-done((bf16[2,32,128]{2,1,0:T(8,128)(2,1)S(1)}, bf16[2,32,128]{2,1,0:T(8,128)(2,1)S(1)}, u32[]{:S(2)}, u32[]{:S(2)}) %collective-permute-start.1) | collective-permute-done | bytes 16416 | tf_op jit(solution)/shard_map/ppermute | solution.py:18
  11.0 1.5 %collective-permute-start.2 = (bf16[4,32,128]{2,1,0:T(8,128)(2,1)S(1)}, bf16[4,32,128]{2,1,0:T(8,128)(2,1)S(1)}, u32[]{:S(2)}, u32[]{:S(2)}) collective-permute-start(bf16[4,32,128]{2,1,0:T(8,128)(2,1)S(1)} %pad_maximum_fusion.1), channel_id=1, source_target_pairs={{0,4},{1,5},{2,6},{3,7},{4,0},{5,1},{6,2},{7,3},{8,12},{9,13},{10,... | collective-permute-start | bytes 98312 | tf_op jit(solution)/shard_map/ppermute | solution.py:18
  12.6 1.3 %collective-permute-done.2 = bf16[4,32,128]{2,1,0:T(8,128)(2,1)S(1)} collective-permute-done((bf16[4,32,128]{2,1,0:T(8,128)(2,1)S(1)}, bf16[4,32,128]{2,1,0:T(8,128)(2,1)S(1)}, u32[]{:S(2)}, u32[]{:S(2)}) %collective-permute-start.2) | collective-permute-done | bytes 32800 | tf_op jit(solution)/shard_map/ppermute | solution.py:18
  13.9 2.5 %collective-permute-start.3 = (bf16[8,32,128]{2,1,0:T(8,128)(2,1)S(1)}, bf16[8,32,128]{2,1,0:T(8,128)(2,1)S(1)}, u32[]{:S(2)}, u32[]{:S(2)}) collective-permute-start(bf16[8,32,128]{2,1,0:T(8,128)(2,1)S(1)} %pad_maximum_fusion), channel_id=1, source_target_pairs={{0,8},{1,9},{2,10},{3,11},{4,12},{5,13},{6,14},{7,15},{8,0},{9,1},... | collective-permute-start | bytes 196616 | tf_op jit(solution)/shard_map/ppermute | solution.py:18
  16.4 1.6 %collective-permute-done.3 = bf16[8,32,128]{2,1,0:T(8,128)(2,1)S(1)} collective-permute-done((bf16[8,32,128]{2,1,0:T(8,128)(2,1)S(1)}, bf16[8,32,128]{2,1,0:T(8,128)(2,1)S(1)}, u32[]{:S(2)}, u32[]{:S(2)}) %collective-permute-start.3) | collective-permute-done | bytes 65568 | tf_op jit(solution)/shard_map/ppermute | solution.py:18
  18.1 0.7 %shard_map.67.spread_ref = bf16[512,2048]{1,0:T(8,128)(2,1)S(1)} custom-call(bf16[2048,128]{1,0:T(8,128)(2,1)S(1)} %get-tuple-element.13.chosen_ref, bf16[128,2048]{1,0:T(8,128)(2,1)S(1)} %get-tuple-element.14.repeat_ref, bf16[16,32,128]{2,1,0:T(8,128)(2,1)S(1)} %constant_dynamic-update-slice_fusion.slip_ref), custom_call_target="tpu_custom_call" | custom-call | tf_op jit(solution)/shard_map/pallas_call | solution.py:242
  18.8 1.3 %shard_map.70 = bf16[4,16,32,128]{3,2,1,0:T(8,128)(2,1)S(1)} custom-call(bf16[512,2048]{1,0:T(8,128)(2,1)S(1)} %shard_map.67.spread_ref, bf16[64,256,128]{2,1,0:T(8,128)(2,1)S(1)} %get-tuple-element.15.low_ref, bf16[64,256,128]{2,1,0:T(8,128)(2,1)S(1)} %get-tuple-element.16.high_ref), custom_call_target="tpu_custom_call" | custom-call | tf_op jit(solution)/shard_map/pallas_call | solution.py:111
  20.1 3.3 %collective-permute-start.5 = (bf16[4,16,32,128]{3,2,1,0:T(8,128)(2,1)S(1)}, bf16[4,16,32,128]{3,2,1,0:T(8,128)(2,1)S(1)}, u32[]{:S(2)}, u32[]{:S(2)}) collective-permute-start(bf16[4,16,32,128]{3,2,1,0:T(8,128)(2,1)S(1)} %shard_map.70), channel_id=1, source_target_pairs={{0,1},{1,0},{2,3},{3,2},{4,5},{5,4},{6,7},{7,6},{8,9},{9,8},{10,11... | collective-permute-start | bytes 1572872 | tf_op jit(solution)/shard_map/ppermute | solution.py:18
  23.3 1.3 %shard_map.68 = bf16[4,16,32,128]{3,2,1,0:T(8,128)(2,1)S(1)} custom-call(bf16[512,2048]{1,0:T(8,128)(2,1)S(1)} %shard_map.67.spread_ref, bf16[64,256,128]{2,1,0:T(8,128)(2,1)S(1)} %get-tuple-element.15.low_ref, bf16[64,256,128]{2,1,0:T(8,128)(2,1)S(1)} %get-tuple-element.16.high_ref), custom_call_target="tpu_custom_call" | custom-call | tf_op jit(solution)/shard_map/pallas_call | solution.py:111
  24.6 0.1 collective-permute-start.4
  24.7 0.2 collective-permute-done.5.rest_0_
  24.8 1.3 %shard_map.71 = (bf16[2,16,32,128]{3,2,1,0:T(8,128)(2,1)S(1)}, bf16[2,16,32,128]{3,2,1,0:T(8,128)(2,1)S(1)}) custom-call(bf16[512,2048]{1,0:T(8,128)(2,1)S(1)} %shard_map.67.spread_ref, bf16[64,256,128]{2,1,0:T(8,128)(2,1)S(1)} %get-tuple-element.15.low_ref, bf16[64,256,128]{2,1,0:T(8,128)(2,1)S(1)} %get-tuple-element.16.high_ref, ...), custom_call_target="tpu_custom_call" | custom-call | tf_op jit(solution)/shard_map/pallas_call | solution.py:111
  26.1 1.7 %collective-permute-start.8 = (bf16[2,16,32,128]{3,2,1,0:T(8,128)(2,1)S(1)}, bf16[2,16,32,128]{3,2,1,0:T(8,128)(2,1)S(1)}, u32[]{:S(2)}, u32[]{:S(2)}) collective-permute-start(bf16[2,16,32,128]{3,2,1,0:T(8,128)(2,1)S(1)} %get-tuple-element.20), channel_id=1, source_target_pairs={{0,4},{1,5},{2,6},{3,7},{4,0},{5,1},{6,2},{7,3},{8,12},{9,13},{10,... | collective-permute-start | bytes 786440 | tf_op jit(solution)/shard_map/ppermute | solution.py:18
  27.8 1.2 %collective-permute-start.6 = (bf16[2,16,32,128]{3,2,1,0:T(8,128)(2,1)S(1)}, bf16[2,16,32,128]{3,2,1,0:T(8,128)(2,1)S(1)}, u32[]{:S(2)}, u32[]{:S(2)}) collective-permute-start(bf16[2,16,32,128]{3,2,1,0:T(8,128)(2,1)S(1)} %get-tuple-element.18), channel_id=1, source_target_pairs={{0,2},{1,3},{2,0},{3,1},{4,6},{5,7},{6,4},{7,5},{8,10},{9,11},{10,... | collective-permute-start | bytes 786440 | tf_op jit(solution)/shard_map/ppermute | solution.py:18
  29.1 0.0 collective-permute-done.4.rest_0_
  29.1 1.3 %shard_map.69 = (f32[2,16,32,128]{3,2,1,0:T(8,128)S(1)}, f32[2,16,32,128]{3,2,1,0:T(8,128)S(1)}) custom-call(bf16[512,2048]{1,0:T(8,128)(2,1)S(1)} %shard_map.67.spread_ref, bf16[64,256,128]{2,1,0:T(8,128)(2,1)S(1)} %get-tuple-element.15.low_ref, bf16[64,256,128]{2,1,0:T(8,128)(2,1)S(1)} %get-tuple-element.16.high_ref, ...), custom_call_target="tpu_custom_call" | custom-call | tf_op jit(solution)/shard_map/pallas_call | solution.py:111
  30.3 0.0 copy-start
  30.3 0.0 copy-start.2
  30.4 3.6 %collective-permute-done.8 = bf16[2,16,32,128]{3,2,1,0:T(8,128)(2,1)S(1)} collective-permute-done((bf16[2,16,32,128]{3,2,1,0:T(8,128)(2,1)S(1)}, bf16[2,16,32,128]{3,2,1,0:T(8,128)(2,1)S(1)}, u32[]{:S(2)}, u32[]{:S(2)}) %collective-permute-start.8) | collective-permute-done | bytes 262176 | tf_op jit(solution)/shard_map/ppermute | solution.py:18
  34.0 0.1 add_bitcast_fusion
  34.1 1.3 %collective-permute-start.9 = (bf16[1,16,32,128]{3,2,1,0:T(8,128)(2,1)S(1)}, bf16[1,16,32,128]{3,2,1,0:T(8,128)(2,1)S(1)}, u32[]{:S(2)}, u32[]{:S(2)}) collective-permute-start(bf16[1,16,32,128]{3,2,1,0:T(8,128)(2,1)S(1)} %fusion.7), channel_id=1, source_target_pairs={{0,2},{1,3},{2,0},{3,1},{4,6},{5,7},{6,4},{7,5},{8,10},{9,11},{10,... | collective-permute-start | bytes 393224 | tf_op jit(solution)/shard_map/ppermute | solution.py:18
  35.4 0.0 collective-permute-done.6
  35.4 0.1 add_bitcast_fusion.1
  35.5 1.4 %collective-permute-start.7 = (bf16[1,16,32,128]{3,2,1,0:T(8,128)(2,1)S(1)}, bf16[1,16,32,128]{3,2,1,0:T(8,128)(2,1)S(1)}, u32[]{:S(2)}, u32[]{:S(2)}) collective-permute-start(bf16[1,16,32,128]{3,2,1,0:T(8,128)(2,1)S(1)} %fusion.6), channel_id=1, source_target_pairs={{0,4},{1,5},{2,6},{3,7},{4,0},{5,1},{6,2},{7,3},{8,12},{9,13},{10,... | collective-permute-start | bytes 393224 | tf_op jit(solution)/shard_map/ppermute | solution.py:18
  36.9 1.1 %collective-permute-done.9 = bf16[1,16,32,128]{3,2,1,0:T(8,128)(2,1)S(1)} collective-permute-done((bf16[1,16,32,128]{3,2,1,0:T(8,128)(2,1)S(1)}, bf16[1,16,32,128]{3,2,1,0:T(8,128)(2,1)S(1)}, u32[]{:S(2)}, u32[]{:S(2)}) %collective-permute-start.9) | collective-permute-done | bytes 131104 | tf_op jit(solution)/shard_map/ppermute | solution.py:18
  38.0 3.1 %collective-permute-start.10 = (bf16[1,16,32,128]{3,2,1,0:T(8,128)(2,1)S(1)}, bf16[1,16,32,128]{3,2,1,0:T(8,128)(2,1)S(1)}, u32[]{:S(2)}, u32[]{:S(2)}) collective-permute-start(bf16[1,16,32,128]{3,2,1,0:T(8,128)(2,1)S(1)} %fusion.1), channel_id=1, source_target_pairs={{0,8},{1,9},{2,10},{3,11},{4,12},{5,13},{6,14},{7,15},{8,0},{9,1},... | collective-permute-start | bytes 393224 | tf_op jit(solution)/shard_map/ppermute | solution.py:18
  41.1 0.0 collective-permute-done.7
  41.1 2.9 %collective-permute-done.10 = bf16[1,16,32,128]{3,2,1,0:T(8,128)(2,1)S(1)} collective-permute-done((bf16[1,16,32,128]{3,2,1,0:T(8,128)(2,1)S(1)}, bf16[1,16,32,128]{3,2,1,0:T(8,128)(2,1)S(1)}, u32[]{:S(2)}, u32[]{:S(2)}) %collective-permute-start.10) | collective-permute-done | bytes 131104 | tf_op jit(solution)/shard_map/ppermute | solution.py:18
  44.0 7.6 %collective-permute-start.11 = (bf16[16,32,128]{2,1,0:T(8,128)(2,1)S(1)}, bf16[16,32,128]{2,1,0:T(8,128)(2,1)S(1)}, u32[]{:S(2)}, u32[]{:S(2)}) collective-permute-start(bf16[16,32,128]{2,1,0:T(8,128)(2,1)S(1)} %fusion.5.own_ref), channel_id=1, source_target_pairs={{0,1},{1,2},{2,3},{3,4},{4,5},{5,6},{6,7},{7,8},{8,9},{9,10},{10,1... | collective-permute-start | bytes 393224 | tf_op jit(solution)/shard_map/ppermute | solution.py:280
  51.6 1.9 %collective-permute-start.12 = (bf16[16,32,128]{2,1,0:T(8,128)(2,1)S(1)}, bf16[16,32,128]{2,1,0:T(8,128)(2,1)S(1)}, u32[]{:S(2)}, u32[]{:S(2)}) collective-permute-start(bf16[16,32,128]{2,1,0:T(8,128)(2,1)S(1)} %fusion.5.own_ref), channel_id=1, source_target_pairs={{1,0},{2,1},{3,2},{4,3},{5,4},{6,5},{7,6},{8,7},{9,8},{10,9},{11,1... | collective-permute-start | bytes 393224 | tf_op jit(solution)/shard_map/ppermute | solution.py:281
  53.5 0.0 copy-done
  53.5 0.6 %shard_map.72.bands_ref = bf16[4352,256]{1,0:T(8,128)(2,1)S(1)} custom-call(f32[33,33]{1,0:T(8,128)S(1)} %copy-done), custom_call_target="tpu_custom_call" | custom-call | tf_op jit(solution)/shard_map/pallas_call | solution.py:234
  54.1 0.0 collective-permute-done.11.low_ref
  54.2 3.7 %collective-permute-done.12.high_ref = bf16[16,32,128]{2,1,0:T(8,128)(2,1)S(1)} collective-permute-done((bf16[16,32,128]{2,1,0:T(8,128)(2,1)S(1)}, bf16[16,32,128]{2,1,0:T(8,128)(2,1)S(1)}, u32[]{:S(2)}, u32[]{:S(2)}) %collective-permute-start.12) | collective-permute-done | bytes 131104 | tf_op jit(solution)/shard_map/ppermute | solution.py:281
  57.9 0.0 copy-done.2
  57.9 1.6 %shard_map.73 = f32[32,16,128]{2,1,0:T(8,128)} custom-call(bf16[16,32,128]{2,1,0:T(8,128)(2,1)S(1)} %collective-permute-done.11.low_ref, bf16[16,32,128]{2,1,0:T(8,128)(2,1)S(1)} %fusion.5.own_ref, bf16[16,32,128]{2,1,0:T(8,128)(2,1)S(1)} %collective-permute-done.12.high_ref, bf16[4352,256]{1,0:T(8,128)(2,1)S(1)} %shard_map.72.bands_ref, s32[16,128]{1,0:T(8,128)S(1)} %copy-done.2), custom_call_target="tpu_custom_call" | custom-call | tf_op jit(solution)/shard_map/pallas_call | solution.py:282
  (12 shorter events, 0.2 us)
Async XLA Ops:
  2.6 4.5 %collective-permute-start = (bf16[1,32,128]{2,1,0:T(8,128)(2,1)S(1)}, bf16[1,32,128]{2,1,0:T(8,128)(2,1)S(1)}, u32[]{:S(2)}, u32[]{:S(2)}) collective-permute-start(bf16[1,32,128]{2,1,0:T(8,128)(2,1)S(1)} %shard_map.66), channel_id=1, source_target_pairs={{0,1},{1,0},{2,3},{3,2},{4,5},{5,4},{6,7},{7,6},{8,9},{9,8},{10,11... | collective-permute-start | bytes 24584 | tf_op jit(solution)/shard_map/ppermute | solution.py:18
  2.7 2.2 %copy-start.1 = (s32[2048]{0:T(1024)S(1)}, s32[2048]{0:T(1024)}, u32[]{:S(2)}) copy-start(s32[2048]{0:T(1024)} %param.9) | copy-start | bytes 24580
  7.1 3.9 %collective-permute-start.1 = (bf16[2,32,128]{2,1,0:T(8,128)(2,1)S(1)}, bf16[2,32,128]{2,1,0:T(8,128)(2,1)S(1)}, u32[]{:S(2)}, u32[]{:S(2)}) collective-permute-start(bf16[2,32,128]{2,1,0:T(8,128)(2,1)S(1)} %pad_maximum_fusion.2), channel_id=1, source_target_pairs={{0,2},{1,3},{2,0},{3,1},{4,6},{5,7},{6,4},{7,5},{8,10},{9,11},{10,... | collective-permute-start | bytes 49160 | tf_op jit(solution)/shard_map/ppermute | solution.py:18
  11.0 2.8 %collective-permute-start.2 = (bf16[4,32,128]{2,1,0:T(8,128)(2,1)S(1)}, bf16[4,32,128]{2,1,0:T(8,128)(2,1)S(1)}, u32[]{:S(2)}, u32[]{:S(2)}) collective-permute-start(bf16[4,32,128]{2,1,0:T(8,128)(2,1)S(1)} %pad_maximum_fusion.1), channel_id=1, source_target_pairs={{0,4},{1,5},{2,6},{3,7},{4,0},{5,1},{6,2},{7,3},{8,12},{9,13},{10,... | collective-permute-start | bytes 98312 | tf_op jit(solution)/shard_map/ppermute | solution.py:18
  13.9 4.2 %collective-permute-start.3 = (bf16[8,32,128]{2,1,0:T(8,128)(2,1)S(1)}, bf16[8,32,128]{2,1,0:T(8,128)(2,1)S(1)}, u32[]{:S(2)}, u32[]{:S(2)}) collective-permute-start(bf16[8,32,128]{2,1,0:T(8,128)(2,1)S(1)} %pad_maximum_fusion), channel_id=1, source_target_pairs={{0,8},{1,9},{2,10},{3,11},{4,12},{5,13},{6,14},{7,15},{8,0},{9,1},... | collective-permute-start | bytes 196616 | tf_op jit(solution)/shard_map/ppermute | solution.py:18
  20.1 4.8 %collective-permute-start.5 = (bf16[4,16,32,128]{3,2,1,0:T(8,128)(2,1)S(1)}, bf16[4,16,32,128]{3,2,1,0:T(8,128)(2,1)S(1)}, u32[]{:S(2)}, u32[]{:S(2)}) collective-permute-start(bf16[4,16,32,128]{3,2,1,0:T(8,128)(2,1)S(1)} %shard_map.70), channel_id=1, source_target_pairs={{0,1},{1,0},{2,3},{3,2},{4,5},{5,4},{6,7},{7,6},{8,9},{9,8},{10,11... | collective-permute-start | bytes 1572872 | tf_op jit(solution)/shard_map/ppermute | solution.py:18
  24.6 4.5 %collective-permute-start.4 = (bf16[4,16,32,128]{3,2,1,0:T(8,128)(2,1)S(1)}, bf16[4,16,32,128]{3,2,1,0:T(8,128)(2,1)S(1)}, u32[]{:S(2)}, u32[]{:S(2)}) collective-permute-start(bf16[4,16,32,128]{3,2,1,0:T(8,128)(2,1)S(1)} %shard_map.68), channel_id=1, source_target_pairs={{0,1},{1,0},{2,3},{3,2},{4,5},{5,4},{6,7},{7,6},{8,9},{9,8},{10,11... | collective-permute-start | bytes 1572872 | tf_op jit(solution)/shard_map/ppermute | solution.py:18
  26.1 7.9 %collective-permute-start.8 = (bf16[2,16,32,128]{3,2,1,0:T(8,128)(2,1)S(1)}, bf16[2,16,32,128]{3,2,1,0:T(8,128)(2,1)S(1)}, u32[]{:S(2)}, u32[]{:S(2)}) collective-permute-start(bf16[2,16,32,128]{3,2,1,0:T(8,128)(2,1)S(1)} %get-tuple-element.20), channel_id=1, source_target_pairs={{0,4},{1,5},{2,6},{3,7},{4,0},{5,1},{6,2},{7,3},{8,12},{9,13},{10,... | collective-permute-start | bytes 786440 | tf_op jit(solution)/shard_map/ppermute | solution.py:18
  27.8 7.6 %collective-permute-start.6 = (bf16[2,16,32,128]{3,2,1,0:T(8,128)(2,1)S(1)}, bf16[2,16,32,128]{3,2,1,0:T(8,128)(2,1)S(1)}, u32[]{:S(2)}, u32[]{:S(2)}) collective-permute-start(bf16[2,16,32,128]{3,2,1,0:T(8,128)(2,1)S(1)} %get-tuple-element.18), channel_id=1, source_target_pairs={{0,2},{1,3},{2,0},{3,1},{4,6},{5,7},{6,4},{7,5},{8,10},{9,11},{10,... | collective-permute-start | bytes 786440 | tf_op jit(solution)/shard_map/ppermute | solution.py:18
  30.3 23.2 %copy-start = (f32[33,33]{1,0:T(8,128)S(1)}, f32[33,33]{1,0:T(8,128)}, u32[]{:S(2)}) copy-start(f32[33,33]{1,0:T(8,128)} %kernel_ref.1) | copy-start | bytes 13072
  30.3 27.5 %copy-start.2 = (s32[16,128]{1,0:T(8,128)S(1)}, s32[16,128]{1,0:T(8,128)}, u32[]{:S(2)}) copy-start(s32[16,128]{1,0:T(8,128)} %mask_ref.1) | copy-start | bytes 24580
  34.1 3.9 %collective-permute-start.9 = (bf16[1,16,32,128]{3,2,1,0:T(8,128)(2,1)S(1)}, bf16[1,16,32,128]{3,2,1,0:T(8,128)(2,1)S(1)}, u32[]{:S(2)}, u32[]{:S(2)}) collective-permute-start(bf16[1,16,32,128]{3,2,1,0:T(8,128)(2,1)S(1)} %fusion.7), channel_id=1, source_target_pairs={{0,2},{1,3},{2,0},{3,1},{4,6},{5,7},{6,4},{7,5},{8,10},{9,11},{10,... | collective-permute-start | bytes 393224 | tf_op jit(solution)/shard_map/ppermute | solution.py:18
  35.5 5.6 %collective-permute-start.7 = (bf16[1,16,32,128]{3,2,1,0:T(8,128)(2,1)S(1)}, bf16[1,16,32,128]{3,2,1,0:T(8,128)(2,1)S(1)}, u32[]{:S(2)}, u32[]{:S(2)}) collective-permute-start(bf16[1,16,32,128]{3,2,1,0:T(8,128)(2,1)S(1)} %fusion.6), channel_id=1, source_target_pairs={{0,4},{1,5},{2,6},{3,7},{4,0},{5,1},{6,2},{7,3},{8,12},{9,13},{10,... | collective-permute-start | bytes 393224 | tf_op jit(solution)/shard_map/ppermute | solution.py:18
  38.0 5.9 %collective-permute-start.10 = (bf16[1,16,32,128]{3,2,1,0:T(8,128)(2,1)S(1)}, bf16[1,16,32,128]{3,2,1,0:T(8,128)(2,1)S(1)}, u32[]{:S(2)}, u32[]{:S(2)}) collective-permute-start(bf16[1,16,32,128]{3,2,1,0:T(8,128)(2,1)S(1)} %fusion.1), channel_id=1, source_target_pairs={{0,8},{1,9},{2,10},{3,11},{4,12},{5,13},{6,14},{7,15},{8,0},{9,1},... | collective-permute-start | bytes 393224 | tf_op jit(solution)/shard_map/ppermute | solution.py:18
  44.0 10.1 %collective-permute-start.11 = (bf16[16,32,128]{2,1,0:T(8,128)(2,1)S(1)}, bf16[16,32,128]{2,1,0:T(8,128)(2,1)S(1)}, u32[]{:S(2)}, u32[]{:S(2)}) collective-permute-start(bf16[16,32,128]{2,1,0:T(8,128)(2,1)S(1)} %fusion.5.own_ref), channel_id=1, source_target_pairs={{0,1},{1,2},{2,3},{3,4},{4,5},{5,6},{6,7},{7,8},{8,9},{9,10},{10,1... | collective-permute-start | bytes 393224 | tf_op jit(solution)/shard_map/ppermute | solution.py:280
  51.6 6.3 %collective-permute-start.12 = (bf16[16,32,128]{2,1,0:T(8,128)(2,1)S(1)}, bf16[16,32,128]{2,1,0:T(8,128)(2,1)S(1)}, u32[]{:S(2)}, u32[]{:S(2)}) collective-permute-start(bf16[16,32,128]{2,1,0:T(8,128)(2,1)S(1)} %fusion.5.own_ref), channel_id=1, source_target_pairs={{1,0},{2,1},{3,2},{4,3},{5,4},{6,5},{7,6},{8,7},{9,8},{10,9},{11,1... | collective-permute-start | bytes 393224 | tf_op jit(solution)/shard_map/ppermute | solution.py:281

commit v3 on v2

--- a/solution.py
+++ b/solution.py
@@ -18,21 +18,29 @@
     return lax.ppermute(block, "space", [(i, i ^ bit) for i in range(count)])
 
 
-def slip_kernel(coefficients_ref, modes_ref, slip_ref, field_ref):
-    step = pl.program_id(0)
-    part = jnp.dot(coefficients_ref[...], modes_ref[...], preferred_element_type=jnp.float32)
-
-    @pl.when(step == 0)
-    def _():
-        field_ref[...] = part
-
-    @pl.when(step > 0)
-    def _():
-        field_ref[...] += part
-
-    @pl.when(step == pl.num_programs(0) - 1)
-    def _():
-        slip_ref[0] = jnp.exp(0.5 * field_ref[...]).astype(slip_ref.dtype)
+def slip_kernel(coefficients_hbm, modes_hbm, slip_ref, coefficients_ref, modes_ref, semaphores):
+    parts = semaphores.shape[0] - 1
+    depth = modes_ref.shape[0] // parts
+    first = pltpu.make_async_copy(coefficients_hbm, coefficients_ref, semaphores.at[parts])
+    first.start()
+    copies = []
+    for part in range(parts):
+        lines = pl.ds(part * depth, depth)
+        copies.append(
+            pltpu.make_async_copy(
+                modes_hbm.at[lines], modes_ref.at[lines], semaphores.at[part]
+            )
+        )
+        copies[part].start()
+    first.wait()
+    field = jnp.zeros(slip_ref.shape[1:], jnp.float32)
+    for part in range(parts):
+        lines = slice(part * depth, (part + 1) * depth)
+        copies[part].wait()
+        field += jnp.dot(
+            coefficients_ref[:, lines], modes_ref[lines], preferred_element_type=jnp.float32
+        )
+    slip_ref[0] = jnp.exp(0.5 * field).astype(slip_ref.dtype)
 
 
 def load(green_ref, part_ref, semaphore, start):
@@ -43,27 +51,34 @@
     return copy
 
 
-def choose_kernel(columns, index_ref, green_ref, part_ref, chosen_ref, semaphore):
-    copy = load(green_ref, part_ref, semaphore, 0)
+def choose_kernel(start, columns, index_hbm, green_ref, part_ref, chosen_ref, index_ref, semaphores):
+    fetch = pltpu.make_async_copy(index_hbm, index_ref, semaphores.at[0])
+    fetch.start()
+    copy = load(green_ref, part_ref, semaphores.at[1], start)
     me = lax.axis_index("space")
     group = index_ref.shape[1]
+    fetch.wait()
     row_ids = index_ref[pl.ds(me, 1), :]
     position = ((row_ids // columns) ^ me) * columns + row_ids % columns
-    for start in range(0, chosen_ref.shape[0], group):
-        row = lax.broadcasted_iota(jnp.int32, (group, group), 0) + start
-        chosen_ref[start : start + group, :] = jnp.where(row == position, 1.0, 0.0).astype(
+    for first in range(0, chosen_ref.shape[0], group):
+        row = lax.broadcasted_iota(jnp.int32, (group, group), 0) + first
+        chosen_ref[first : first + group, :] = jnp.where(row == position, 1.0, 0.0).astype(
             jnp.bfloat16
         )
     copy.wait()
 
 
-def repeat_kernel(rows, green_ref, part_ref, repeat_ref, semaphore):
-    copy = load(green_ref, part_ref, semaphore, green_ref.shape[0] - part_ref.shape[0])
+def repeat_kernel(start, rows, green_ref, part_ref, repeat_ref, semaphore):
+    copy = load(green_ref, part_ref, semaphore, start)
     source = lax.broadcasted_iota(jnp.int32, repeat_ref.shape, 0)
     target = lax.broadcasted_iota(jnp.int32, repeat_ref.shape, 1)
     near = (target >= source * rows) & (target < (source + 1) * rows)
     repeat_ref[...] = jnp.where(near, 1.0, 0.0).astype(jnp.bfloat16)
     copy.wait()
+
+
+def rest_kernel(start, green_ref, part_ref, semaphore):
+    load(green_ref, part_ref, semaphore, start).wait()
 
 
 def select_kernel(chosen_ref, repeat_ref, slip_ref, spread_ref):
@@ -81,18 +96,17 @@
         ).astype(jnp.bfloat16)
 
 
-def uplift_kernel(groups, rows, spread_ref, low_ref, high_ref, *rest):
-    arrived, outs = rest[: -len(groups)], rest[-len(groups) :]
-    depth = low_ref.shape[0] * rows
-    width = low_ref.shape[2]
+def uplift_kernel(groups, parts, rows, spread_ref, *refs):
+    parts, arrived, outs = refs[:parts], refs[parts : -len(groups)], refs[-len(groups) :]
+    width = parts[0].shape[2]
     me = lax.axis_index("space")
 
     def block(place):
         first = pl.multiple_of((me ^ place) * rows, rows)
-        parts = [
-            ref[:, pl.ds(first, rows), :].reshape(depth, width) for ref in (low_ref, high_ref)
+        pieces = [
+            ref[:, pl.ds(first, rows), :].reshape(ref.shape[0] * rows, width) for ref in parts
         ]
-        return jnp.concatenate(parts, axis=0)
+        return jnp.concatenate(pieces, axis=0)
 
     columns = jnp.concatenate([block(place) for group in groups for place in group], axis=1)
     value = jnp.dot(spread_ref[...], columns, preferred_element_type=jnp.float32)
@@ -109,12 +123,12 @@
 def uplift_blocks(groups, rows, realizations, dtype, spread, parts, *arrived):
     width = parts[0].shape[2]
     return pl.pallas_call(
-        functools.partial(uplift_kernel, groups, rows),
+        functools.partial(uplift_kernel, groups, len(parts), rows),
         out_shape=[
             jax.ShapeDtypeStruct((len(group), rows, realizations, width), dtype)
             for group in groups
         ],
-        in_specs=[VMEM] * (3 + len(arrived)),
+        in_specs=[VMEM] * (1 + len(parts) + len(arrived)),
         out_specs=[VMEM] * len(groups),
         compiler_params=PARAMS,
     )(spread, *parts, *arrived)
@@ -184,7 +198,7 @@
 
 
 def body(coefficients, kl_modes, green, sub_index, kernel, wet_mask):
-    realizations, modes = coefficients.shape
+    realizations, _ = coefficients.shape
     columns = kl_modes.shape[1]
     group, _, width = green.shape
     rows = wet_mask.shape[0]
@@ -198,13 +212,13 @@
     slip = pl.pallas_call(
         slip_kernel,
         out_shape=jax.ShapeDtypeStruct((1, realizations, columns), jnp.bfloat16),
-        grid=(4,),
-        in_specs=[
-            pl.BlockSpec((realizations, modes // 4), lambda i: (0, i)),
-            pl.BlockSpec((modes // 4, columns), lambda i: (i, 0)),
+        in_specs=[HBM, HBM],
+        out_specs=VMEM,
+        scratch_shapes=[
+            pltpu.VMEM(coefficients.shape, coefficients.dtype),
+            pltpu.VMEM(kl_modes.shape, kl_modes.dtype),
+            pltpu.SemaphoreType.DMA((5,)),
         ],
-        out_specs=pl.BlockSpec((1, realizations, columns), lambda i: (0, 0, 0)),
-        scratch_shapes=[pltpu.VMEM((realizations, columns), jnp.float32)],
         compiler_params=PARAMS,
     )(
         pltpu.with_memory_space_constraint(coefficients, pltpu.HBM),
@@ -214,23 +228,43 @@
         arrived = swap(slip, 1 << level)
         slip = jnp.concatenate([slip, arrived], axis=0)
 
-    part = jax.ShapeDtypeStruct((group // 2,) + green.shape[1:], green.dtype)
-    low, chosen = pl.pallas_call(
-        functools.partial(choose_kernel, columns),
-        out_shape=(part, jax.ShapeDtypeStruct((sub_index.shape[0], group), jnp.bfloat16)),
-        in_specs=[VMEM, HBM],
+    bounds = [0, group // 4, group * 5 // 8, group]
+    shapes = [
+        jax.ShapeDtypeStruct((stop - start,) + green.shape[1:], green.dtype)
+        for start, stop in zip(bounds, bounds[1:])
+    ]
+    index = pltpu.with_memory_space_constraint(sub_index.reshape(-1, group), pltpu.HBM)
+    part0, chosen = pl.pallas_call(
+        functools.partial(choose_kernel, bounds[0], columns),
+        out_shape=(
+            shapes[0],
+            jax.ShapeDtypeStruct((sub_index.shape[0], group), jnp.bfloat16),
+        ),
+        in_specs=[HBM, HBM],
         out_specs=(VMEM, VMEM),
-        scratch_shapes=[pltpu.SemaphoreType.DMA],
-        compiler_params=PARAMS,
-    )(sub_index.reshape(-1, group), green)
-    high, repeat = pl.pallas_call(
-        functools.partial(repeat_kernel, rows),
-        out_shape=(part, jax.ShapeDtypeStruct((group, group * rows), jnp.bfloat16)),
+        scratch_shapes=[
+            pltpu.VMEM(index.shape, index.dtype),
+            pltpu.SemaphoreType.DMA((2,)),
+        ],
+        compiler_params=PARAMS,
+    )(index, green)
+    part1, repeat = pl.pallas_call(
+        functools.partial(repeat_kernel, bounds[1], rows),
+        out_shape=(shapes[1], jax.ShapeDtypeStruct((group, group * rows), jnp.bfloat16)),
         in_specs=[HBM],
         out_specs=(VMEM, VMEM),
         scratch_shapes=[pltpu.SemaphoreType.DMA],
         compiler_params=PARAMS,
     )(green)
+    part2 = pl.pallas_call(
+        functools.partial(rest_kernel, bounds[2]),
+        out_shape=shapes[2],
+        in_specs=[HBM],
+        out_specs=VMEM,
+        scratch_shapes=[pltpu.SemaphoreType.DMA],
+        compiler_params=PARAMS,
+    )(green)
+    parts = (part0, part1, part2)
     bands = pl.pallas_call(
         bands_kernel,
         out_shape=jax.ShapeDtypeStruct(((taps + 1) * width, 2 * width), jnp.bfloat16),
@@ -253,19 +287,24 @@
     away_second = [p for p in even if p >= top and p & 4]
     keep_first = [p for p in even if p < top and not p & 2]
     keep_second = [p for p in even if p >= top and not p & 4]
-    away = away_first + away_second
     keep = keep_first + keep_second
 
-    def blocks(places, dtype, *arrived):
-        return uplift_blocks(places, rows, realizations, dtype, spread, (low, high), *arrived)
-
-    (to_send,) = blocks([[place | 1 for place in away]], jnp.bfloat16)
-    arrived_away = swap(to_send, 1)
-    (to_keep,) = blocks([[place | 1 for place in keep]], jnp.bfloat16)
-    arrived_keep = swap(to_keep, 1)
-    sent = blocks([away_first, away_second], jnp.bfloat16, arrived_away)
-    arrived_first = swap(sent[0], 2)
-    arrived_second = swap(sent[1], 4)
+    def blocks(groups, dtype, *arrived):
+        return uplift_blocks(groups, rows, realizations, dtype, spread, parts, *arrived)
+
+    def other(places):
+        return [place | 1 for place in places]
+
+    (other_first,) = blocks([other(away_first)], jnp.bfloat16)
+    arrived_first = swap(other_first, 1)
+    (other_second,) = blocks([other(away_second)], jnp.bfloat16)
+    arrived_second = swap(other_second, 1)
+    (sent_first,) = blocks([away_first], jnp.bfloat16, arrived_first)
+    arrived_first = swap(sent_first, 2)
+    (sent_second,) = blocks([away_second], jnp.bfloat16, arrived_second)
+    arrived_second = swap(sent_second, 4)
+    (other_keep,) = blocks([other(keep)], jnp.bfloat16)
+    arrived_keep = swap(other_keep, 1)
     kept = blocks([keep_first, keep_second], jnp.float32, arrived_keep)
     later = [8 << level for level in range(levels - 4)]
     first = reduce_halves(

time: 59.8 us -> 60.5 us (1.012)
    pallas_call x6 -> x9, Pallas kernels: 9.47 us -> 10.9 us  [the longest x6 5.44 us: uplift_blocks(): pl.pallas_call(functools.partial(uplift_kernel, groups, len(parts), rows)...]
    pallas_call x1, Pallas kernels: 2.56 us -> 1.7 us  [body(): pl.pallas_call(slip_kernel, out_shape=jax.ShapeDtypeStruct((1, realizatio...]
    ppermute x11 -> x12, waiting for transfers between devices: 11.8 us -> 12 us  [swap(): return lax.ppermute(block, 'space', [(i, i ^ bit) for i in range(count)])]
    ppermute x11 -> x12, starting transfers between devices: 19 us -> 19 us  [swap(): return lax.ppermute(block, 'space', [(i, i ^ bit) for i in range(count)])]
  transfers between devices with their start and end apart: 13 -> 14, of which waited for: 8 -> 9; matrix products, arithmetic and copies ran while one was open for 0% -> 0% of each run, Pallas kernels for 15% -> 16%
where the time goes in v3:
time: 60.5 us; the launch traced here: 60.3 us
  starting transfers between devices  28.5 us (47%)
  waiting for transfers between devices  15.7 us (26%)
  Pallas kernels  15.5 us (26%)
    ppermute x12, starting transfers between devices, swap(): return lax.ppermute(block, 'space', [(i, i ^ bit) for i in range(count)])  19 us
    ppermute x12, waiting for transfers between devices, swap(): return lax.ppermute(block, 'space', [(i, i ^ bit) for i in range(count)])  12 us
    ppermute x1, starting transfers between devices, body(): lax.ppermute(seafloor[rows - half:], 'space', [(i, i + 1) for i in range(...  7.55 us
    pallas_call x6, Pallas kernels, uplift_blocks(): pl.pallas_call(functools.partial(uplift_kernel, groups, len(parts), rows)...  5.44 us
    ppermute x1, waiting for transfers between devices, body(): lax.ppermute(seafloor[:half], 'space', [(i + 1, i) for i in range(count -...  3.73 us
    ppermute x1, starting transfers between devices, body(): lax.ppermute(seafloor[:half], 'space', [(i + 1, i) for i in range(count -...  1.92 us
    pallas_call x1, Pallas kernels, body(): pl.pallas_call(functools.partial(repeat_kernel, bounds[1], rows), out_sha...  1.9 us
    pallas_call x1, Pallas kernels, body(): pl.pallas_call(functools.partial(rest_kernel, bounds[2]), out_shape=shape...  1.9 us
  transfers between devices with their start and end apart: 14, of which 9 were waited for; matrix products, arithmetic and copies ran while one was open for 0% of the time, Pallas kernels for 16%

profile of v3, /device:TPU:1, one launch (start us, length us, event | category | flops | bytes accessed | tf_op | source)
XLA Modules:
  0.0 60.3 jit_solution(10967351704564275956)
XLA Ops:
  0.0 1.7 %shard_map.66 = bf16[1,32,128]{2,1,0:T(8,128)(2,1)S(1)} custom-call(bf16[32,4096]{1,0:T(8,128)(2,1)} %coefficients_hbm.1, bf16[4096,128]{1,0:T(8,128)(2,1)} %modes_hbm.1), custom_call_target="tpu_custom_call" | custom-call | tf_op jit(solution)/shard_map/pallas_call | solution.py:212
  1.7 0.1 collective-permute-start
  1.8 1.9 %shard_map.65 = (bf16[48,256,128]{2,1,0:T(8,128)(2,1)S(1)}, bf16[128,2048]{1,0:T(8,128)(2,1)S(1)}) custom-call(bf16[128,256,128]{2,1,0:T(8,128)(2,1)} %green_ref.5), custom_call_target="tpu_custom_call" | custom-call | tf_op jit(solution)/shard_map/pallas_call | solution.py:251
  3.7 1.9 %shard_map.68.refs_2_ = bf16[48,256,128]{2,1,0:T(8,128)(2,1)S(1)} custom-call(bf16[128,256,128]{2,1,0:T(8,128)(2,1)} %green_ref.5), custom_call_target="tpu_custom_call" | custom-call | tf_op jit(solution)/shard_map/pallas_call | solution.py:259
  5.6 1.6 %shard_map.64 = (bf16[32,256,128]{2,1,0:T(8,128)(2,1)S(1)}, bf16[2048,128]{1,0:T(8,128)(2,1)S(1)}) custom-call(s32[16,128]{1,0:T(8,128)} %bitcast.27, bf16[128,256,128]{2,1,0:T(8,128)(2,1)} %green_ref.5), custom_call_target="tpu_custom_call" | custom-call | tf_op jit(solution)/shard_map/pallas_call | solution.py:237
  7.2 0.0 collective-permute-done
  7.3 2.8 %collective-permute-start.1 = (bf16[2,32,128]{2,1,0:T(8,128)(2,1)S(1)}, bf16[2,32,128]{2,1,0:T(8,128)(2,1)S(1)}, u32[]{:S(2)}, u32[]{:S(2)}) collective-permute-start(bf16[2,32,128]{2,1,0:T(8,128)(2,1)S(1)} %pad_maximum_fusion.2), channel_id=1, source_target_pairs={{0,2},{1,3},{2,0},{3,1},{4,6},{5,7},{6,4},{7,5},{8,10},{9,11},{10,... | collective-permute-start | bytes 49160 | tf_op jit(solution)/shard_map/ppermute | solution.py:18
  10.1 1.1 %collective-permute-done.1 = bf16[2,32,128]{2,1,0:T(8,128)(2,1)S(1)} collective-permute-done((bf16[2,32,128]{2,1,0:T(8,128)(2,1)S(1)}, bf16[2,32,128]{2,1,0:T(8,128)(2,1)S(1)}, u32[]{:S(2)}, u32[]{:S(2)}) %collective-permute-start.1) | collective-permute-done | bytes 16416 | tf_op jit(solution)/shard_map/ppermute | solution.py:18
  11.2 1.5 %collective-permute-start.2 = (bf16[4,32,128]{2,1,0:T(8,128)(2,1)S(1)}, bf16[4,32,128]{2,1,0:T(8,128)(2,1)S(1)}, u32[]{:S(2)}, u32[]{:S(2)}) collective-permute-start(bf16[4,32,128]{2,1,0:T(8,128)(2,1)S(1)} %pad_maximum_fusion.1), channel_id=1, source_target_pairs={{0,4},{1,5},{2,6},{3,7},{4,0},{5,1},{6,2},{7,3},{8,12},{9,13},{10,... | collective-permute-start | bytes 98312 | tf_op jit(solution)/shard_map/ppermute | solution.py:18
  12.7 1.3 %collective-permute-done.2 = bf16[4,32,128]{2,1,0:T(8,128)(2,1)S(1)} collective-permute-done((bf16[4,32,128]{2,1,0:T(8,128)(2,1)S(1)}, bf16[4,32,128]{2,1,0:T(8,128)(2,1)S(1)}, u32[]{:S(2)}, u32[]{:S(2)}) %collective-permute-start.2) | collective-permute-done | bytes 32800 | tf_op jit(solution)/shard_map/ppermute | solution.py:18
  14.0 2.5 %collective-permute-start.3 = (bf16[8,32,128]{2,1,0:T(8,128)(2,1)S(1)}, bf16[8,32,128]{2,1,0:T(8,128)(2,1)S(1)}, u32[]{:S(2)}, u32[]{:S(2)}) collective-permute-start(bf16[8,32,128]{2,1,0:T(8,128)(2,1)S(1)} %pad_maximum_fusion), channel_id=1, source_target_pairs={{0,8},{1,9},{2,10},{3,11},{4,12},{5,13},{6,14},{7,15},{8,0},{9,1},... | collective-permute-start | bytes 196616 | tf_op jit(solution)/shard_map/ppermute | solution.py:18
  16.6 1.6 %collective-permute-done.3 = bf16[8,32,128]{2,1,0:T(8,128)(2,1)S(1)} collective-permute-done((bf16[8,32,128]{2,1,0:T(8,128)(2,1)S(1)}, bf16[8,32,128]{2,1,0:T(8,128)(2,1)S(1)}, u32[]{:S(2)}, u32[]{:S(2)}) %collective-permute-start.3) | collective-permute-done | bytes 65568 | tf_op jit(solution)/shard_map/ppermute | solution.py:18
  18.2 0.7 %shard_map.67.spread_ref = bf16[512,2048]{1,0:T(8,128)(2,1)S(1)} custom-call(bf16[2048,128]{1,0:T(8,128)(2,1)S(1)} %get-tuple-element.11.chosen_ref, bf16[128,2048]{1,0:T(8,128)(2,1)S(1)} %get-tuple-element.12.repeat_ref, bf16[16,32,128]{2,1,0:T(8,128)(2,1)S(1)} %constant_dynamic-update-slice_fusion.slip_ref), custom_call_target="tpu_custom_call" | custom-call | tf_op jit(solution)/shard_map/pallas_call | solution.py:276
  18.9 1.3 %shard_map.69 = bf16[4,16,32,128]{3,2,1,0:T(8,128)(2,1)S(1)} custom-call(bf16[512,2048]{1,0:T(8,128)(2,1)S(1)} %shard_map.67.spread_ref, bf16[32,256,128]{2,1,0:T(8,128)(2,1)S(1)} %get-tuple-element.13.refs_0_, bf16[48,256,128]{2,1,0:T(8,128)(2,1)S(1)} %get-tuple-element.14.refs_1_, bf16[48,256,128]{2,1,0:T(8,128)(2,1)S(1)} %shard_map.68.refs_2_), custom_call_target="tpu_custom_call" | custom-call | tf_op jit(solution)/shard_map/pallas_call | solution.py:125
  20.2 0.7 %shard_map.73 = bf16[2,16,32,128]{3,2,1,0:T(8,128)(2,1)S(1)} custom-call(bf16[512,2048]{1,0:T(8,128)(2,1)S(1)} %shard_map.67.spread_ref, bf16[32,256,128]{2,1,0:T(8,128)(2,1)S(1)} %get-tuple-element.13.refs_0_, bf16[48,256,128]{2,1,0:T(8,128)(2,1)S(1)} %get-tuple-element.14.refs_1_, bf16[48,256,128]{2,1,0:T(8,128)(2,1)S(1)} %shard_map.68.refs_2_), custom_call_target="tpu_custom_call" | custom-call | tf_op jit(solution)/shard_map/pallas_call | solution.py:125
  20.9 3.3 %collective-permute-start.4 = (bf16[4,16,32,128]{3,2,1,0:T(8,128)(2,1)S(1)}, bf16[4,16,32,128]{3,2,1,0:T(8,128)(2,1)S(1)}, u32[]{:S(2)}, u32[]{:S(2)}) collective-permute-start(bf16[4,16,32,128]{3,2,1,0:T(8,128)(2,1)S(1)} %shard_map.69), channel_id=1, source_target_pairs={{0,1},{1,0},{2,3},{3,2},{4,5},{5,4},{6,7},{7,6},{8,9},{9,8},{10,11... | collective-permute-start | bytes 1572872 | tf_op jit(solution)/shard_map/ppermute | solution.py:18
  24.2 0.1 collective-permute-start.8
  24.3 0.7 %shard_map.71 = bf16[2,16,32,128]{3,2,1,0:T(8,128)(2,1)S(1)} custom-call(bf16[512,2048]{1,0:T(8,128)(2,1)S(1)} %shard_map.67.spread_ref, bf16[32,256,128]{2,1,0:T(8,128)(2,1)S(1)} %get-tuple-element.13.refs_0_, bf16[48,256,128]{2,1,0:T(8,128)(2,1)S(1)} %get-tuple-element.14.refs_1_, bf16[48,256,128]{2,1,0:T(8,128)(2,1)S(1)} %shard_map.68.refs_2_), custom_call_target="tpu_custom_call" | custom-call | tf_op jit(solution)/shard_map/pallas_call | solution.py:125
  25.0 0.5 collective-permute-start.5
  25.5 0.6 %collective-permute-done.8.refs_3_ = bf16[2,16,32,128]{3,2,1,0:T(8,128)(2,1)S(1)} collective-permute-done((bf16[2,16,32,128]{3,2,1,0:T(8,128)(2,1)S(1)}, bf16[2,16,32,128]{3,2,1,0:T(8,128)(2,1)S(1)}, u32[]{:S(2)}, u32[]{:S(2)}) %collective-permute-start.8) | collective-permute-done | bytes 262176 | tf_op jit(solution)/shard_map/ppermute | solution.py:18
  26.1 0.7 %shard_map.74 = bf16[2,16,32,128]{3,2,1,0:T(8,128)(2,1)S(1)} custom-call(bf16[512,2048]{1,0:T(8,128)(2,1)S(1)} %shard_map.67.spread_ref, bf16[32,256,128]{2,1,0:T(8,128)(2,1)S(1)} %get-tuple-element.13.refs_0_, bf16[48,256,128]{2,1,0:T(8,128)(2,1)S(1)} %get-tuple-element.14.refs_1_, bf16[48,256,128]{2,1,0:T(8,128)(2,1)S(1)} %shard_map.68.refs_2_, ...), custom_call_target="tpu_custom_call" | custom-call | tf_op jit(solution)/shard_map/pallas_call | solution.py:125
  26.8 1.7 %collective-permute-start.9 = (bf16[2,16,32,128]{3,2,1,0:T(8,128)(2,1)S(1)}, bf16[2,16,32,128]{3,2,1,0:T(8,128)(2,1)S(1)}, u32[]{:S(2)}, u32[]{:S(2)}) collective-permute-start(bf16[2,16,32,128]{3,2,1,0:T(8,128)(2,1)S(1)} %shard_map.74), channel_id=1, source_target_pairs={{0,4},{1,5},{2,6},{3,7},{4,0},{5,1},{6,2},{7,3},{8,12},{9,13},{10,... | collective-permute-start | bytes 786440 | tf_op jit(solution)/shard_map/ppermute | solution.py:18
  28.5 0.0 collective-permute-done.5.refs_3_
  28.5 0.7 %shard_map.72 = bf16[2,16,32,128]{3,2,1,0:T(8,128)(2,1)S(1)} custom-call(bf16[512,2048]{1,0:T(8,128)(2,1)S(1)} %shard_map.67.spread_ref, bf16[32,256,128]{2,1,0:T(8,128)(2,1)S(1)} %get-tuple-element.13.refs_0_, bf16[48,256,128]{2,1,0:T(8,128)(2,1)S(1)} %get-tuple-element.14.refs_1_, bf16[48,256,128]{2,1,0:T(8,128)(2,1)S(1)} %shard_map.68.refs_2_, ...), custom_call_target="tpu_custom_call" | custom-call | tf_op jit(solution)/shard_map/pallas_call | solution.py:125
  29.3 1.3 %collective-permute-start.6 = (bf16[2,16,32,128]{3,2,1,0:T(8,128)(2,1)S(1)}, bf16[2,16,32,128]{3,2,1,0:T(8,128)(2,1)S(1)}, u32[]{:S(2)}, u32[]{:S(2)}) collective-permute-start(bf16[2,16,32,128]{3,2,1,0:T(8,128)(2,1)S(1)} %shard_map.72), channel_id=1, source_target_pairs={{0,2},{1,3},{2,0},{3,1},{4,6},{5,7},{6,4},{7,5},{8,10},{9,11},{10,... | collective-permute-start | bytes 786440 | tf_op jit(solution)/shard_map/ppermute | solution.py:18
  30.6 0.0 collective-permute-done.4.refs_3_
  30.6 1.3 %shard_map.70 = (f32[2,16,32,128]{3,2,1,0:T(8,128)S(1)}, f32[2,16,32,128]{3,2,1,0:T(8,128)S(1)}) custom-call(bf16[512,2048]{1,0:T(8,128)(2,1)S(1)} %shard_map.67.spread_ref, bf16[32,256,128]{2,1,0:T(8,128)(2,1)S(1)} %get-tuple-element.13.refs_0_, bf16[48,256,128]{2,1,0:T(8,128)(2,1)S(1)} %get-tuple-element.14.refs_1_, ...), custom_call_target="tpu_custom_call" | custom-call | tf_op jit(solution)/shard_map/pallas_call | solution.py:125
  31.9 0.0 copy-start
  31.9 2.9 %collective-permute-done.9 = bf16[2,16,32,128]{3,2,1,0:T(8,128)(2,1)S(1)} collective-permute-done((bf16[2,16,32,128]{3,2,1,0:T(8,128)(2,1)S(1)}, bf16[2,16,32,128]{3,2,1,0:T(8,128)(2,1)S(1)}, u32[]{:S(2)}, u32[]{:S(2)}) %collective-permute-start.9) | collective-permute-done | bytes 262176 | tf_op jit(solution)/shard_map/ppermute | solution.py:18
  34.7 0.0 copy-start.1
  34.7 0.1 add_bitcast_fusion
  34.8 1.3 %collective-permute-start.10 = (bf16[1,16,32,128]{3,2,1,0:T(8,128)(2,1)S(1)}, bf16[1,16,32,128]{3,2,1,0:T(8,128)(2,1)S(1)}, u32[]{:S(2)}, u32[]{:S(2)}) collective-permute-start(bf16[1,16,32,128]{3,2,1,0:T(8,128)(2,1)S(1)} %fusion.7), channel_id=1, source_target_pairs={{0,2},{1,3},{2,0},{3,1},{4,6},{5,7},{6,4},{7,5},{8,10},{9,11},{10,... | collective-permute-start | bytes 393224 | tf_op jit(solution)/shard_map/ppermute | solution.py:18
  36.1 0.4 collective-permute-done.6
  36.5 0.1 add_bitcast_fusion.1
  36.6 1.0 %collective-permute-start.7 = (bf16[1,16,32,128]{3,2,1,0:T(8,128)(2,1)S(1)}, bf16[1,16,32,128]{3,2,1,0:T(8,128)(2,1)S(1)}, u32[]{:S(2)}, u32[]{:S(2)}) collective-permute-start(bf16[1,16,32,128]{3,2,1,0:T(8,128)(2,1)S(1)} %fusion.6), channel_id=1, source_target_pairs={{0,4},{1,5},{2,6},{3,7},{4,0},{5,1},{6,2},{7,3},{8,12},{9,13},{10,... | collective-permute-start | bytes 393224 | tf_op jit(solution)/shard_map/ppermute | solution.py:18
  37.6 1.2 %collective-permute-done.10 = bf16[1,16,32,128]{3,2,1,0:T(8,128)(2,1)S(1)} collective-permute-done((bf16[1,16,32,128]{3,2,1,0:T(8,128)(2,1)S(1)}, bf16[1,16,32,128]{3,2,1,0:T(8,128)(2,1)S(1)}, u32[]{:S(2)}, u32[]{:S(2)}) %collective-permute-start.10) | collective-permute-done | bytes 131104 | tf_op jit(solution)/shard_map/ppermute | solution.py:18
  38.8 3.0 %collective-permute-start.11 = (bf16[1,16,32,128]{3,2,1,0:T(8,128)(2,1)S(1)}, bf16[1,16,32,128]{3,2,1,0:T(8,128)(2,1)S(1)}, u32[]{:S(2)}, u32[]{:S(2)}) collective-permute-start(bf16[1,16,32,128]{3,2,1,0:T(8,128)(2,1)S(1)} %fusion.1), channel_id=1, source_target_pairs={{0,8},{1,9},{2,10},{3,11},{4,12},{5,13},{6,14},{7,15},{8,0},{9,1},... | collective-permute-start | bytes 393224 | tf_op jit(solution)/shard_map/ppermute | solution.py:18
  41.9 0.0 collective-permute-done.7
  41.9 2.9 %collective-permute-done.11 = bf16[1,16,32,128]{3,2,1,0:T(8,128)(2,1)S(1)} collective-permute-done((bf16[1,16,32,128]{3,2,1,0:T(8,128)(2,1)S(1)}, bf16[1,16,32,128]{3,2,1,0:T(8,128)(2,1)S(1)}, u32[]{:S(2)}, u32[]{:S(2)}) %collective-permute-start.11) | collective-permute-done | bytes 131104 | tf_op jit(solution)/shard_map/ppermute | solution.py:18
  44.8 7.6 %collective-permute-start.12 = (bf16[16,32,128]{2,1,0:T(8,128)(2,1)S(1)}, bf16[16,32,128]{2,1,0:T(8,128)(2,1)S(1)}, u32[]{:S(2)}, u32[]{:S(2)}) collective-permute-start(bf16[16,32,128]{2,1,0:T(8,128)(2,1)S(1)} %fusion.5.own_ref), channel_id=1, source_target_pairs={{0,1},{1,2},{2,3},{3,4},{4,5},{5,6},{6,7},{7,8},{8,9},{9,10},{10,1... | collective-permute-start | bytes 393224 | tf_op jit(solution)/shard_map/ppermute | solution.py:319
  52.4 1.9 %collective-permute-start.13 = (bf16[16,32,128]{2,1,0:T(8,128)(2,1)S(1)}, bf16[16,32,128]{2,1,0:T(8,128)(2,1)S(1)}, u32[]{:S(2)}, u32[]{:S(2)}) collective-permute-start(bf16[16,32,128]{2,1,0:T(8,128)(2,1)S(1)} %fusion.5.own_ref), channel_id=1, source_target_pairs={{1,0},{2,1},{3,2},{4,3},{5,4},{6,5},{7,6},{8,7},{9,8},{10,9},{11,1... | collective-permute-start | bytes 393224 | tf_op jit(solution)/shard_map/ppermute | solution.py:320
  54.3 0.0 copy-done
  54.3 0.6 %shard_map.75.bands_ref = bf16[4352,256]{1,0:T(8,128)(2,1)S(1)} custom-call(f32[33,33]{1,0:T(8,128)S(1)} %copy-done), custom_call_target="tpu_custom_call" | custom-call | tf_op jit(solution)/shard_map/pallas_call | solution.py:268
  54.9 0.0 collective-permute-done.12.low_ref
  54.9 3.7 %collective-permute-done.13.high_ref = bf16[16,32,128]{2,1,0:T(8,128)(2,1)S(1)} collective-permute-done((bf16[16,32,128]{2,1,0:T(8,128)(2,1)S(1)}, bf16[16,32,128]{2,1,0:T(8,128)(2,1)S(1)}, u32[]{:S(2)}, u32[]{:S(2)}) %collective-permute-start.13) | collective-permute-done | bytes 131104 | tf_op jit(solution)/shard_map/ppermute | solution.py:320
  58.6 0.0 copy-done.1
  58.6 1.6 %shard_map.76 = f32[32,16,128]{2,1,0:T(8,128)} custom-call(bf16[16,32,128]{2,1,0:T(8,128)(2,1)S(1)} %collective-permute-done.12.low_ref, bf16[16,32,128]{2,1,0:T(8,128)(2,1)S(1)} %fusion.5.own_ref, bf16[16,32,128]{2,1,0:T(8,128)(2,1)S(1)} %collective-permute-done.13.high_ref, bf16[4352,256]{1,0:T(8,128)(2,1)S(1)} %shard_map.75.bands_ref, s32[16,128]{1,0:T(8,128)S(1)} %copy-done.1), custom_call_target="tpu_custom_call" | custom-call | tf_op jit(solution)/shard_map/pallas_call | solution.py:321
  (12 shorter events, 0.2 us)
Async XLA Ops:
  1.7 5.5 %collective-permute-start = (bf16[1,32,128]{2,1,0:T(8,128)(2,1)S(1)}, bf16[1,32,128]{2,1,0:T(8,128)(2,1)S(1)}, u32[]{:S(2)}, u32[]{:S(2)}) collective-permute-start(bf16[1,32,128]{2,1,0:T(8,128)(2,1)S(1)} %shard_map.66), channel_id=1, source_target_pairs={{0,1},{1,0},{2,3},{3,2},{4,5},{5,4},{6,7},{7,6},{8,9},{9,8},{10,11... | collective-permute-start | bytes 24584 | tf_op jit(solution)/shard_map/ppermute | solution.py:18
  7.3 3.9 %collective-permute-start.1 = (bf16[2,32,128]{2,1,0:T(8,128)(2,1)S(1)}, bf16[2,32,128]{2,1,0:T(8,128)(2,1)S(1)}, u32[]{:S(2)}, u32[]{:S(2)}) collective-permute-start(bf16[2,32,128]{2,1,0:T(8,128)(2,1)S(1)} %pad_maximum_fusion.2), channel_id=1, source_target_pairs={{0,2},{1,3},{2,0},{3,1},{4,6},{5,7},{6,4},{7,5},{8,10},{9,11},{10,... | collective-permute-start | bytes 49160 | tf_op jit(solution)/shard_map/ppermute | solution.py:18
  11.2 2.8 %collective-permute-start.2 = (bf16[4,32,128]{2,1,0:T(8,128)(2,1)S(1)}, bf16[4,32,128]{2,1,0:T(8,128)(2,1)S(1)}, u32[]{:S(2)}, u32[]{:S(2)}) collective-permute-start(bf16[4,32,128]{2,1,0:T(8,128)(2,1)S(1)} %pad_maximum_fusion.1), channel_id=1, source_target_pairs={{0,4},{1,5},{2,6},{3,7},{4,0},{5,1},{6,2},{7,3},{8,12},{9,13},{10,... | collective-permute-start | bytes 98312 | tf_op jit(solution)/shard_map/ppermute | solution.py:18
  14.0 4.2 %collective-permute-start.3 = (bf16[8,32,128]{2,1,0:T(8,128)(2,1)S(1)}, bf16[8,32,128]{2,1,0:T(8,128)(2,1)S(1)}, u32[]{:S(2)}, u32[]{:S(2)}) collective-permute-start(bf16[8,32,128]{2,1,0:T(8,128)(2,1)S(1)} %pad_maximum_fusion), channel_id=1, source_target_pairs={{0,8},{1,9},{2,10},{3,11},{4,12},{5,13},{6,14},{7,15},{8,0},{9,1},... | collective-permute-start | bytes 196616 | tf_op jit(solution)/shard_map/ppermute | solution.py:18
  20.9 9.6 %collective-permute-start.4 = (bf16[4,16,32,128]{3,2,1,0:T(8,128)(2,1)S(1)}, bf16[4,16,32,128]{3,2,1,0:T(8,128)(2,1)S(1)}, u32[]{:S(2)}, u32[]{:S(2)}) collective-permute-start(bf16[4,16,32,128]{3,2,1,0:T(8,128)(2,1)S(1)} %shard_map.69), channel_id=1, source_target_pairs={{0,1},{1,0},{2,3},{3,2},{4,5},{5,4},{6,7},{7,6},{8,9},{9,8},{10,11... | collective-permute-start | bytes 1572872 | tf_op jit(solution)/shard_map/ppermute | solution.py:18
  24.2 1.9 %collective-permute-start.8 = (bf16[2,16,32,128]{3,2,1,0:T(8,128)(2,1)S(1)}, bf16[2,16,32,128]{3,2,1,0:T(8,128)(2,1)S(1)}, u32[]{:S(2)}, u32[]{:S(2)}) collective-permute-start(bf16[2,16,32,128]{3,2,1,0:T(8,128)(2,1)S(1)} %shard_map.73), channel_id=1, source_target_pairs={{0,1},{1,0},{2,3},{3,2},{4,5},{5,4},{6,7},{7,6},{8,9},{9,8},{10,11... | collective-permute-start | bytes 786440 | tf_op jit(solution)/shard_map/ppermute | solution.py:18
  25.0 3.5 %collective-permute-start.5 = (bf16[2,16,32,128]{3,2,1,0:T(8,128)(2,1)S(1)}, bf16[2,16,32,128]{3,2,1,0:T(8,128)(2,1)S(1)}, u32[]{:S(2)}, u32[]{:S(2)}) collective-permute-start(bf16[2,16,32,128]{3,2,1,0:T(8,128)(2,1)S(1)} %shard_map.71), channel_id=1, source_target_pairs={{0,1},{1,0},{2,3},{3,2},{4,5},{5,4},{6,7},{7,6},{8,9},{9,8},{10,11... | collective-permute-start | bytes 786440 | tf_op jit(solution)/shard_map/ppermute | solution.py:18
  26.8 7.9 %collective-permute-start.9 = (bf16[2,16,32,128]{3,2,1,0:T(8,128)(2,1)S(1)}, bf16[2,16,32,128]{3,2,1,0:T(8,128)(2,1)S(1)}, u32[]{:S(2)}, u32[]{:S(2)}) collective-permute-start(bf16[2,16,32,128]{3,2,1,0:T(8,128)(2,1)S(1)} %shard_map.74), channel_id=1, source_target_pairs={{0,4},{1,5},{2,6},{3,7},{4,0},{5,1},{6,2},{7,3},{8,12},{9,13},{10,... | collective-permute-start | bytes 786440 | tf_op jit(solution)/shard_map/ppermute | solution.py:18
  29.3 7.3 %collective-permute-start.6 = (bf16[2,16,32,128]{3,2,1,0:T(8,128)(2,1)S(1)}, bf16[2,16,32,128]{3,2,1,0:T(8,128)(2,1)S(1)}, u32[]{:S(2)}, u32[]{:S(2)}) collective-permute-start(bf16[2,16,32,128]{3,2,1,0:T(8,128)(2,1)S(1)} %shard_map.72), channel_id=1, source_target_pairs={{0,2},{1,3},{2,0},{3,1},{4,6},{5,7},{6,4},{7,5},{8,10},{9,11},{10,... | collective-permute-start | bytes 786440 | tf_op jit(solution)/shard_map/ppermute | solution.py:18
  31.9 22.4 %copy-start = (f32[33,33]{1,0:T(8,128)S(1)}, f32[33,33]{1,0:T(8,128)}, u32[]{:S(2)}) copy-start(f32[33,33]{1,0:T(8,128)} %kernel_ref.1) | copy-start | bytes 13072
  34.7 23.9 %copy-start.1 = (s32[16,128]{1,0:T(8,128)S(1)}, s32[16,128]{1,0:T(8,128)}, u32[]{:S(2)}) copy-start(s32[16,128]{1,0:T(8,128)} %mask_ref.1) | copy-start | bytes 24580
  34.8 3.9 %collective-permute-start.10 = (bf16[1,16,32,128]{3,2,1,0:T(8,128)(2,1)S(1)}, bf16[1,16,32,128]{3,2,1,0:T(8,128)(2,1)S(1)}, u32[]{:S(2)}, u32[]{:S(2)}) collective-permute-start(bf16[1,16,32,128]{3,2,1,0:T(8,128)(2,1)S(1)} %fusion.7), channel_id=1, source_target_pairs={{0,2},{1,3},{2,0},{3,1},{4,6},{5,7},{6,4},{7,5},{8,10},{9,11},{10,... | collective-permute-start | bytes 393224 | tf_op jit(solution)/shard_map/ppermute | solution.py:18
  36.6 5.2 %collective-permute-start.7 = (bf16[1,16,32,128]{3,2,1,0:T(8,128)(2,1)S(1)}, bf16[1,16,32,128]{3,2,1,0:T(8,128)(2,1)S(1)}, u32[]{:S(2)}, u32[]{:S(2)}) collective-permute-start(bf16[1,16,32,128]{3,2,1,0:T(8,128)(2,1)S(1)} %fusion.6), channel_id=1, source_target_pairs={{0,4},{1,5},{2,6},{3,7},{4,0},{5,1},{6,2},{7,3},{8,12},{9,13},{10,... | collective-permute-start | bytes 393224 | tf_op jit(solution)/shard_map/ppermute | solution.py:18
  38.8 5.9 %collective-permute-start.11 = (bf16[1,16,32,128]{3,2,1,0:T(8,128)(2,1)S(1)}, bf16[1,16,32,128]{3,2,1,0:T(8,128)(2,1)S(1)}, u32[]{:S(2)}, u32[]{:S(2)}) collective-permute-start(bf16[1,16,32,128]{3,2,1,0:T(8,128)(2,1)S(1)} %fusion.1), channel_id=1, source_target_pairs={{0,8},{1,9},{2,10},{3,11},{4,12},{5,13},{6,14},{7,15},{8,0},{9,1},... | collective-permute-start | bytes 393224 | tf_op jit(solution)/shard_map/ppermute | solution.py:18
  44.8 10.1 %collective-permute-start.12 = (bf16[16,32,128]{2,1,0:T(8,128)(2,1)S(1)}, bf16[16,32,128]{2,1,0:T(8,128)(2,1)S(1)}, u32[]{:S(2)}, u32[]{:S(2)}) collective-permute-start(bf16[16,32,128]{2,1,0:T(8,128)(2,1)S(1)} %fusion.5.own_ref), channel_id=1, source_target_pairs={{0,1},{1,2},{2,3},{3,4},{4,5},{5,6},{6,7},{7,8},{8,9},{9,10},{10,1... | collective-permute-start | bytes 393224 | tf_op jit(solution)/shard_map/ppermute | solution.py:319
  52.4 6.3 %collective-permute-start.13 = (bf16[16,32,128]{2,1,0:T(8,128)(2,1)S(1)}, bf16[16,32,128]{2,1,0:T(8,128)(2,1)S(1)}, u32[]{:S(2)}, u32[]{:S(2)}) collective-permute-start(bf16[16,32,128]{2,1,0:T(8,128)(2,1)S(1)} %fusion.5.own_ref), channel_id=1, source_target_pairs={{1,0},{2,1},{3,2},{4,3},{5,4},{6,5},{7,6},{8,7},{9,8},{10,9},{11,1... | collective-permute-start | bytes 393224 | tf_op jit(solution)/shard_map/ppermute | solution.py:320

commit v4 on v3

v4 whole, which is shorter than its diff:
```python
import functools

import jax
import jax.numpy as jnp
from jax import lax
from jax.experimental import pallas as pl
from jax.experimental.pallas import tpu as pltpu
from jax.sharding import PartitionSpec as P


VMEM = pl.BlockSpec(memory_space=pltpu.VMEM)
HBM = pl.BlockSpec(memory_space=pltpu.HBM)
STREAMS = 2
PARAMS = pltpu.CompilerParams(vmem_limit_bytes=20 << 20)


def swap(block, bit, odd_bit=None):
    count = lax.axis_size("space")
    bits = (bit, bit if odd_bit is None else odd_bit)
    return lax.ppermute(block, "space", [(i, i ^ bits[i & 1]) for i in range(count)])


def slip_kernel(coefficients_hbm, modes_hbm, slip_ref, coefficients_ref, modes_ref, semaphores):
    parts = semaphores.shape[0] - 1
    depth = modes_ref.shape[0] // parts
    first = pltpu.make_async_copy(coefficients_hbm, coefficients_ref, semaphores.at[parts])
    first.start()
    copies = []
    for part in range(parts):
        lines = pl.ds(part * depth, depth)
        copies.append(
            pltpu.make_async_copy(
                modes_hbm.at[lines], modes_ref.at[lines], semaphores.at[part]
            )
        )
        copies[part].start()
    first.wait()
    field = jnp.zeros(slip_ref.shape[1:], jnp.float32)
    for part in range(parts):
        lines = slice(part * depth, (part + 1) * depth)
        copies[part].wait()
        field += jnp.dot(
            coefficients_ref[:, lines], modes_ref[lines], preferred_element_type=jnp.float32
        )
    slip_ref[0] = jnp.exp(0.5 * field).astype(slip_ref.dtype)


def load(green_ref, part_ref, semaphore, start, parity):
    copy = pltpu.make_async_copy(
        green_ref.at[pl.ds(start, part_ref.shape[0]), :, parity], part_ref, semaphore
    )
    copy.start()
    return copy


def choose_kernel(columns, index_hbm, green_ref, part_ref, chosen_ref, index_ref, semaphores):
    me = lax.axis_index("space")
    fetch = pltpu.make_async_copy(index_hbm, index_ref, semaphores.at[0])
    fetch.start()
    copy = load(green_ref, part_ref, semaphores.at[1], 0, 1 - (me & 1))
    group = index_ref.shape[1]
    fetch.wait()
    for side in range(2):
        row_ids = index_ref[pl.ds(me ^ side, 1), :]
        position = ((row_ids // columns) ^ me) * columns + row_ids % columns
        for first in range(0, chosen_ref.shape[0], group):
            row = lax.broadcasted_iota(jnp.int32, (group, group), 0) + first
            chosen_ref[first : first + group, side * group : (side + 1) * group] = jnp.where(
                row == position, 1.0, 0.0
            ).astype(jnp.bfloat16)
    copy.wait()


def repeat_kernel(start, rows, green_ref, part_ref, repeat_ref, semaphore):
    copy = load(green_ref, part_ref, semaphore, start, lax.axis_index("space") & 1)
    source = lax.broadcasted_iota(jnp.int32, repeat_ref.shape, 0)
    target = lax.broadcasted_iota(jnp.int32, repeat_ref.shape, 1)
    near = (target >= source * rows) & (target < (source + 1) * rows)
    repeat_ref[...] = jnp.where(near, 1.0, 0.0).astype(jnp.bfloat16)
    copy.wait()


def rest_kernel(start, green_ref, part_ref, semaphore):
    load(green_ref, part_ref, semaphore, start, lax.axis_index("space") & 1).wait()


def select_kernel(chosen_ref, repeat_ref, slip_ref, spread_ref):
    owners, realizations, _ = slip_ref.shape
    rows = spread_ref.shape[0] // realizations
    group, depth = repeat_ref.shape
    slip = jnp.concatenate([slip_ref[owner] for owner in range(owners)], axis=1)
    picked = jnp.dot(slip, chosen_ref[...], preferred_element_type=jnp.float32)
    picked = picked.astype(jnp.bfloat16)
    row_of = lax.broadcasted_iota(jnp.int32, (realizations, depth), 1) % rows
    for side in range(2):
        wide = jnp.dot(
            picked[:, side * group : (side + 1) * group],
            repeat_ref[...],
            preferred_element_type=jnp.float32,
        )
        for row in range(rows):
            spread_ref[
                row * realizations : (row + 1) * realizations, side * depth : (side + 1) * depth
            ] = jnp.where(row_of == row, wide, 0.0).astype(jnp.bfloat16)


def turned(place):
    return (place & ~3) | ((place & 1) << 1) | ((place >> 1) & 1)


def uplift_kernel(places, stream, spread_ref, *refs):
    parts, out_ref = refs[:-1], refs[-1]
    rows, width = parts[0].shape[2:]
    me = lax.axis_index("space")

    def block(place):
        pair = (me >> 1) ^ jnp.where((me & 1) == 0, place, turned(place))
        pieces = [ref[:, pair].reshape(ref.shape[0] * rows, width) for ref in parts]
        return jnp.concatenate(pieces, axis=0)

    columns = jnp.concatenate([block(place) for place in places], axis=1)
    depth = out_ref.shape[1] * out_ref.shape[2]
    lines = spread_ref[stream * depth : (stream + 1) * depth, :]
    value = jnp.dot(lines, columns, preferred_element_type=jnp.float32)
    for slot in range(len(places)):
        part = value[:, slot * width : (slot + 1) * width].reshape(out_ref.shape[1:])
        out_ref[slot] = part.astype(out_ref.dtype)


def uplift_blocks(places, stream, realizations, dtype, spread, parts):
    rows, width = parts[0].shape[2:]
    return pl.pallas_call(
        functools.partial(uplift_kernel, places, stream),
        out_shape=jax.ShapeDtypeStruct((len(places), rows // STREAMS, realizations, width), dtype),
        in_specs=[VMEM] * (1 + len(parts)),
        out_specs=VMEM,
        compiler_params=PARAMS,
    )(spread, *parts)


def bands_kernel(kernel_ref, bands_ref):
    taps = kernel_ref.shape[0]
    half = taps // 2
    width = bands_ref.shape[1] // 2
    weights = (kernel_ref[...] / jnp.sum(kernel_ref[...])).astype(jnp.bfloat16)
    first = lax.broadcasted_iota(jnp.int32, (taps, width), 0)
    second = lax.broadcasted_iota(jnp.int32, (taps, width), 1)
    mirror = jnp.where(first + second == taps - 1, 1.0, 0.0).astype(jnp.bfloat16)
    lines = jnp.dot(weights, mirror, preferred_element_type=jnp.float32)
    source = lax.broadcasted_iota(jnp.int32, (width, width), 0)
    target = lax.broadcasted_iota(jnp.int32, (width, width), 1)
    inside = jnp.abs(source - target) <= half
    for tap in range(-1, taps + 1):
        if 0 <= tap < taps:
            line = jnp.broadcast_to(lines[tap : tap + 1, :], (width, width))
            rolled = pltpu.roll(line, width - half, 1, stride=1, stride_axis=0)
            band = jnp.where(inside, rolled, 0.0).astype(jnp.bfloat16)
        else:
            band = jnp.zeros((width, width), jnp.bfloat16)
        if tap >= 0:
            bands_ref[tap * width : (tap + 1) * width, :width] = band
        if tap < taps:
            bands_ref[(tap + 1) * width : (tap + 2) * width, width:] = band


def smooth_kernel(beside_ref, across_ref, own_ref, bands_ref, mask_ref, out_ref, tall_ref, lines_ref):
    rows, realizations, width = own_ref.shape
    half = (tall_ref.shape[0] - rows) // 2
    odd = lax.axis_index("space") & 1
    for parity, before_ref, after_ref in ((0, across_ref, beside_ref), (1, beside_ref, across_ref)):

        @pl.when(odd == parity)
        def _():
            tall_ref[:half] = before_ref[rows - half :]
            tall_ref[half + rows :] = after_ref[:half]

    tall_ref[half : half + rows] = own_ref[...]
    for shift in range(2 * half + 2):
        for pair in range(rows // 2):
            lines_ref[
                pair * realizations : (pair + 1) * realizations,
                shift * width : (shift + 1) * width,
            ] = tall_ref[2 * pair + shift]
    value = jnp.dot(lines_ref[...], bands_ref[...], preferred_element_type=jnp.float32)
    value = value.reshape(rows // 2, realizations, 2 * width)
    both = jnp.stack([value[:, :, :width], value[:, :, width:]], axis=1)
    both = both.reshape(rows, realizations, width)
    mask = mask_ref[...].astype(jnp.float32)
    out_ref[...] = jnp.transpose(both, (1, 0, 2)) * mask[None]


def body(coefficients, kl_modes, green, sub_index, kernel, wet_mask):
    realizations, _ = coefficients.shape
    columns = kl_modes.shape[1]
    group, _, width = green.shape
    rows = wet_mask.shape[0]
    taps = kernel.shape[0]
    half = taps // 2
    count = lax.axis_size("space")
    levels = count.bit_length() - 1
    assert 1 << levels == count and half <= rows and levels >= 4
    green = green.reshape(group, count // 2, 2, rows, width)
    green = pltpu.with_memory_space_constraint(green, pltpu.HBM)

    slip = pl.pallas_call(
        slip_kernel,
        out_shape=jax.ShapeDtypeStruct((1, realizations, columns), jnp.bfloat16),
        in_specs=[HBM, HBM],
        out_specs=VMEM,
        scratch_shapes=[
            pltpu.VMEM(coefficients.shape, coefficients.dtype),
            pltpu.VMEM(kl_modes.shape, kl_modes.dtype),
            pltpu.SemaphoreType.DMA((5,)),
        ],
        compiler_params=PARAMS,
    )(
        pltpu.with_memory_space_constraint(coefficients, pltpu.HBM),
        pltpu.with_memory_space_constraint(kl_modes, pltpu.HBM),
    )
    for level in range(levels):
        arrived = swap(slip, 1 << level)
        slip = jnp.concatenate([slip, arrived], axis=0)

    def part(depth):
        return jax.ShapeDtypeStruct((depth, count // 2, rows, width), green.dtype)

    index = pltpu.with_memory_space_constraint(sub_index.reshape(-1, group), pltpu.HBM)
    away, chosen = pl.pallas_call(
        functools.partial(choose_kernel, columns),
        out_shape=(
            part(group),
            jax.ShapeDtypeStruct((sub_index.shape[0], 2 * group), jnp.bfloat16),
        ),
        in_specs=[HBM, HBM],
        out_specs=(VMEM, VMEM),
        scratch_shapes=[
            pltpu.VMEM(index.shape, index.dtype),
            pltpu.SemaphoreType.DMA((2,)),
        ],
        compiler_params=PARAMS,
    )(index, green)
    beside = swap(away, 1)
    own_low, repeat = pl.pallas_call(
        functools.partial(repeat_kernel, 0, rows),
        out_shape=(
            part(group // 2),
            jax.ShapeDtypeStruct((group, group * rows), jnp.bfloat16),
        ),
        in_specs=[HBM],
        out_specs=(VMEM, VMEM),
        scratch_shapes=[pltpu.SemaphoreType.DMA],
        compiler_params=PARAMS,
    )(green)
    own_high = pl.pallas_call(
        functools.partial(rest_kernel, group // 2),
        out_shape=part(group - group // 2),
        in_specs=[HBM],
        out_specs=VMEM,
        scratch_shapes=[pltpu.SemaphoreType.DMA],
        compiler_params=PARAMS,
    )(green)
    parts = (own_low, own_high, beside)
    bands = pl.pallas_call(
        bands_kernel,
        out_shape=jax.ShapeDtypeStruct(((taps + 1) * width, 2 * width), jnp.bfloat16),
        in_specs=[VMEM],
        out_specs=VMEM,
        compiler_params=PARAMS,
    )(kernel)

    spread = pl.pallas_call(
        select_kernel,
        out_shape=jax.ShapeDtypeStruct((rows * realizations, 2 * group * rows), jnp.bfloat16),
        in_specs=[VMEM] * 3,
        out_specs=VMEM,
        compiler_params=PARAMS,
    )(chosen, repeat, slip)

    places = list(range(count // 2))
    streams = range(STREAMS)
    arrived, kept = [], []
    for stream in streams:
        sent = uplift_blocks(places[1::2], stream, realizations, jnp.bfloat16, spread, parts)
        arrived.append(swap(sent, 2, 4))
    for stream in streams:
        block = uplift_blocks(places[::2], stream, realizations, jnp.float32, spread, parts)
        kept.append(block + arrived[stream].astype(jnp.float32))
    for level in range(2, levels):
        for stream in streams:
            pairs = kept[stream].reshape((-1, 2) + kept[stream].shape[1:])
            sent = pairs[:, 1].astype(jnp.bfloat16)
            moved = swap(sent, 4, 2) if level == 2 else swap(sent, 1 << level)
            kept[stream] = pairs[:, 0] + moved.astype(jnp.float32)
    seafloor = jnp.concatenate([block[0].astype(jnp.bfloat16) for block in kept], axis=0)

    crossing = [(i, i + 1) for i in range(1, count - 1, 2)]
    crossing += [(target, source) for source, target in crossing]
    across = lax.ppermute(seafloor, "space", crossing)
    beside = swap(seafloor, 1)
    return pl.pallas_call(
        smooth_kernel,
        out_shape=jax.ShapeDtypeStruct((realizations, rows, width), jnp.float32),
        in_specs=[VMEM] * 5,
        out_specs=VMEM,
        scratch_shapes=[
            pltpu.VMEM((rows + 2 * half, realizations, width), jnp.bfloat16),
            pltpu.VMEM((rows // 2 * realizations, (taps + 1) * width), jnp.bfloat16),
        ],
        compiler_params=PARAMS,
    )(beside, across, seafloor, bands, wet_mask)


def solution(mesh):
    placed = (
        P("parts", None),
        P("parts", "space"),
        P(("parts", "space"), None, None),
        P("parts"),
        P(),
        P(("parts", "space"), None),
    )
    return jax.shard_map(
        body, mesh=mesh, in_specs=placed, out_specs=P("parts", "space", None), check_vma=False
    )
```

time: 60.5 us -> 58.6 us (0.969)
  the two profiles are of different devices: /device:TPU:1 before, /device:TPU:27 now
where the time goes in v4:
time: 58.6 us; the launch traced here: 58.4 us
  waiting for transfers between devices  24.3 us (41%)
  starting transfers between devices  17.6 us (30%)
  Pallas kernels  15.9 us (27%)
    ppermute x12, waiting for transfers between devices, swap(): lax.ppermute(block, 'space', [(i, i ^ bits[i & 1]) for i in range(count)])  20.3 us
    ppermute x12, starting transfers between devices, swap(): lax.ppermute(block, 'space', [(i, i ^ bits[i & 1]) for i in range(count)])  14.5 us
    pallas_call x4, Pallas kernels, uplift_blocks(): pl.pallas_call(functools.partial(uplift_kernel, places, stream), out_shap...  5.17 us
    ppermute x1, waiting for transfers between devices, body(): across = lax.ppermute(seafloor, 'space', crossing)  4.01 us
    ppermute x1, starting transfers between devices, body(): across = lax.ppermute(seafloor, 'space', crossing)  3.03 us
    pallas_call x1, Pallas kernels, body(): pl.pallas_call(functools.partial(choose_kernel, columns), out_shape=(part...  2.22 us
    pallas_call x1, Pallas kernels, body(): pl.pallas_call(slip_kernel, out_shape=jax.ShapeDtypeStruct((1, realizatio...  1.7 us
    pallas_call x1, Pallas kernels, body(): pl.pallas_call(smooth_kernel, out_shape=jax.ShapeDtypeStruct((realization...  1.69 us
  transfers between devices with their start and end apart: 13, of which 10 were waited for; matrix products, arithmetic and copies ran while one was open for 1% of the time, Pallas kernels for 18%

profile of v4, /device:TPU:27, one launch (start us, length us, event | category | flops | bytes accessed | tf_op | source)
XLA Modules:
  0.0 58.4 jit_solution(18280429568394777089)
XLA Ops:
  0.0 2.2 %shard_map.64 = (bf16[128,8,16,128]{3,2,1,0:T(8,128)(2,1)S(1)}, bf16[2048,256]{1,0:T(8,128)(2,1)S(1)}) custom-call(s32[16,128]{1,0:T(8,128)} %bitcast.55, bf16[128,8,2,16,128]{4,3,2,1,0:T(8,128)(2,1)} %bitcast.48), custom_call_target="tpu_custom_call" | custom-call | tf_op jit(solution)/shard_map/pallas_call | solution.py:228
  2.2 0.7 %collective-permute-start.4 = (bf16[128,8,16,128]{3,2,1,0:T(8,128)(2,1)S(1)}, bf16[128,8,16,128]{3,2,1,0:T(8,128)(2,1)S(1)}, u32[]{:S(2)}, u32[]{:S(2)}) collective-permute-start(bf16[128,8,16,128]{3,2,1,0:T(8,128)(2,1)S(1)} %get-tuple-element.12), channel_id=1, source_target_pairs={{0,1},{1,0},{2,3},{3,2},{4,5},{5,4},{6,7},{7,6},{8,9},{9,8},{10,11... | collective-permute-start | bytes 12582920 | tf_op jit(solution)/shard_map/ppermute | solution.py:20
  3.0 1.7 %shard_map.66 = bf16[1,32,128]{2,1,0:T(8,128)(2,1)S(1)} custom-call(bf16[32,4096]{1,0:T(8,128)(2,1)} %coefficients_hbm.1, bf16[4096,128]{1,0:T(8,128)(2,1)} %modes_hbm.1), custom_call_target="tpu_custom_call" | custom-call | tf_op jit(solution)/shard_map/pallas_call | solution.py:205
  4.7 0.1 collective-permute-start
  4.8 1.6 %shard_map.65 = (bf16[64,8,16,128]{3,2,1,0:T(8,128)(2,1)S(1)}, bf16[128,2048]{1,0:T(8,128)(2,1)S(1)}) custom-call(bf16[128,8,2,16,128]{4,3,2,1,0:T(8,128)(2,1)} %bitcast.49), custom_call_target="tpu_custom_call" | custom-call | tf_op jit(solution)/shard_map/pallas_call | solution.py:243
  6.4 1.6 %shard_map.68.refs_1_ = bf16[64,8,16,128]{3,2,1,0:T(8,128)(2,1)S(1)} custom-call(bf16[128,8,2,16,128]{4,3,2,1,0:T(8,128)(2,1)} %bitcast.50), custom_call_target="tpu_custom_call" | custom-call | tf_op jit(solution)/shard_map/pallas_call | solution.py:254
  8.0 1.8 %collective-permute-done = bf16[1,32,128]{2,1,0:T(8,128)(2,1)S(1)} collective-permute-done((bf16[1,32,128]{2,1,0:T(8,128)(2,1)S(1)}, bf16[1,32,128]{2,1,0:T(8,128)(2,1)S(1)}, u32[]{:S(2)}, u32[]{:S(2)}) %collective-permute-start) | collective-permute-done | bytes 8224 | tf_op jit(solution)/shard_map/ppermute | solution.py:20
  9.8 1.2 %collective-permute-start.1 = (bf16[2,32,128]{2,1,0:T(8,128)(2,1)S(1)}, bf16[2,32,128]{2,1,0:T(8,128)(2,1)S(1)}, u32[]{:S(2)}, u32[]{:S(2)}) collective-permute-start(bf16[2,32,128]{2,1,0:T(8,128)(2,1)S(1)} %pad_maximum_fusion.3), channel_id=1, source_target_pairs={{0,2},{1,3},{2,0},{3,1},{4,6},{5,7},{6,4},{7,5},{8,10},{9,11},{10,... | collective-permute-start | bytes 49160 | tf_op jit(solution)/shard_map/ppermute | solution.py:20
  11.0 1.3 %collective-permute-done.1 = bf16[2,32,128]{2,1,0:T(8,128)(2,1)S(1)} collective-permute-done((bf16[2,32,128]{2,1,0:T(8,128)(2,1)S(1)}, bf16[2,32,128]{2,1,0:T(8,128)(2,1)S(1)}, u32[]{:S(2)}, u32[]{:S(2)}) %collective-permute-start.1) | collective-permute-done | bytes 16416 | tf_op jit(solution)/shard_map/ppermute | solution.py:20
  12.4 0.2 collective-permute-start.2
  12.5 2.6 %collective-permute-done.2 = bf16[4,32,128]{2,1,0:T(8,128)(2,1)S(1)} collective-permute-done((bf16[4,32,128]{2,1,0:T(8,128)(2,1)S(1)}, bf16[4,32,128]{2,1,0:T(8,128)(2,1)S(1)}, u32[]{:S(2)}, u32[]{:S(2)}) %collective-permute-start.2) | collective-permute-done | bytes 32800 | tf_op jit(solution)/shard_map/ppermute | solution.py:20
  15.1 0.1 collective-permute-start.3
  15.3 4.5 %collective-permute-done.3 = bf16[8,32,128]{2,1,0:T(8,128)(2,1)S(1)} collective-permute-done((bf16[8,32,128]{2,1,0:T(8,128)(2,1)S(1)}, bf16[8,32,128]{2,1,0:T(8,128)(2,1)S(1)}, u32[]{:S(2)}, u32[]{:S(2)}) %collective-permute-start.3) | collective-permute-done | bytes 65568 | tf_op jit(solution)/shard_map/ppermute | solution.py:20
  19.8 1.3 %shard_map.67.spread_ref = bf16[512,4096]{1,0:T(8,128)(2,1)S(1)} custom-call(bf16[2048,256]{1,0:T(8,128)(2,1)S(1)} %get-tuple-element.9.chosen_ref, bf16[128,2048]{1,0:T(8,128)(2,1)S(1)} %get-tuple-element.10.repeat_ref, bf16[16,32,128]{2,1,0:T(8,128)(2,1)S(1)} %constant_dynamic-update-slice_fusion.slip_ref), custom_call_target="tpu_custom_call" | custom-call | tf_op jit(solution)/shard_map/pallas_call | solution.py:271
  21.1 0.0 collective-permute-done.4.refs_2_
  21.1 1.3 %shard_map.70 = bf16[4,8,32,128]{3,2,1,0:T(8,128)(2,1)S(1)} custom-call(bf16[512,4096]{1,0:T(8,128)(2,1)S(1)} %shard_map.67.spread_ref, bf16[64,8,16,128]{3,2,1,0:T(8,128)(2,1)S(1)} %get-tuple-element.11.refs_0_, bf16[64,8,16,128]{3,2,1,0:T(8,128)(2,1)S(1)} %shard_map.68.refs_1_, bf16[128,8,16,128]{3,2,1,0:T(8,128)(2,1)S(1)} %collective-permute-done.4.refs_2_), custom_call_target="tpu_custom_call" | custom-call | tf_op jit(solution)/shard_map/pallas_call | solution.py:132
  22.4 0.1 collective-permute-start.5
  22.5 1.3 %shard_map.72 = bf16[4,8,32,128]{3,2,1,0:T(8,128)(2,1)S(1)} custom-call(bf16[512,4096]{1,0:T(8,128)(2,1)S(1)} %shard_map.67.spread_ref, bf16[64,8,16,128]{3,2,1,0:T(8,128)(2,1)S(1)} %get-tuple-element.11.refs_0_, bf16[64,8,16,128]{3,2,1,0:T(8,128)(2,1)S(1)} %shard_map.68.refs_1_, bf16[128,8,16,128]{3,2,1,0:T(8,128)(2,1)S(1)} %collective-permute-done.4.refs_2_), custom_call_target="tpu_custom_call" | custom-call | tf_op jit(solution)/shard_map/pallas_call | solution.py:132
  23.8 1.5 %collective-permute-start.8 = (bf16[4,8,32,128]{3,2,1,0:T(8,128)(2,1)S(1)}, bf16[4,8,32,128]{3,2,1,0:T(8,128)(2,1)S(1)}, u32[]{:S(2)}, u32[]{:S(2)}) collective-permute-start(bf16[4,8,32,128]{3,2,1,0:T(8,128)(2,1)S(1)} %shard_map.72), channel_id=1, source_target_pairs={{0,2},{1,5},{2,0},{3,7},{4,6},{5,1},{6,4},{7,3},{8,10},{9,13},{10,... | collective-permute-start | bytes 786440 | tf_op jit(solution)/shard_map/ppermute | solution.py:20
  25.3 1.3 %shard_map.69 = f32[4,8,32,128]{3,2,1,0:T(8,128)S(1)} custom-call(bf16[512,4096]{1,0:T(8,128)(2,1)S(1)} %shard_map.67.spread_ref, bf16[64,8,16,128]{3,2,1,0:T(8,128)(2,1)S(1)} %get-tuple-element.11.refs_0_, bf16[64,8,16,128]{3,2,1,0:T(8,128)(2,1)S(1)} %shard_map.68.refs_1_, bf16[128,8,16,128]{3,2,1,0:T(8,128)(2,1)S(1)} %collective-permute-done.4.refs_2_), custom_call_target="tpu_custom_call" | custom-call | tf_op jit(solution)/shard_map/pallas_call | solution.py:132
  26.6 1.3 %shard_map.71 = f32[4,8,32,128]{3,2,1,0:T(8,128)S(1)} custom-call(bf16[512,4096]{1,0:T(8,128)(2,1)S(1)} %shard_map.67.spread_ref, bf16[64,8,16,128]{3,2,1,0:T(8,128)(2,1)S(1)} %get-tuple-element.11.refs_0_, bf16[64,8,16,128]{3,2,1,0:T(8,128)(2,1)S(1)} %shard_map.68.refs_1_, bf16[128,8,16,128]{3,2,1,0:T(8,128)(2,1)S(1)} %collective-permute-done.4.refs_2_), custom_call_target="tpu_custom_call" | custom-call | tf_op jit(solution)/shard_map/pallas_call | solution.py:132
  27.9 0.0 copy-start
  27.9 0.0 copy-start.1
  27.9 0.0 collective-permute-done.5
  28.0 0.1 convert_add_fusion.1
  28.1 1.3 %collective-permute-start.6 = (bf16[2,8,32,128]{3,2,1,0:T(8,128)(2,1)S(1)}, bf16[2,8,32,128]{3,2,1,0:T(8,128)(2,1)S(1)}, u32[]{:S(2)}, u32[]{:S(2)}) collective-permute-start(bf16[2,8,32,128]{3,2,1,0:T(8,128)(2,1)S(1)} %fusion.4), channel_id=1, source_target_pairs={{0,4},{1,3},{2,6},{3,1},{4,0},{5,7},{6,2},{7,5},{8,12},{9,11},{10,... | collective-permute-start | bytes 393224 | tf_op jit(solution)/shard_map/ppermute | solution.py:20
  29.4 1.4 %collective-permute-done.8 = bf16[4,8,32,128]{3,2,1,0:T(8,128)(2,1)S(1)} collective-permute-done((bf16[4,8,32,128]{3,2,1,0:T(8,128)(2,1)S(1)}, bf16[4,8,32,128]{3,2,1,0:T(8,128)(2,1)S(1)}, u32[]{:S(2)}, u32[]{:S(2)}) %collective-permute-start.8) | collective-permute-done | bytes 262176 | tf_op jit(solution)/shard_map/ppermute | solution.py:20
  30.8 0.1 convert_add_fusion
  30.9 1.3 %collective-permute-start.9 = (bf16[2,8,32,128]{3,2,1,0:T(8,128)(2,1)S(1)}, bf16[2,8,32,128]{3,2,1,0:T(8,128)(2,1)S(1)}, u32[]{:S(2)}, u32[]{:S(2)}) collective-permute-start(bf16[2,8,32,128]{3,2,1,0:T(8,128)(2,1)S(1)} %fusion.5), channel_id=1, source_target_pairs={{0,4},{1,3},{2,6},{3,1},{4,0},{5,7},{6,2},{7,5},{8,12},{9,11},{10,... | collective-permute-start | bytes 393224 | tf_op jit(solution)/shard_map/ppermute | solution.py:20
  32.2 1.4 %collective-permute-done.6 = bf16[2,8,32,128]{3,2,1,0:T(8,128)(2,1)S(1)} collective-permute-done((bf16[2,8,32,128]{3,2,1,0:T(8,128)(2,1)S(1)}, bf16[2,8,32,128]{3,2,1,0:T(8,128)(2,1)S(1)}, u32[]{:S(2)}, u32[]{:S(2)}) %collective-permute-start.6) | collective-permute-done | bytes 131104 | tf_op jit(solution)/shard_map/ppermute | solution.py:20
  33.7 0.1 collective-permute-start.7
  33.8 2.7 %collective-permute-done.9 = bf16[2,8,32,128]{3,2,1,0:T(8,128)(2,1)S(1)} collective-permute-done((bf16[2,8,32,128]{3,2,1,0:T(8,128)(2,1)S(1)}, bf16[2,8,32,128]{3,2,1,0:T(8,128)(2,1)S(1)}, u32[]{:S(2)}, u32[]{:S(2)}) %collective-permute-start.9) | collective-permute-done | bytes 131104 | tf_op jit(solution)/shard_map/ppermute | solution.py:20
  36.5 0.1 collective-permute-start.10
  36.6 1.8 %collective-permute-done.7 = bf16[1,8,32,128]{3,2,1,0:T(8,128)(2,1)S(1)} collective-permute-done((bf16[1,8,32,128]{3,2,1,0:T(8,128)(2,1)S(1)}, bf16[1,8,32,128]{3,2,1,0:T(8,128)(2,1)S(1)}, u32[]{:S(2)}, u32[]{:S(2)}) %collective-permute-start.7) | collective-permute-done | bytes 65568 | tf_op jit(solution)/shard_map/ppermute | solution.py:20
  38.5 2.6 %collective-permute-done.10 = bf16[1,8,32,128]{3,2,1,0:T(8,128)(2,1)S(1)} collective-permute-done((bf16[1,8,32,128]{3,2,1,0:T(8,128)(2,1)S(1)}, bf16[1,8,32,128]{3,2,1,0:T(8,128)(2,1)S(1)}, u32[]{:S(2)}, u32[]{:S(2)}) %collective-permute-start.10) | collective-permute-done | bytes 65568 | tf_op jit(solution)/shard_map/ppermute | solution.py:20
  41.1 7.9 %collective-permute-start.11 = (bf16[16,32,128]{2,1,0:T(8,128)(2,1)S(1)}, bf16[16,32,128]{2,1,0:T(8,128)(2,1)S(1)}, u32[]{:S(2)}, u32[]{:S(2)}) collective-permute-start(bf16[16,32,128]{2,1,0:T(8,128)(2,1)S(1)} %pad_maximum_fusion.own_ref), channel_id=1, source_target_pairs={{0,1},{1,0},{2,3},{3,2},{4,5},{5,4},{6,7},{7,6},{8,9},{9,8},{10,11... | collective-permute-start | bytes 393224 | tf_op jit(solution)/shard_map/ppermute | solution.py:20
  49.0 3.0 %collective-permute-start.12 = (bf16[16,32,128]{2,1,0:T(8,128)(2,1)S(1)}, bf16[16,32,128]{2,1,0:T(8,128)(2,1)S(1)}, u32[]{:S(2)}, u32[]{:S(2)}) collective-permute-start(bf16[16,32,128]{2,1,0:T(8,128)(2,1)S(1)} %pad_maximum_fusion.own_ref), channel_id=1, source_target_pairs={{1,2},{3,4},{5,6},{7,8},{9,10},{11,12},{13,14},{2,1},{4,3},{6,5},{... | collective-permute-start | bytes 393224 | tf_op jit(solution)/shard_map/ppermute | solution.py:298
  52.0 0.0 copy-done
  52.0 0.6 %shard_map.73.bands_ref = bf16[4352,256]{1,0:T(8,128)(2,1)S(1)} custom-call(f32[33,33]{1,0:T(8,128)S(1)} %copy-done), custom_call_target="tpu_custom_call" | custom-call | tf_op jit(solution)/shard_map/pallas_call | solution.py:263
  52.6 0.0 collective-permute-done.11.beside_ref
  52.7 4.0 %collective-permute-done.12.across_ref = bf16[16,32,128]{2,1,0:T(8,128)(2,1)S(1)} collective-permute-done((bf16[16,32,128]{2,1,0:T(8,128)(2,1)S(1)}, bf16[16,32,128]{2,1,0:T(8,128)(2,1)S(1)}, u32[]{:S(2)}, u32[]{:S(2)}) %collective-permute-start.12) | collective-permute-done | bytes 131104 | tf_op jit(solution)/shard_map/ppermute | solution.py:298
  56.7 0.0 copy-done.1
  56.7 1.7 %shard_map.74 = f32[32,16,128]{2,1,0:T(8,128)} custom-call(bf16[16,32,128]{2,1,0:T(8,128)(2,1)S(1)} %collective-permute-done.11.beside_ref, bf16[16,32,128]{2,1,0:T(8,128)(2,1)S(1)} %collective-permute-done.12.across_ref, bf16[16,32,128]{2,1,0:T(8,128)(2,1)S(1)} %pad_maximum_fusion.own_ref, bf16[4352,256]{1,0:T(8,128)(2,1)S(1)} %shard_map.73.bands_ref, ...), custom_call_target="tpu_custom_call" | custom-call | tf_op jit(solution)/shard_map/pallas_call | solution.py:300
  (17 shorter events, 0.2 us)
Async XLA Ops:
  2.2 18.9 %collective-permute-start.4 = (bf16[128,8,16,128]{3,2,1,0:T(8,128)(2,1)S(1)}, bf16[128,8,16,128]{3,2,1,0:T(8,128)(2,1)S(1)}, u32[]{:S(2)}, u32[]{:S(2)}) collective-permute-start(bf16[128,8,16,128]{3,2,1,0:T(8,128)(2,1)S(1)} %get-tuple-element.12), channel_id=1, source_target_pairs={{0,1},{1,0},{2,3},{3,2},{4,5},{5,4},{6,7},{7,6},{8,9},{9,8},{10,11... | collective-permute-start | bytes 12582920 | tf_op jit(solution)/shard_map/ppermute | solution.py:20
  4.7 5.1 %collective-permute-start = (bf16[1,32,128]{2,1,0:T(8,128)(2,1)S(1)}, bf16[1,32,128]{2,1,0:T(8,128)(2,1)S(1)}, u32[]{:S(2)}, u32[]{:S(2)}) collective-permute-start(bf16[1,32,128]{2,1,0:T(8,128)(2,1)S(1)} %shard_map.66), channel_id=1, source_target_pairs={{0,1},{1,0},{2,3},{3,2},{4,5},{5,4},{6,7},{7,6},{8,9},{9,8},{10,11... | collective-permute-start | bytes 24584 | tf_op jit(solution)/shard_map/ppermute | solution.py:20
  9.8 2.6 %collective-permute-start.1 = (bf16[2,32,128]{2,1,0:T(8,128)(2,1)S(1)}, bf16[2,32,128]{2,1,0:T(8,128)(2,1)S(1)}, u32[]{:S(2)}, u32[]{:S(2)}) collective-permute-start(bf16[2,32,128]{2,1,0:T(8,128)(2,1)S(1)} %pad_maximum_fusion.3), channel_id=1, source_target_pairs={{0,2},{1,3},{2,0},{3,1},{4,6},{5,7},{6,4},{7,5},{8,10},{9,11},{10,... | collective-permute-start | bytes 49160 | tf_op jit(solution)/shard_map/ppermute | solution.py:20
  12.4 2.8 %collective-permute-start.2 = (bf16[4,32,128]{2,1,0:T(8,128)(2,1)S(1)}, bf16[4,32,128]{2,1,0:T(8,128)(2,1)S(1)}, u32[]{:S(2)}, u32[]{:S(2)}) collective-permute-start(bf16[4,32,128]{2,1,0:T(8,128)(2,1)S(1)} %pad_maximum_fusion.2), channel_id=1, source_target_pairs={{0,4},{1,5},{2,6},{3,7},{4,0},{5,1},{6,2},{7,3},{8,12},{9,13},{10,... | collective-permute-start | bytes 98312 | tf_op jit(solution)/shard_map/ppermute | solution.py:20
  15.1 4.7 %collective-permute-start.3 = (bf16[8,32,128]{2,1,0:T(8,128)(2,1)S(1)}, bf16[8,32,128]{2,1,0:T(8,128)(2,1)S(1)}, u32[]{:S(2)}, u32[]{:S(2)}) collective-permute-start(bf16[8,32,128]{2,1,0:T(8,128)(2,1)S(1)} %pad_maximum_fusion.1), channel_id=1, source_target_pairs={{0,8},{1,9},{2,10},{3,11},{4,12},{5,13},{6,14},{7,15},{8,0},{9,1},... | collective-permute-start | bytes 196616 | tf_op jit(solution)/shard_map/ppermute | solution.py:20
  22.4 5.5 %collective-permute-start.5 = (bf16[4,8,32,128]{3,2,1,0:T(8,128)(2,1)S(1)}, bf16[4,8,32,128]{3,2,1,0:T(8,128)(2,1)S(1)}, u32[]{:S(2)}, u32[]{:S(2)}) collective-permute-start(bf16[4,8,32,128]{3,2,1,0:T(8,128)(2,1)S(1)} %shard_map.70), channel_id=1, source_target_pairs={{0,2},{1,5},{2,0},{3,7},{4,6},{5,1},{6,4},{7,3},{8,10},{9,13},{10,... | collective-permute-start | bytes 786440 | tf_op jit(solution)/shard_map/ppermute | solution.py:20
  23.8 7.0 %collective-permute-start.8 = (bf16[4,8,32,128]{3,2,1,0:T(8,128)(2,1)S(1)}, bf16[4,8,32,128]{3,2,1,0:T(8,128)(2,1)S(1)}, u32[]{:S(2)}, u32[]{:S(2)}) collective-permute-start(bf16[4,8,32,128]{3,2,1,0:T(8,128)(2,1)S(1)} %shard_map.72), channel_id=1, source_target_pairs={{0,2},{1,5},{2,0},{3,7},{4,6},{5,1},{6,4},{7,3},{8,10},{9,13},{10,... | collective-permute-start | bytes 786440 | tf_op jit(solution)/shard_map/ppermute | solution.py:20
  27.9 24.1 %copy-start = (f32[33,33]{1,0:T(8,128)S(1)}, f32[33,33]{1,0:T(8,128)}, u32[]{:S(2)}) copy-start(f32[33,33]{1,0:T(8,128)} %kernel_ref.1) | copy-start | bytes 13072
  27.9 28.7 %copy-start.1 = (s32[16,128]{1,0:T(8,128)S(1)}, s32[16,128]{1,0:T(8,128)}, u32[]{:S(2)}) copy-start(s32[16,128]{1,0:T(8,128)} %mask_ref.1) | copy-start | bytes 24580
  28.1 5.6 %collective-permute-start.6 = (bf16[2,8,32,128]{3,2,1,0:T(8,128)(2,1)S(1)}, bf16[2,8,32,128]{3,2,1,0:T(8,128)(2,1)S(1)}, u32[]{:S(2)}, u32[]{:S(2)}) collective-permute-start(bf16[2,8,32,128]{3,2,1,0:T(8,128)(2,1)S(1)} %fusion.4), channel_id=1, source_target_pairs={{0,4},{1,3},{2,6},{3,1},{4,0},{5,7},{6,2},{7,5},{8,12},{9,11},{10,... | collective-permute-start | bytes 393224 | tf_op jit(solution)/shard_map/ppermute | solution.py:20
  30.9 5.6 %collective-permute-start.9 = (bf16[2,8,32,128]{3,2,1,0:T(8,128)(2,1)S(1)}, bf16[2,8,32,128]{3,2,1,0:T(8,128)(2,1)S(1)}, u32[]{:S(2)}, u32[]{:S(2)}) collective-permute-start(bf16[2,8,32,128]{3,2,1,0:T(8,128)(2,1)S(1)} %fusion.5), channel_id=1, source_target_pairs={{0,4},{1,3},{2,6},{3,1},{4,0},{5,7},{6,2},{7,5},{8,12},{9,11},{10,... | collective-permute-start | bytes 393224 | tf_op jit(solution)/shard_map/ppermute | solution.py:20
  33.7 4.7 %collective-permute-start.7 = (bf16[1,8,32,128]{3,2,1,0:T(8,128)(2,1)S(1)}, bf16[1,8,32,128]{3,2,1,0:T(8,128)(2,1)S(1)}, u32[]{:S(2)}, u32[]{:S(2)}) collective-permute-start(bf16[1,8,32,128]{3,2,1,0:T(8,128)(2,1)S(1)} %fusion.11), channel_id=1, source_target_pairs={{0,8},{1,9},{2,10},{3,11},{4,12},{5,13},{6,14},{7,15},{8,0},{9,1},... | collective-permute-start | bytes 196616 | tf_op jit(solution)/shard_map/ppermute | solution.py:20
  36.5 4.5 %collective-permute-start.10 = (bf16[1,8,32,128]{3,2,1,0:T(8,128)(2,1)S(1)}, bf16[1,8,32,128]{3,2,1,0:T(8,128)(2,1)S(1)}, u32[]{:S(2)}, u32[]{:S(2)}) collective-permute-start(bf16[1,8,32,128]{3,2,1,0:T(8,128)(2,1)S(1)} %fusion.13), channel_id=1, source_target_pairs={{0,8},{1,9},{2,10},{3,11},{4,12},{5,13},{6,14},{7,15},{8,0},{9,1},... | collective-permute-start | bytes 196616 | tf_op jit(solution)/shard_map/ppermute | solution.py:20
  41.1 11.5 %collective-permute-start.11 = (bf16[16,32,128]{2,1,0:T(8,128)(2,1)S(1)}, bf16[16,32,128]{2,1,0:T(8,128)(2,1)S(1)}, u32[]{:S(2)}, u32[]{:S(2)}) collective-permute-start(bf16[16,32,128]{2,1,0:T(8,128)(2,1)S(1)} %pad_maximum_fusion.own_ref), channel_id=1, source_target_pairs={{0,1},{1,0},{2,3},{3,2},{4,5},{5,4},{6,7},{7,6},{8,9},{9,8},{10,11... | collective-permute-start | bytes 393224 | tf_op jit(solution)/shard_map/ppermute | solution.py:20
  49.0 7.7 %collective-permute-start.12 = (bf16[16,32,128]{2,1,0:T(8,128)(2,1)S(1)}, bf16[16,32,128]{2,1,0:T(8,128)(2,1)S(1)}, u32[]{:S(2)}, u32[]{:S(2)}) collective-permute-start(bf16[16,32,128]{2,1,0:T(8,128)(2,1)S(1)} %pad_maximum_fusion.own_ref), channel_id=1, source_target_pairs={{1,2},{3,4},{5,6},{7,8},{9,10},{11,12},{13,14},{2,1},{4,3},{6,5},{... | collective-permute-start | bytes 393224 | tf_op jit(solution)/shard_map/ppermute | solution.py:298

commit v5 on v4

--- a/solution.py
+++ b/solution.py
@@ -53,7 +53,7 @@
     return copy
 
 
-def choose_kernel(columns, index_hbm, green_ref, part_ref, chosen_ref, index_ref, semaphores):
+def choose_kernel(columns, levels, index_hbm, green_ref, part_ref, chosen_ref, index_ref, semaphores):
     me = lax.axis_index("space")
     fetch = pltpu.make_async_copy(index_hbm, index_ref, semaphores.at[0])
     fetch.start()
@@ -62,7 +62,9 @@
     fetch.wait()
     for side in range(2):
         row_ids = index_ref[pl.ds(me ^ side, 1), :]
-        position = ((row_ids // columns) ^ me) * columns + row_ids % columns
+        distance = (row_ids // columns) ^ me
+        slot = (distance >> 1) | ((distance & 1) << (levels - 1))
+        position = slot * columns + row_ids % columns
         for first in range(0, chosen_ref.shape[0], group):
             row = lax.broadcasted_iota(jnp.int32, (group, group), 0) + first
             chosen_ref[first : first + group, side * group : (side + 1) * group] = jnp.where(
@@ -71,22 +73,28 @@
     copy.wait()
 
 
-def repeat_kernel(start, rows, green_ref, part_ref, repeat_ref, semaphore):
-    copy = load(green_ref, part_ref, semaphore, start, lax.axis_index("space") & 1)
+def repeat_kernel(rows, green_ref, away_ref, own_ref, repeat_ref, semaphores):
+    odd = lax.axis_index("space") & 1
+    first = green_ref.shape[0] - away_ref.shape[0]
+    copies = (
+        load(green_ref, away_ref, semaphores.at[0], first, 1 - odd),
+        load(green_ref, own_ref, semaphores.at[1], 0, odd),
+    )
     source = lax.broadcasted_iota(jnp.int32, repeat_ref.shape, 0)
     target = lax.broadcasted_iota(jnp.int32, repeat_ref.shape, 1)
     near = (target >= source * rows) & (target < (source + 1) * rows)
     repeat_ref[...] = jnp.where(near, 1.0, 0.0).astype(jnp.bfloat16)
-    copy.wait()
-
-
-def rest_kernel(start, green_ref, part_ref, semaphore):
-    load(green_ref, part_ref, semaphore, start, lax.axis_index("space") & 1).wait()
-
-
-def select_kernel(chosen_ref, repeat_ref, slip_ref, spread_ref):
+    for copy in copies:
+        copy.wait()
+
+
+def rest_kernel(green_ref, own_ref, semaphore):
+    first = green_ref.shape[0] - own_ref.shape[0]
+    load(green_ref, own_ref, semaphore, first, lax.axis_index("space") & 1).wait()
+
+
+def select_kernel(rows, start, chosen_ref, repeat_ref, slip_ref, spread_ref):
     owners, realizations, _ = slip_ref.shape
-    rows = spread_ref.shape[0] // realizations
     group, depth = repeat_ref.shape
     slip = jnp.concatenate([slip_ref[owner] for owner in range(owners)], axis=1)
     picked = jnp.dot(slip, chosen_ref[...], preferred_element_type=jnp.float32)
@@ -98,10 +106,10 @@
             repeat_ref[...],
             preferred_element_type=jnp.float32,
         )
-        for row in range(rows):
+        for row in range(spread_ref.shape[0] // realizations):
             spread_ref[
                 row * realizations : (row + 1) * realizations, side * depth : (side + 1) * depth
-            ] = jnp.where(row_of == row, wide, 0.0).astype(jnp.bfloat16)
+            ] = jnp.where(row_of == start + row, wide, 0.0).astype(jnp.bfloat16)
 
 
 def turned(place):
@@ -114,24 +122,23 @@
     me = lax.axis_index("space")
 
     def block(place):
-        pair = (me >> 1) ^ jnp.where((me & 1) == 0, place, turned(place))
+        pair = (me >> 1) ^ jnp.where((me & 1) == stream % 2, place, turned(place))
         pieces = [ref[:, pair].reshape(ref.shape[0] * rows, width) for ref in parts]
         return jnp.concatenate(pieces, axis=0)
 
     columns = jnp.concatenate([block(place) for place in places], axis=1)
-    depth = out_ref.shape[1] * out_ref.shape[2]
-    lines = spread_ref[stream * depth : (stream + 1) * depth, :]
-    value = jnp.dot(lines, columns, preferred_element_type=jnp.float32)
+    value = jnp.dot(spread_ref[...], columns, preferred_element_type=jnp.float32)
     for slot in range(len(places)):
         part = value[:, slot * width : (slot + 1) * width].reshape(out_ref.shape[1:])
         out_ref[slot] = part.astype(out_ref.dtype)
 
 
 def uplift_blocks(places, stream, realizations, dtype, spread, parts):
-    rows, width = parts[0].shape[2:]
+    width = parts[0].shape[3]
+    lines = spread.shape[0] // realizations
     return pl.pallas_call(
         functools.partial(uplift_kernel, places, stream),
-        out_shape=jax.ShapeDtypeStruct((len(places), rows // STREAMS, realizations, width), dtype),
+        out_shape=jax.ShapeDtypeStruct((len(places), lines, realizations, width), dtype),
         in_specs=[VMEM] * (1 + len(parts)),
         out_specs=VMEM,
         compiler_params=PARAMS,
@@ -163,24 +170,26 @@
             bands_ref[(tap + 1) * width : (tap + 2) * width, width:] = band
 
 
-def smooth_kernel(beside_ref, across_ref, own_ref, bands_ref, mask_ref, out_ref, tall_ref, lines_ref):
+def smooth_kernel(
+    half, bands_ref, mask_ref, beside_ref, across_ref, own_ref, out_ref, tall_ref, lines_ref
+):
     rows, realizations, width = own_ref.shape
-    half = (tall_ref.shape[0] - rows) // 2
     odd = lax.axis_index("space") & 1
+
     for parity, before_ref, after_ref in ((0, across_ref, beside_ref), (1, beside_ref, across_ref)):
 
         @pl.when(odd == parity)
         def _():
-            tall_ref[:half] = before_ref[rows - half :]
-            tall_ref[half + rows :] = after_ref[:half]
-
-    tall_ref[half : half + rows] = own_ref[...]
+            tall_ref[:rows] = before_ref[...]
+            tall_ref[2 * rows :] = after_ref[...]
+
+    tall_ref[rows : 2 * rows] = own_ref[...]
     for shift in range(2 * half + 2):
         for pair in range(rows // 2):
             lines_ref[
                 pair * realizations : (pair + 1) * realizations,
                 shift * width : (shift + 1) * width,
-            ] = tall_ref[2 * pair + shift]
+            ] = tall_ref[rows - half + 2 * pair + shift]
     value = jnp.dot(lines_ref[...], bands_ref[...], preferred_element_type=jnp.float32)
     value = value.reshape(rows // 2, realizations, 2 * width)
     both = jnp.stack([value[:, :, :width], value[:, :, width:]], axis=1)
@@ -217,7 +226,7 @@
         pltpu.with_memory_space_constraint(coefficients, pltpu.HBM),
         pltpu.with_memory_space_constraint(kl_modes, pltpu.HBM),
     )
-    for level in range(levels):
+    for level in (*range(1, levels), 0):
         arrived = swap(slip, 1 << level)
         slip = jnp.concatenate([slip, arrived], axis=0)
 
@@ -225,10 +234,10 @@
         return jax.ShapeDtypeStruct((depth, count // 2, rows, width), green.dtype)
 
     index = pltpu.with_memory_space_constraint(sub_index.reshape(-1, group), pltpu.HBM)
-    away, chosen = pl.pallas_call(
-        functools.partial(choose_kernel, columns),
+    away_low, chosen = pl.pallas_call(
+        functools.partial(choose_kernel, columns, levels),
         out_shape=(
-            part(group),
+            part(group // 2),
             jax.ShapeDtypeStruct((sub_index.shape[0], 2 * group), jnp.bfloat16),
         ),
         in_specs=[HBM, HBM],
@@ -239,27 +248,29 @@
         ],
         compiler_params=PARAMS,
     )(index, green)
-    beside = swap(away, 1)
-    own_low, repeat = pl.pallas_call(
-        functools.partial(repeat_kernel, 0, rows),
+    beside_low = swap(away_low, 1)
+    away_high, own_low, repeat = pl.pallas_call(
+        functools.partial(repeat_kernel, rows),
         out_shape=(
-            part(group // 2),
+            part(group - group // 2),
+            part(group // 4),
             jax.ShapeDtypeStruct((group, group * rows), jnp.bfloat16),
         ),
         in_specs=[HBM],
-        out_specs=(VMEM, VMEM),
+        out_specs=(VMEM, VMEM, VMEM),
+        scratch_shapes=[pltpu.SemaphoreType.DMA((2,))],
+        compiler_params=PARAMS,
+    )(green)
+    beside_high = swap(away_high, 1)
+    own_high = pl.pallas_call(
+        rest_kernel,
+        out_shape=part(group - group // 4),
+        in_specs=[HBM],
+        out_specs=VMEM,
         scratch_shapes=[pltpu.SemaphoreType.DMA],
         compiler_params=PARAMS,
     )(green)
-    own_high = pl.pallas_call(
-        functools.partial(rest_kernel, group // 2),
-        out_shape=part(group - group // 2),
-        in_specs=[HBM],
-        out_specs=VMEM,
-        scratch_shapes=[pltpu.SemaphoreType.DMA],
-        compiler_params=PARAMS,
-    )(green)
-    parts = (own_low, own_high, beside)
+    parts = (own_low, own_high, beside_low, beside_high)
     bands = pl.pallas_call(
         bands_kernel,
         out_shape=jax.ShapeDtypeStruct(((taps + 1) * width, 2 * width), jnp.bfloat16),
@@ -268,46 +279,59 @@
         compiler_params=PARAMS,
     )(kernel)
 
-    spread = pl.pallas_call(
-        select_kernel,
-        out_shape=jax.ShapeDtypeStruct((rows * realizations, 2 * group * rows), jnp.bfloat16),
-        in_specs=[VMEM] * 3,
-        out_specs=VMEM,
-        compiler_params=PARAMS,
-    )(chosen, repeat, slip)
+    lines = rows // STREAMS
+
+    def spread(stream):
+        return pl.pallas_call(
+            functools.partial(select_kernel, rows, stream * lines),
+            out_shape=jax.ShapeDtypeStruct(
+                (lines * realizations, 2 * group * rows), jnp.bfloat16
+            ),
+            in_specs=[VMEM] * 3,
+            out_specs=VMEM,
+            compiler_params=PARAMS,
+        )(chosen, repeat, slip)
 
     places = list(range(count // 2))
     streams = range(STREAMS)
-    arrived, kept = [], []
+    turns = ((2, 4), (4, 2))
+    spreads, arrived, kept = [], [], []
     for stream in streams:
-        sent = uplift_blocks(places[1::2], stream, realizations, jnp.bfloat16, spread, parts)
-        arrived.append(swap(sent, 2, 4))
+        spreads.append(spread(stream))
+        sent = uplift_blocks(
+            places[1::2], stream, realizations, jnp.bfloat16, spreads[stream], parts
+        )
+        arrived.append(swap(sent, *turns[stream % 2]))
     for stream in streams:
-        block = uplift_blocks(places[::2], stream, realizations, jnp.float32, spread, parts)
+        block = uplift_blocks(
+            places[::2], stream, realizations, jnp.float32, spreads[stream], parts
+        )
         kept.append(block + arrived[stream].astype(jnp.float32))
     for level in range(2, levels):
         for stream in streams:
             pairs = kept[stream].reshape((-1, 2) + kept[stream].shape[1:])
             sent = pairs[:, 1].astype(jnp.bfloat16)
-            moved = swap(sent, 4, 2) if level == 2 else swap(sent, 1 << level)
+            bits = turns[1 - stream % 2] if level == 2 else (1 << level,)
+            moved = swap(sent, *bits)
             kept[stream] = pairs[:, 0] + moved.astype(jnp.float32)
-    seafloor = jnp.concatenate([block[0].astype(jnp.bfloat16) for block in kept], axis=0)
+    seafloor = [block[0].astype(jnp.bfloat16) for block in kept]
 
     crossing = [(i, i + 1) for i in range(1, count - 1, 2)]
     crossing += [(target, source) for source, target in crossing]
+    seafloor = jnp.concatenate(seafloor, axis=0)
     across = lax.ppermute(seafloor, "space", crossing)
     beside = swap(seafloor, 1)
     return pl.pallas_call(
-        smooth_kernel,
+        functools.partial(smooth_kernel, half),
         out_shape=jax.ShapeDtypeStruct((realizations, rows, width), jnp.float32),
         in_specs=[VMEM] * 5,
         out_specs=VMEM,
         scratch_shapes=[
-            pltpu.VMEM((rows + 2 * half, realizations, width), jnp.bfloat16),
+            pltpu.VMEM((3 * rows, realizations, width), jnp.bfloat16),
             pltpu.VMEM((rows // 2 * realizations, (taps + 1) * width), jnp.bfloat16),
         ],
         compiler_params=PARAMS,
-    )(beside, across, seafloor, bands, wet_mask)
+    )(bands, wet_mask, beside, across, seafloor)
 
 
 def solution(mesh):

time: 58.6 us -> 54.6 us (0.932)
  the two profiles are of different devices: /device:TPU:27 before, /device:TPU:1 now
where the time goes in v5:
time: 54.6 us; the launch traced here: 53.7 us
  starting transfers between devices  24.9 us (46%)
  Pallas kernels  16.3 us (30%)
  waiting for transfers between devices  11.9 us (22%)
    ppermute x13, starting transfers between devices, swap(): lax.ppermute(block, 'space', [(i, i ^ bits[i & 1]) for i in range(count)])  23 us
    ppermute x13, waiting for transfers between devices, swap(): lax.ppermute(block, 'space', [(i, i ^ bits[i & 1]) for i in range(count)])  8.2 us
    pallas_call x4, Pallas kernels, uplift_blocks(): pl.pallas_call(functools.partial(uplift_kernel, places, stream), out_shap...  5.19 us
    ppermute x1, waiting for transfers between devices, body(): across = lax.ppermute(seafloor, 'space', crossing)  3.66 us
    ppermute x1, starting transfers between devices, body(): across = lax.ppermute(seafloor, 'space', crossing)  1.98 us
    pallas_call x1, Pallas kernels, body(): pl.pallas_call(rest_kernel, out_shape=part(group - group // 4), in_specs=...  1.9 us
    pallas_call x1, Pallas kernels, body(): pl.pallas_call(functools.partial(repeat_kernel, rows), out_shape=(part(gr...  1.88 us
    pallas_call x2, Pallas kernels, spread(): pl.pallas_call(functools.partial(select_kernel, rows, stream * lines), ou...  1.7 us
  transfers between devices with their start and end apart: 14, of which 8 were waited for; matrix products, arithmetic and copies ran while one was open for 1% of the time, Pallas kernels for 21%

profile of v5, /device:TPU:1, one launch (start us, length us, event | category | flops | bytes accessed | tf_op | source)
XLA Modules:
  0.0 53.7 jit_solution(13750355736319909074)
XLA Ops:
  0.0 1.9 %shard_map.66 = (bf16[64,8,16,128]{3,2,1,0:T(8,128)(2,1)S(1)}, bf16[32,8,16,128]{3,2,1,0:T(8,128)(2,1)S(1)}, bf16[128,2048]{1,0:T(8,128)(2,1)S(1)}) custom-call(bf16[128,8,2,16,128]{4,3,2,1,0:T(8,128)(2,1)} %bitcast.48), custom_call_target="tpu_custom_call" | custom-call | tf_op jit(solution)/shard_map/pallas_call | solution.py:252
  1.9 0.1 collective-permute-start.5
  2.0 1.6 %shard_map.65 = (bf16[64,8,16,128]{3,2,1,0:T(8,128)(2,1)S(1)}, bf16[2048,256]{1,0:T(8,128)(2,1)S(1)}) custom-call(s32[16,128]{1,0:T(8,128)} %bitcast.55, bf16[128,8,2,16,128]{4,3,2,1,0:T(8,128)(2,1)} %bitcast.49), custom_call_target="tpu_custom_call" | custom-call | tf_op jit(solution)/shard_map/pallas_call | solution.py:237
  3.6 0.6 %collective-permute-start.4 = (bf16[64,8,16,128]{3,2,1,0:T(8,128)(2,1)S(1)}, bf16[64,8,16,128]{3,2,1,0:T(8,128)(2,1)S(1)}, u32[]{:S(2)}, u32[]{:S(2)}) collective-permute-start(bf16[64,8,16,128]{3,2,1,0:T(8,128)(2,1)S(1)} %get-tuple-element.13), channel_id=1, source_target_pairs={{0,1},{1,0},{2,3},{3,2},{4,5},{5,4},{6,7},{7,6},{8,9},{9,8},{10,11... | collective-permute-start | bytes 6291464 | tf_op jit(solution)/shard_map/ppermute | solution.py:20
  4.2 1.7 %shard_map.67 = bf16[1,32,128]{2,1,0:T(8,128)(2,1)S(1)} custom-call(bf16[32,4096]{1,0:T(8,128)(2,1)} %coefficients_hbm.1, bf16[4096,128]{1,0:T(8,128)(2,1)} %modes_hbm.1), custom_call_target="tpu_custom_call" | custom-call | tf_op jit(solution)/shard_map/pallas_call | solution.py:214
  5.9 2.3 %collective-permute-start = (bf16[1,32,128]{2,1,0:T(8,128)(2,1)S(1)}, bf16[1,32,128]{2,1,0:T(8,128)(2,1)S(1)}, u32[]{:S(2)}, u32[]{:S(2)}) collective-permute-start(bf16[1,32,128]{2,1,0:T(8,128)(2,1)S(1)} %shard_map.67), channel_id=1, source_target_pairs={{0,2},{1,3},{2,0},{3,1},{4,6},{5,7},{6,4},{7,5},{8,10},{9,11},{10,... | collective-permute-start | bytes 24584 | tf_op jit(solution)/shard_map/ppermute | solution.py:20
  8.2 1.9 %shard_map.69.refs_1_ = bf16[96,8,16,128]{3,2,1,0:T(8,128)(2,1)S(1)} custom-call(bf16[128,8,2,16,128]{4,3,2,1,0:T(8,128)(2,1)} %bitcast.50), custom_call_target="tpu_custom_call" | custom-call | tf_op jit(solution)/shard_map/pallas_call | solution.py:265
  10.1 0.0 collective-permute-done
  10.1 1.4 %collective-permute-start.1 = (bf16[2,32,128]{2,1,0:T(8,128)(2,1)S(1)}, bf16[2,32,128]{2,1,0:T(8,128)(2,1)S(1)}, u32[]{:S(2)}, u32[]{:S(2)}) collective-permute-start(bf16[2,32,128]{2,1,0:T(8,128)(2,1)S(1)} %pad_maximum_fusion.3), channel_id=1, source_target_pairs={{0,4},{1,5},{2,6},{3,7},{4,0},{5,1},{6,2},{7,3},{8,12},{9,13},{10,... | collective-permute-start | bytes 49160 | tf_op jit(solution)/shard_map/ppermute | solution.py:20
  11.5 1.3 %collective-permute-done.1 = bf16[2,32,128]{2,1,0:T(8,128)(2,1)S(1)} collective-permute-done((bf16[2,32,128]{2,1,0:T(8,128)(2,1)S(1)}, bf16[2,32,128]{2,1,0:T(8,128)(2,1)S(1)}, u32[]{:S(2)}, u32[]{:S(2)}) %collective-permute-start.1) | collective-permute-done | bytes 16416 | tf_op jit(solution)/shard_map/ppermute | solution.py:20
  12.8 2.3 %collective-permute-start.2 = (bf16[4,32,128]{2,1,0:T(8,128)(2,1)S(1)}, bf16[4,32,128]{2,1,0:T(8,128)(2,1)S(1)}, u32[]{:S(2)}, u32[]{:S(2)}) collective-permute-start(bf16[4,32,128]{2,1,0:T(8,128)(2,1)S(1)} %pad_maximum_fusion.2), channel_id=1, source_target_pairs={{0,8},{1,9},{2,10},{3,11},{4,12},{5,13},{6,14},{7,15},{8,0},{9,1},... | collective-permute-start | bytes 98312 | tf_op jit(solution)/shard_map/ppermute | solution.py:20
  15.1 1.3 %collective-permute-done.2 = bf16[4,32,128]{2,1,0:T(8,128)(2,1)S(1)} collective-permute-done((bf16[4,32,128]{2,1,0:T(8,128)(2,1)S(1)}, bf16[4,32,128]{2,1,0:T(8,128)(2,1)S(1)}, u32[]{:S(2)}, u32[]{:S(2)}) %collective-permute-start.2) | collective-permute-done | bytes 32800 | tf_op jit(solution)/shard_map/ppermute | solution.py:20
  16.4 3.1 %collective-permute-start.3 = (bf16[8,32,128]{2,1,0:T(8,128)(2,1)S(1)}, bf16[8,32,128]{2,1,0:T(8,128)(2,1)S(1)}, u32[]{:S(2)}, u32[]{:S(2)}) collective-permute-start(bf16[8,32,128]{2,1,0:T(8,128)(2,1)S(1)} %pad_maximum_fusion.1), channel_id=1, source_target_pairs={{0,1},{1,0},{2,3},{3,2},{4,5},{5,4},{6,7},{7,6},{8,9},{9,8},{10,11... | collective-permute-start | bytes 196616 | tf_op jit(solution)/shard_map/ppermute | solution.py:20
  19.6 0.9 %collective-permute-done.3 = bf16[8,32,128]{2,1,0:T(8,128)(2,1)S(1)} collective-permute-done((bf16[8,32,128]{2,1,0:T(8,128)(2,1)S(1)}, bf16[8,32,128]{2,1,0:T(8,128)(2,1)S(1)}, u32[]{:S(2)}, u32[]{:S(2)}) %collective-permute-start.3) | collective-permute-done | bytes 65568 | tf_op jit(solution)/shard_map/ppermute | solution.py:20
  20.5 0.8 %shard_map.68.spread_ref = bf16[256,4096]{1,0:T(8,128)(2,1)S(1)} custom-call(bf16[2048,256]{1,0:T(8,128)(2,1)S(1)} %get-tuple-element.10.chosen_ref, bf16[128,2048]{1,0:T(8,128)(2,1)S(1)} %get-tuple-element.11.repeat_ref, bf16[16,32,128]{2,1,0:T(8,128)(2,1)S(1)} %constant_dynamic-update-slice_fusion.slip_ref), custom_call_target="tpu_custom_call" | custom-call | tf_op jit(solution)/shard_map/pallas_call | solution.py:285
  21.4 0.0 collective-permute-done.5.refs_3_
  21.4 0.0 collective-permute-done.4.refs_2_
  21.4 1.3 %shard_map.71 = bf16[4,8,32,128]{3,2,1,0:T(8,128)(2,1)S(1)} custom-call(bf16[256,4096]{1,0:T(8,128)(2,1)S(1)} %shard_map.68.spread_ref, bf16[32,8,16,128]{3,2,1,0:T(8,128)(2,1)S(1)} %get-tuple-element.12.refs_0_, bf16[96,8,16,128]{3,2,1,0:T(8,128)(2,1)S(1)} %shard_map.69.refs_1_, bf16[64,8,16,128]{3,2,1,0:T(8,128)(2,1)S(1)} %collective-permute-done.4.refs_2_, ...), custom_call_target="tpu_custom_call" | custom-call | tf_op jit(solution)/shard_map/pallas_call | solution.py:139
  22.7 1.5 %collective-permute-start.6 = (bf16[4,8,32,128]{3,2,1,0:T(8,128)(2,1)S(1)}, bf16[4,8,32,128]{3,2,1,0:T(8,128)(2,1)S(1)}, u32[]{:S(2)}, u32[]{:S(2)}) collective-permute-start(bf16[4,8,32,128]{3,2,1,0:T(8,128)(2,1)S(1)} %shard_map.71), channel_id=1, source_target_pairs={{0,2},{1,5},{2,0},{3,7},{4,6},{5,1},{6,4},{7,3},{8,10},{9,13},{10,... | collective-permute-start | bytes 786440 | tf_op jit(solution)/shard_map/ppermute | solution.py:20
  24.2 0.8 %shard_map.72.spread_ref = bf16[256,4096]{1,0:T(8,128)(2,1)S(1)} custom-call(bf16[2048,256]{1,0:T(8,128)(2,1)S(1)} %get-tuple-element.10.chosen_ref, bf16[128,2048]{1,0:T(8,128)(2,1)S(1)} %get-tuple-element.11.repeat_ref, bf16[16,32,128]{2,1,0:T(8,128)(2,1)S(1)} %constant_dynamic-update-slice_fusion.slip_ref), custom_call_target="tpu_custom_call" | custom-call | tf_op jit(solution)/shard_map/pallas_call | solution.py:285
  25.0 1.3 %shard_map.74 = bf16[4,8,32,128]{3,2,1,0:T(8,128)(2,1)S(1)} custom-call(bf16[256,4096]{1,0:T(8,128)(2,1)S(1)} %shard_map.72.spread_ref, bf16[32,8,16,128]{3,2,1,0:T(8,128)(2,1)S(1)} %get-tuple-element.12.refs_0_, bf16[96,8,16,128]{3,2,1,0:T(8,128)(2,1)S(1)} %shard_map.69.refs_1_, bf16[64,8,16,128]{3,2,1,0:T(8,128)(2,1)S(1)} %collective-permute-done.4.refs_2_, ...), custom_call_target="tpu_custom_call" | custom-call | tf_op jit(solution)/shard_map/pallas_call | solution.py:139
  26.4 1.3 %collective-permute-start.9 = (bf16[4,8,32,128]{3,2,1,0:T(8,128)(2,1)S(1)}, bf16[4,8,32,128]{3,2,1,0:T(8,128)(2,1)S(1)}, u32[]{:S(2)}, u32[]{:S(2)}) collective-permute-start(bf16[4,8,32,128]{3,2,1,0:T(8,128)(2,1)S(1)} %shard_map.74), channel_id=1, source_target_pairs={{0,4},{1,3},{2,6},{3,1},{4,0},{5,7},{6,2},{7,5},{8,12},{9,11},{10,... | collective-permute-start | bytes 786440 | tf_op jit(solution)/shard_map/ppermute | solution.py:20
  27.6 1.3 %shard_map.70 = f32[4,8,32,128]{3,2,1,0:T(8,128)S(1)} custom-call(bf16[256,4096]{1,0:T(8,128)(2,1)S(1)} %shard_map.68.spread_ref, bf16[32,8,16,128]{3,2,1,0:T(8,128)(2,1)S(1)} %get-tuple-element.12.refs_0_, bf16[96,8,16,128]{3,2,1,0:T(8,128)(2,1)S(1)} %shard_map.69.refs_1_, bf16[64,8,16,128]{3,2,1,0:T(8,128)(2,1)S(1)} %collective-permute-done.4.refs_2_, ...), custom_call_target="tpu_custom_call" | custom-call | tf_op jit(solution)/shard_map/pallas_call | solution.py:139
  28.9 1.3 %shard_map.73 = f32[4,8,32,128]{3,2,1,0:T(8,128)S(1)} custom-call(bf16[256,4096]{1,0:T(8,128)(2,1)S(1)} %shard_map.72.spread_ref, bf16[32,8,16,128]{3,2,1,0:T(8,128)(2,1)S(1)} %get-tuple-element.12.refs_0_, bf16[96,8,16,128]{3,2,1,0:T(8,128)(2,1)S(1)} %shard_map.69.refs_1_, bf16[64,8,16,128]{3,2,1,0:T(8,128)(2,1)S(1)} %collective-permute-done.4.refs_2_, ...), custom_call_target="tpu_custom_call" | custom-call | tf_op jit(solution)/shard_map/pallas_call | solution.py:139
  30.2 0.0 collective-permute-done.6
  30.2 0.1 convert_add_fusion.1
  30.3 0.0 copy-start
  30.4 0.3 collective-permute-start.7
  30.7 1.3 %collective-permute-done.9 = bf16[4,8,32,128]{3,2,1,0:T(8,128)(2,1)S(1)} collective-permute-done((bf16[4,8,32,128]{3,2,1,0:T(8,128)(2,1)S(1)}, bf16[4,8,32,128]{3,2,1,0:T(8,128)(2,1)S(1)}, u32[]{:S(2)}, u32[]{:S(2)}) %collective-permute-start.9) | collective-permute-done | bytes 262176 | tf_op jit(solution)/shard_map/ppermute | solution.py:20
  31.9 0.1 convert_add_fusion
  32.0 1.5 %collective-permute-start.10 = (bf16[2,8,32,128]{3,2,1,0:T(8,128)(2,1)S(1)}, bf16[2,8,32,128]{3,2,1,0:T(8,128)(2,1)S(1)}, u32[]{:S(2)}, u32[]{:S(2)}) collective-permute-start(bf16[2,8,32,128]{3,2,1,0:T(8,128)(2,1)S(1)} %fusion.5), channel_id=1, source_target_pairs={{0,2},{1,5},{2,0},{3,7},{4,6},{5,1},{6,4},{7,3},{8,10},{9,13},{10,... | collective-permute-start | bytes 393224 | tf_op jit(solution)/shard_map/ppermute | solution.py:20
  33.5 1.0 %collective-permute-done.7 = bf16[2,8,32,128]{3,2,1,0:T(8,128)(2,1)S(1)} collective-permute-done((bf16[2,8,32,128]{3,2,1,0:T(8,128)(2,1)S(1)}, bf16[2,8,32,128]{3,2,1,0:T(8,128)(2,1)S(1)}, u32[]{:S(2)}, u32[]{:S(2)}) %collective-permute-start.7) | collective-permute-done | bytes 131104 | tf_op jit(solution)/shard_map/ppermute | solution.py:20
  34.6 0.0 copy-start.1
  34.6 2.6 %collective-permute-start.8 = (bf16[1,8,32,128]{3,2,1,0:T(8,128)(2,1)S(1)}, bf16[1,8,32,128]{3,2,1,0:T(8,128)(2,1)S(1)}, u32[]{:S(2)}, u32[]{:S(2)}) collective-permute-start(bf16[1,8,32,128]{3,2,1,0:T(8,128)(2,1)S(1)} %fusion.11), channel_id=1, source_target_pairs={{0,8},{1,9},{2,10},{3,11},{4,12},{5,13},{6,14},{7,15},{8,0},{9,1},... | collective-permute-start | bytes 196616 | tf_op jit(solution)/shard_map/ppermute | solution.py:20
  37.2 0.1 collective-permute-done.10
  37.4 2.6 %collective-permute-start.11 = (bf16[1,8,32,128]{3,2,1,0:T(8,128)(2,1)S(1)}, bf16[1,8,32,128]{3,2,1,0:T(8,128)(2,1)S(1)}, u32[]{:S(2)}, u32[]{:S(2)}) collective-permute-start(bf16[1,8,32,128]{3,2,1,0:T(8,128)(2,1)S(1)} %fusion.13), channel_id=1, source_target_pairs={{0,8},{1,9},{2,10},{3,11},{4,12},{5,13},{6,14},{7,15},{8,0},{9,1},... | collective-permute-start | bytes 196616 | tf_op jit(solution)/shard_map/ppermute | solution.py:20
  40.0 0.0 collective-permute-done.8
  40.0 2.3 %collective-permute-done.11 = bf16[1,8,32,128]{3,2,1,0:T(8,128)(2,1)S(1)} collective-permute-done((bf16[1,8,32,128]{3,2,1,0:T(8,128)(2,1)S(1)}, bf16[1,8,32,128]{3,2,1,0:T(8,128)(2,1)S(1)}, u32[]{:S(2)}, u32[]{:S(2)}) %collective-permute-start.11) | collective-permute-done | bytes 65568 | tf_op jit(solution)/shard_map/ppermute | solution.py:20
  42.3 3.4 %collective-permute-start.12 = (bf16[16,32,128]{2,1,0:T(8,128)(2,1)S(1)}, bf16[16,32,128]{2,1,0:T(8,128)(2,1)S(1)}, u32[]{:S(2)}, u32[]{:S(2)}) collective-permute-start(bf16[16,32,128]{2,1,0:T(8,128)(2,1)S(1)} %pad_maximum_fusion.own_ref), channel_id=1, source_target_pairs={{0,1},{1,0},{2,3},{3,2},{4,5},{5,4},{6,7},{7,6},{8,9},{9,8},{10,11... | collective-permute-start | bytes 393224 | tf_op jit(solution)/shard_map/ppermute | solution.py:20
  45.8 2.0 %collective-permute-start.13 = (bf16[16,32,128]{2,1,0:T(8,128)(2,1)S(1)}, bf16[16,32,128]{2,1,0:T(8,128)(2,1)S(1)}, u32[]{:S(2)}, u32[]{:S(2)}) collective-permute-start(bf16[16,32,128]{2,1,0:T(8,128)(2,1)S(1)} %pad_maximum_fusion.own_ref), channel_id=1, source_target_pairs={{1,2},{3,4},{5,6},{7,8},{9,10},{11,12},{13,14},{2,1},{4,3},{6,5},{... | collective-permute-start | bytes 393224 | tf_op jit(solution)/shard_map/ppermute | solution.py:322
  47.7 0.0 copy-done
  47.8 0.6 %shard_map.64.bands_ref = bf16[4352,256]{1,0:T(8,128)(2,1)S(1)} custom-call(f32[33,33]{1,0:T(8,128)S(1)} %copy-done), custom_call_target="tpu_custom_call" | custom-call | tf_op jit(solution)/shard_map/pallas_call | solution.py:274
  48.4 0.0 collective-permute-done.12.beside_ref
  48.4 3.7 %collective-permute-done.13.across_ref = bf16[16,32,128]{2,1,0:T(8,128)(2,1)S(1)} collective-permute-done((bf16[16,32,128]{2,1,0:T(8,128)(2,1)S(1)}, bf16[16,32,128]{2,1,0:T(8,128)(2,1)S(1)}, u32[]{:S(2)}, u32[]{:S(2)}) %collective-permute-start.13) | collective-permute-done | bytes 131104 | tf_op jit(solution)/shard_map/ppermute | solution.py:322
  52.0 0.0 copy-done.1
  52.0 1.7 %shard_map.75 = f32[32,16,128]{2,1,0:T(8,128)} custom-call(bf16[4352,256]{1,0:T(8,128)(2,1)S(1)} %shard_map.64.bands_ref, s32[16,128]{1,0:T(8,128)S(1)} %copy-done.1, bf16[16,32,128]{2,1,0:T(8,128)(2,1)S(1)} %collective-permute-done.12.beside_ref, bf16[16,32,128]{2,1,0:T(8,128)(2,1)S(1)} %collective-permute-done.13.across_ref, ...), custom_call_target="tpu_custom_call" | custom-call | tf_op jit(solution)/shard_map/pallas_call | solution.py:324
  (17 shorter events, 0.2 us)
Async XLA Ops:
  1.9 19.5 %collective-permute-start.5 = (bf16[64,8,16,128]{3,2,1,0:T(8,128)(2,1)S(1)}, bf16[64,8,16,128]{3,2,1,0:T(8,128)(2,1)S(1)}, u32[]{:S(2)}, u32[]{:S(2)}) collective-permute-start(bf16[64,8,16,128]{3,2,1,0:T(8,128)(2,1)S(1)} %get-tuple-element.14), channel_id=1, source_target_pairs={{0,1},{1,0},{2,3},{3,2},{4,5},{5,4},{6,7},{7,6},{8,9},{9,8},{10,11... | collective-permute-start | bytes 6291464 | tf_op jit(solution)/shard_map/ppermute | solution.py:20
  3.6 17.8 %collective-permute-start.4 = (bf16[64,8,16,128]{3,2,1,0:T(8,128)(2,1)S(1)}, bf16[64,8,16,128]{3,2,1,0:T(8,128)(2,1)S(1)}, u32[]{:S(2)}, u32[]{:S(2)}) collective-permute-start(bf16[64,8,16,128]{3,2,1,0:T(8,128)(2,1)S(1)} %get-tuple-element.13), channel_id=1, source_target_pairs={{0,1},{1,0},{2,3},{3,2},{4,5},{5,4},{6,7},{7,6},{8,9},{9,8},{10,11... | collective-permute-start | bytes 6291464 | tf_op jit(solution)/shard_map/ppermute | solution.py:20
  5.9 4.2 %collective-permute-start = (bf16[1,32,128]{2,1,0:T(8,128)(2,1)S(1)}, bf16[1,32,128]{2,1,0:T(8,128)(2,1)S(1)}, u32[]{:S(2)}, u32[]{:S(2)}) collective-permute-start(bf16[1,32,128]{2,1,0:T(8,128)(2,1)S(1)} %shard_map.67), channel_id=1, source_target_pairs={{0,2},{1,3},{2,0},{3,1},{4,6},{5,7},{6,4},{7,5},{8,10},{9,11},{10,... | collective-permute-start | bytes 24584 | tf_op jit(solution)/shard_map/ppermute | solution.py:20
  10.1 2.7 %collective-permute-start.1 = (bf16[2,32,128]{2,1,0:T(8,128)(2,1)S(1)}, bf16[2,32,128]{2,1,0:T(8,128)(2,1)S(1)}, u32[]{:S(2)}, u32[]{:S(2)}) collective-permute-start(bf16[2,32,128]{2,1,0:T(8,128)(2,1)S(1)} %pad_maximum_fusion.3), channel_id=1, source_target_pairs={{0,4},{1,5},{2,6},{3,7},{4,0},{5,1},{6,2},{7,3},{8,12},{9,13},{10,... | collective-permute-start | bytes 49160 | tf_op jit(solution)/shard_map/ppermute | solution.py:20
  12.8 3.7 %collective-permute-start.2 = (bf16[4,32,128]{2,1,0:T(8,128)(2,1)S(1)}, bf16[4,32,128]{2,1,0:T(8,128)(2,1)S(1)}, u32[]{:S(2)}, u32[]{:S(2)}) collective-permute-start(bf16[4,32,128]{2,1,0:T(8,128)(2,1)S(1)} %pad_maximum_fusion.2), channel_id=1, source_target_pairs={{0,8},{1,9},{2,10},{3,11},{4,12},{5,13},{6,14},{7,15},{8,0},{9,1},... | collective-permute-start | bytes 98312 | tf_op jit(solution)/shard_map/ppermute | solution.py:20
  16.4 4.0 %collective-permute-start.3 = (bf16[8,32,128]{2,1,0:T(8,128)(2,1)S(1)}, bf16[8,32,128]{2,1,0:T(8,128)(2,1)S(1)}, u32[]{:S(2)}, u32[]{:S(2)}) collective-permute-start(bf16[8,32,128]{2,1,0:T(8,128)(2,1)S(1)} %pad_maximum_fusion.1), channel_id=1, source_target_pairs={{0,1},{1,0},{2,3},{3,2},{4,5},{5,4},{6,7},{7,6},{8,9},{9,8},{10,11... | collective-permute-start | bytes 196616 | tf_op jit(solution)/shard_map/ppermute | solution.py:20
  22.7 7.5 %collective-permute-start.6 = (bf16[4,8,32,128]{3,2,1,0:T(8,128)(2,1)S(1)}, bf16[4,8,32,128]{3,2,1,0:T(8,128)(2,1)S(1)}, u32[]{:S(2)}, u32[]{:S(2)}) collective-permute-start(bf16[4,8,32,128]{3,2,1,0:T(8,128)(2,1)S(1)} %shard_map.71), channel_id=1, source_target_pairs={{0,2},{1,5},{2,0},{3,7},{4,6},{5,1},{6,4},{7,3},{8,10},{9,13},{10,... | collective-permute-start | bytes 786440 | tf_op jit(solution)/shard_map/ppermute | solution.py:20
  26.4 5.6 %collective-permute-start.9 = (bf16[4,8,32,128]{3,2,1,0:T(8,128)(2,1)S(1)}, bf16[4,8,32,128]{3,2,1,0:T(8,128)(2,1)S(1)}, u32[]{:S(2)}, u32[]{:S(2)}) collective-permute-start(bf16[4,8,32,128]{3,2,1,0:T(8,128)(2,1)S(1)} %shard_map.74), channel_id=1, source_target_pairs={{0,4},{1,3},{2,6},{3,1},{4,0},{5,7},{6,2},{7,5},{8,12},{9,11},{10,... | collective-permute-start | bytes 786440 | tf_op jit(solution)/shard_map/ppermute | solution.py:20
  30.3 17.4 %copy-start = (f32[33,33]{1,0:T(8,128)S(1)}, f32[33,33]{1,0:T(8,128)}, u32[]{:S(2)}) copy-start(f32[33,33]{1,0:T(8,128)} %kernel_ref.1) | copy-start | bytes 13072
  30.4 4.2 %collective-permute-start.7 = (bf16[2,8,32,128]{3,2,1,0:T(8,128)(2,1)S(1)}, bf16[2,8,32,128]{3,2,1,0:T(8,128)(2,1)S(1)}, u32[]{:S(2)}, u32[]{:S(2)}) collective-permute-start(bf16[2,8,32,128]{3,2,1,0:T(8,128)(2,1)S(1)} %fusion.4), channel_id=1, source_target_pairs={{0,4},{1,3},{2,6},{3,1},{4,0},{5,7},{6,2},{7,5},{8,12},{9,11},{10,... | collective-permute-start | bytes 393224 | tf_op jit(solution)/shard_map/ppermute | solution.py:20
  32.0 5.3 %collective-permute-start.10 = (bf16[2,8,32,128]{3,2,1,0:T(8,128)(2,1)S(1)}, bf16[2,8,32,128]{3,2,1,0:T(8,128)(2,1)S(1)}, u32[]{:S(2)}, u32[]{:S(2)}) collective-permute-start(bf16[2,8,32,128]{3,2,1,0:T(8,128)(2,1)S(1)} %fusion.5), channel_id=1, source_target_pairs={{0,2},{1,5},{2,0},{3,7},{4,6},{5,1},{6,4},{7,3},{8,10},{9,13},{10,... | collective-permute-start | bytes 393224 | tf_op jit(solution)/shard_map/ppermute | solution.py:20
  34.6 17.5 %copy-start.1 = (s32[16,128]{1,0:T(8,128)S(1)}, s32[16,128]{1,0:T(8,128)}, u32[]{:S(2)}) copy-start(s32[16,128]{1,0:T(8,128)} %mask_ref.1) | copy-start | bytes 24580
  34.6 5.4 %collective-permute-start.8 = (bf16[1,8,32,128]{3,2,1,0:T(8,128)(2,1)S(1)}, bf16[1,8,32,128]{3,2,1,0:T(8,128)(2,1)S(1)}, u32[]{:S(2)}, u32[]{:S(2)}) collective-permute-start(bf16[1,8,32,128]{3,2,1,0:T(8,128)(2,1)S(1)} %fusion.11), channel_id=1, source_target_pairs={{0,8},{1,9},{2,10},{3,11},{4,12},{5,13},{6,14},{7,15},{8,0},{9,1},... | collective-permute-start | bytes 196616 | tf_op jit(solution)/shard_map/ppermute | solution.py:20
  37.4 4.9 %collective-permute-start.11 = (bf16[1,8,32,128]{3,2,1,0:T(8,128)(2,1)S(1)}, bf16[1,8,32,128]{3,2,1,0:T(8,128)(2,1)S(1)}, u32[]{:S(2)}, u32[]{:S(2)}) collective-permute-start(bf16[1,8,32,128]{3,2,1,0:T(8,128)(2,1)S(1)} %fusion.13), channel_id=1, source_target_pairs={{0,8},{1,9},{2,10},{3,11},{4,12},{5,13},{6,14},{7,15},{8,0},{9,1},... | collective-permute-start | bytes 196616 | tf_op jit(solution)/shard_map/ppermute | solution.py:20
  42.3 6.0 %collective-permute-start.12 = (bf16[16,32,128]{2,1,0:T(8,128)(2,1)S(1)}, bf16[16,32,128]{2,1,0:T(8,128)(2,1)S(1)}, u32[]{:S(2)}, u32[]{:S(2)}) collective-permute-start(bf16[16,32,128]{2,1,0:T(8,128)(2,1)S(1)} %pad_maximum_fusion.own_ref), channel_id=1, source_target_pairs={{0,1},{1,0},{2,3},{3,2},{4,5},{5,4},{6,7},{7,6},{8,9},{9,8},{10,11... | collective-permute-start | bytes 393224 | tf_op jit(solution)/shard_map/ppermute | solution.py:20
  45.8 6.3 %collective-permute-start.13 = (bf16[16,32,128]{2,1,0:T(8,128)(2,1)S(1)}, bf16[16,32,128]{2,1,0:T(8,128)(2,1)S(1)}, u32[]{:S(2)}, u32[]{:S(2)}) collective-permute-start(bf16[16,32,128]{2,1,0:T(8,128)(2,1)S(1)} %pad_maximum_fusion.own_ref), channel_id=1, source_target_pairs={{1,2},{3,4},{5,6},{7,8},{9,10},{11,12},{13,14},{2,1},{4,3},{6,5},{... | collective-permute-start | bytes 393224 | tf_op jit(solution)/shard_map/ppermute | solution.py:322

commit v6 on v5

--- a/solution.py
+++ b/solution.py
@@ -11,6 +11,7 @@
 VMEM = pl.BlockSpec(memory_space=pltpu.VMEM)
 HBM = pl.BlockSpec(memory_space=pltpu.HBM)
 STREAMS = 2
+ORDERS = (((0, 1, 2), (1, 2, 0)), ((0, 1, 2), (1, 0, 2)))
 PARAMS = pltpu.CompilerParams(vmem_limit_bytes=20 << 20)
 
 
@@ -93,7 +94,7 @@
     load(green_ref, own_ref, semaphore, first, lax.axis_index("space") & 1).wait()
 
 
-def select_kernel(rows, start, chosen_ref, repeat_ref, slip_ref, spread_ref):
+def fill_spread(rows, start, chosen_ref, repeat_ref, slip_ref, spread_ref):
     owners, realizations, _ = slip_ref.shape
     group, depth = repeat_ref.shape
     slip = jnp.concatenate([slip_ref[owner] for owner in range(owners)], axis=1)
@@ -112,17 +113,31 @@
             ] = jnp.where(row_of == start + row, wide, 0.0).astype(jnp.bfloat16)
 
 
-def turned(place):
-    return (place & ~3) | ((place & 1) << 1) | ((place >> 1) & 1)
+def away_kernel(places, stream, rows, start, chosen_ref, repeat_ref, slip_ref, *refs):
+    fill_spread(rows, start, chosen_ref, repeat_ref, slip_ref, refs[-1])
+    uplift_kernel(places, stream, refs[-1], *refs[:-1])
+
+
+def stage_bits(stream, odd, count):
+    leading = ORDERS[stream][odd]
+    return leading + tuple(range(len(leading), count))
+
+
+def spread_bits(place, bits):
+    return sum(((place >> stage) & 1) << bit for stage, bit in enumerate(bits))
 
 
 def uplift_kernel(places, stream, spread_ref, *refs):
     parts, out_ref = refs[:-1], refs[-1]
     rows, width = parts[0].shape[2:]
     me = lax.axis_index("space")
+    levels = parts[0].shape[1].bit_length() - 1
+    even, odd = (stage_bits(stream, side, levels) for side in range(2))
 
     def block(place):
-        pair = (me >> 1) ^ jnp.where((me & 1) == stream % 2, place, turned(place))
+        pair = (me >> 1) ^ jnp.where(
+            (me & 1) == 0, spread_bits(place, even), spread_bits(place, odd)
+        )
         pieces = [ref[:, pair].reshape(ref.shape[0] * rows, width) for ref in parts]
         return jnp.concatenate(pieces, axis=0)
 
@@ -170,27 +185,35 @@
             bands_ref[(tap + 1) * width : (tap + 2) * width, width:] = band
 
 
-def smooth_kernel(
-    half, bands_ref, mask_ref, beside_ref, across_ref, own_ref, out_ref, tall_ref, lines_ref
-):
+def smooth_kernel(half, bands_ref, mask_ref, beside_ref, across_ref, own_ref, out_ref, pairs_ref):
     rows, realizations, width = own_ref.shape
     odd = lax.axis_index("space") & 1
 
+    def place(ref, first, start, count):
+        for row in range(count):
+            pair, side = divmod(start + row, 2)
+            pairs_ref[
+                pair * realizations : (pair + 1) * realizations,
+                side * width : (side + 1) * width,
+            ] = ref[first + row]
+
     for parity, before_ref, after_ref in ((0, across_ref, beside_ref), (1, beside_ref, across_ref)):
 
         @pl.when(odd == parity)
         def _():
-            tall_ref[:rows] = before_ref[...]
-            tall_ref[2 * rows :] = after_ref[...]
-
-    tall_ref[rows : 2 * rows] = own_ref[...]
-    for shift in range(2 * half + 2):
-        for pair in range(rows // 2):
-            lines_ref[
-                pair * realizations : (pair + 1) * realizations,
-                shift * width : (shift + 1) * width,
-            ] = tall_ref[rows - half + 2 * pair + shift]
-    value = jnp.dot(lines_ref[...], bands_ref[...], preferred_element_type=jnp.float32)
+            place(before_ref, rows - half, 0, half)
+            place(after_ref, 0, half + rows, half)
+
+    place(own_ref, 0, half, rows)
+    depth = rows // 2 * realizations
+    lines = jnp.concatenate(
+        [
+            pairs_ref[shift * realizations : shift * realizations + depth, :]
+            for shift in range(half + 1)
+        ],
+        axis=1,
+    )
+    value = jnp.dot(lines, bands_ref[...], preferred_element_type=jnp.float32)
     value = value.reshape(rows // 2, realizations, 2 * width)
     both = jnp.stack([value[:, :, :width], value[:, :, width:]], axis=1)
     both = both.reshape(rows, realizations, width)
@@ -219,7 +242,7 @@
         scratch_shapes=[
             pltpu.VMEM(coefficients.shape, coefficients.dtype),
             pltpu.VMEM(kl_modes.shape, kl_modes.dtype),
-            pltpu.SemaphoreType.DMA((5,)),
+            pltpu.SemaphoreType.DMA((3,)),
         ],
         compiler_params=PARAMS,
     )(
@@ -281,27 +304,31 @@
 
     lines = rows // STREAMS
 
-    def spread(stream):
+    def away_blocks(stream):
+        size = lines * realizations
         return pl.pallas_call(
-            functools.partial(select_kernel, rows, stream * lines),
-            out_shape=jax.ShapeDtypeStruct(
-                (lines * realizations, 2 * group * rows), jnp.bfloat16
+            functools.partial(away_kernel, places[1::2], stream, rows, stream * lines),
+            out_shape=(
+                jax.ShapeDtypeStruct((count // 4, lines, realizations, width), jnp.bfloat16),
+                jax.ShapeDtypeStruct((size, 2 * group * rows), jnp.bfloat16),
             ),
-            in_specs=[VMEM] * 3,
-            out_specs=VMEM,
+            in_specs=[VMEM] * (3 + len(parts)),
+            out_specs=(VMEM, VMEM),
             compiler_params=PARAMS,
-        )(chosen, repeat, slip)
+        )(chosen, repeat, slip, *parts)
 
     places = list(range(count // 2))
     streams = range(STREAMS)
-    turns = ((2, 4), (4, 2))
+
+    def stage_swap(block, stream, stage):
+        even, odd = (stage_bits(stream, side, levels - 1)[stage] for side in range(2))
+        return swap(block, 2 << even, 2 << odd)
+
     spreads, arrived, kept = [], [], []
     for stream in streams:
-        spreads.append(spread(stream))
-        sent = uplift_blocks(
-            places[1::2], stream, realizations, jnp.bfloat16, spreads[stream], parts
-        )
-        arrived.append(swap(sent, *turns[stream % 2]))
+        sent, spread = away_blocks(stream)
+        spreads.append(spread)
+        arrived.append(stage_swap(sent, stream, 0))
     for stream in streams:
         block = uplift_blocks(
             places[::2], stream, realizations, jnp.float32, spreads[stream], parts
@@ -311,8 +338,7 @@
         for stream in streams:
             pairs = kept[stream].reshape((-1, 2) + kept[stream].shape[1:])
             sent = pairs[:, 1].astype(jnp.bfloat16)
-            bits = turns[1 - stream % 2] if level == 2 else (1 << level,)
-            moved = swap(sent, *bits)
+            moved = stage_swap(sent, stream, level - 1)
             kept[stream] = pairs[:, 0] + moved.astype(jnp.float32)
     seafloor = [block[0].astype(jnp.bfloat16) for block in kept]
 
@@ -327,8 +353,7 @@
         in_specs=[VMEM] * 5,
         out_specs=VMEM,
         scratch_shapes=[
-            pltpu.VMEM((3 * rows, realizations, width), jnp.bfloat16),
-            pltpu.VMEM((rows // 2 * realizations, (taps + 1) * width), jnp.bfloat16),
+            pltpu.VMEM(((rows // 2 + half) * realizations, 2 * width), jnp.bfloat16),
         ],
         compiler_params=PARAMS,
     )(bands, wet_mask, beside, across, seafloor)

time: 54.6 us -> 53 us (0.971)
  the two profiles are of different devices: /device:TPU:1 before, /device:TPU:11 now
where the time goes in v6:
time: 53 us; the launch traced here: 52.8 us
  starting transfers between devices  23.6 us (45%)
  Pallas kernels  15.7 us (30%)
  waiting for transfers between devices  12.9 us (24%)
    ppermute x13, starting transfers between devices, swap(): lax.ppermute(block, 'space', [(i, i ^ bits[i & 1]) for i in range(count)])  20.5 us
    ppermute x13, waiting for transfers between devices, swap(): lax.ppermute(block, 'space', [(i, i ^ bits[i & 1]) for i in range(count)])  8.9 us
    pallas_call x2, Pallas kernels, away_blocks(): pl.pallas_call(functools.partial(away_kernel, places[1::2], stream, rows,...  4.01 us
    ppermute x1, waiting for transfers between devices, body(): across = lax.ppermute(seafloor, 'space', crossing)  3.97 us
    ppermute x1, starting transfers between devices, body(): across = lax.ppermute(seafloor, 'space', crossing)  3.07 us
    pallas_call x2, Pallas kernels, uplift_blocks(): pl.pallas_call(functools.partial(uplift_kernel, places, stream), out_shap...  2.58 us
    pallas_call x1, Pallas kernels, body(): pl.pallas_call(rest_kernel, out_shape=part(group - group // 4), in_specs=...  1.9 us
    pallas_call x1, Pallas kernels, body(): pl.pallas_call(functools.partial(repeat_kernel, rows), out_shape=(part(gr...  1.88 us
  transfers between devices with their start and end apart: 14, of which 6 were waited for; matrix products, arithmetic and copies ran while one was open for 1% of the time, Pallas kernels for 19%

profile of v6, /device:TPU:11, one launch (start us, length us, event | category | flops | bytes accessed | tf_op | source)
XLA Modules:
  0.0 52.8 jit_solution(9988648172212260650)
XLA Ops:
  0.0 1.9 %shard_map.66 = (bf16[64,8,16,128]{3,2,1,0:T(8,128)(2,1)S(1)}, bf16[32,8,16,128]{3,2,1,0:T(8,128)(2,1)S(1)}, bf16[128,2048]{1,0:T(8,128)(2,1)S(1)}) custom-call(bf16[128,8,2,16,128]{4,3,2,1,0:T(8,128)(2,1)} %bitcast.48), custom_call_target="tpu_custom_call" | custom-call | tf_op jit(solution)/shard_map/pallas_call | solution.py:275
  1.9 0.7 %collective-permute-start.5 = (bf16[64,8,16,128]{3,2,1,0:T(8,128)(2,1)S(1)}, bf16[64,8,16,128]{3,2,1,0:T(8,128)(2,1)S(1)}, u32[]{:S(2)}, u32[]{:S(2)}) collective-permute-start(bf16[64,8,16,128]{3,2,1,0:T(8,128)(2,1)S(1)} %get-tuple-element.18), channel_id=1, source_target_pairs={{0,1},{1,0},{2,3},{3,2},{4,5},{5,4},{6,7},{7,6},{8,9},{9,8},{10,11... | collective-permute-start | bytes 6291464 | tf_op jit(solution)/shard_map/ppermute | solution.py:21
  2.6 1.6 %shard_map.65 = (bf16[64,8,16,128]{3,2,1,0:T(8,128)(2,1)S(1)}, bf16[2048,256]{1,0:T(8,128)(2,1)S(1)}) custom-call(s32[16,128]{1,0:T(8,128)} %bitcast.55, bf16[128,8,2,16,128]{4,3,2,1,0:T(8,128)(2,1)} %bitcast.49), custom_call_target="tpu_custom_call" | custom-call | tf_op jit(solution)/shard_map/pallas_call | solution.py:260
  4.3 0.1 collective-permute-start.4
  4.3 1.6 %shard_map.67 = bf16[1,32,128]{2,1,0:T(8,128)(2,1)S(1)} custom-call(bf16[32,4096]{1,0:T(8,128)(2,1)} %coefficients_hbm.1, bf16[4096,128]{1,0:T(8,128)(2,1)} %modes_hbm.1), custom_call_target="tpu_custom_call" | custom-call | tf_op jit(solution)/shard_map/pallas_call | solution.py:237
  5.9 1.3 %collective-permute-start = (bf16[1,32,128]{2,1,0:T(8,128)(2,1)S(1)}, bf16[1,32,128]{2,1,0:T(8,128)(2,1)S(1)}, u32[]{:S(2)}, u32[]{:S(2)}) collective-permute-start(bf16[1,32,128]{2,1,0:T(8,128)(2,1)S(1)} %shard_map.67), channel_id=1, source_target_pairs={{0,2},{1,3},{2,0},{3,1},{4,6},{5,7},{6,4},{7,5},{8,10},{9,11},{10,... | collective-permute-start | bytes 24584 | tf_op jit(solution)/shard_map/ppermute | solution.py:21
  7.2 1.9 %shard_map.68.refs_1_ = bf16[96,8,16,128]{3,2,1,0:T(8,128)(2,1)S(1)} custom-call(bf16[128,8,2,16,128]{4,3,2,1,0:T(8,128)(2,1)} %bitcast.50), custom_call_target="tpu_custom_call" | custom-call | tf_op jit(solution)/shard_map/pallas_call | solution.py:288
  9.1 0.0 collective-permute-done
  9.2 0.2 collective-permute-start.1
  9.4 2.4 %collective-permute-done.1 = bf16[2,32,128]{2,1,0:T(8,128)(2,1)S(1)} collective-permute-done((bf16[2,32,128]{2,1,0:T(8,128)(2,1)S(1)}, bf16[2,32,128]{2,1,0:T(8,128)(2,1)S(1)}, u32[]{:S(2)}, u32[]{:S(2)}) %collective-permute-start.1) | collective-permute-done | bytes 16416 | tf_op jit(solution)/shard_map/ppermute | solution.py:21
  11.8 2.3 %collective-permute-start.2 = (bf16[4,32,128]{2,1,0:T(8,128)(2,1)S(1)}, bf16[4,32,128]{2,1,0:T(8,128)(2,1)S(1)}, u32[]{:S(2)}, u32[]{:S(2)}) collective-permute-start(bf16[4,32,128]{2,1,0:T(8,128)(2,1)S(1)} %pad_maximum_fusion.2), channel_id=1, source_target_pairs={{0,8},{1,9},{2,10},{3,11},{4,12},{5,13},{6,14},{7,15},{8,0},{9,1},... | collective-permute-start | bytes 98312 | tf_op jit(solution)/shard_map/ppermute | solution.py:21
  14.2 1.3 %collective-permute-done.2 = bf16[4,32,128]{2,1,0:T(8,128)(2,1)S(1)} collective-permute-done((bf16[4,32,128]{2,1,0:T(8,128)(2,1)S(1)}, bf16[4,32,128]{2,1,0:T(8,128)(2,1)S(1)}, u32[]{:S(2)}, u32[]{:S(2)}) %collective-permute-start.2) | collective-permute-done | bytes 32800 | tf_op jit(solution)/shard_map/ppermute | solution.py:21
  15.5 3.3 %collective-permute-start.3 = (bf16[8,32,128]{2,1,0:T(8,128)(2,1)S(1)}, bf16[8,32,128]{2,1,0:T(8,128)(2,1)S(1)}, u32[]{:S(2)}, u32[]{:S(2)}) collective-permute-start(bf16[8,32,128]{2,1,0:T(8,128)(2,1)S(1)} %pad_maximum_fusion.1), channel_id=1, source_target_pairs={{0,1},{1,0},{2,3},{3,2},{4,5},{5,4},{6,7},{7,6},{8,9},{9,8},{10,11... | collective-permute-start | bytes 196616 | tf_op jit(solution)/shard_map/ppermute | solution.py:21
  18.8 0.9 %collective-permute-done.3 = bf16[8,32,128]{2,1,0:T(8,128)(2,1)S(1)} collective-permute-done((bf16[8,32,128]{2,1,0:T(8,128)(2,1)S(1)}, bf16[8,32,128]{2,1,0:T(8,128)(2,1)S(1)}, u32[]{:S(2)}, u32[]{:S(2)}) %collective-permute-start.3) | collective-permute-done | bytes 65568 | tf_op jit(solution)/shard_map/ppermute | solution.py:21
  19.7 0.0 collective-permute-done.5.refs_3_
  19.7 0.0 collective-permute-done.4.refs_2_
  19.7 2.0 %shard_map.69 = (bf16[4,8,32,128]{3,2,1,0:T(8,128)(2,1)S(1)}, bf16[256,4096]{1,0:T(8,128)(2,1)S(1)}) custom-call(bf16[2048,256]{1,0:T(8,128)(2,1)S(1)} %get-tuple-element.14.chosen_ref, bf16[128,2048]{1,0:T(8,128)(2,1)S(1)} %get-tuple-element.15.repeat_ref, bf16[16,32,128]{2,1,0:T(8,128)(2,1)S(1)} %constant_dynamic-update-slice_fusion.slip_ref, ...), custom_call_target="tpu_custom_call" | custom-call | tf_op jit(solution)/shard_map/pallas_call | solution.py:309
  21.7 0.3 collective-permute-start.6
  22.0 2.0 %shard_map.71 = (bf16[4,8,32,128]{3,2,1,0:T(8,128)(2,1)S(1)}, bf16[256,4096]{1,0:T(8,128)(2,1)S(1)}) custom-call(bf16[2048,256]{1,0:T(8,128)(2,1)S(1)} %get-tuple-element.14.chosen_ref, bf16[128,2048]{1,0:T(8,128)(2,1)S(1)} %get-tuple-element.15.repeat_ref, bf16[16,32,128]{2,1,0:T(8,128)(2,1)S(1)} %constant_dynamic-update-slice_fusion.slip_ref, ...), custom_call_target="tpu_custom_call" | custom-call | tf_op jit(solution)/shard_map/pallas_call | solution.py:309
  24.0 1.4 %collective-permute-start.9 = (bf16[4,8,32,128]{3,2,1,0:T(8,128)(2,1)S(1)}, bf16[4,8,32,128]{3,2,1,0:T(8,128)(2,1)S(1)}, u32[]{:S(2)}, u32[]{:S(2)}) collective-permute-start(bf16[4,8,32,128]{3,2,1,0:T(8,128)(2,1)S(1)} %get-tuple-element.22), channel_id=1, source_target_pairs={{0,2},{1,5},{2,0},{3,7},{4,6},{5,1},{6,4},{7,3},{8,10},{9,13},{10,... | collective-permute-start | bytes 786440 | tf_op jit(solution)/shard_map/ppermute | solution.py:21
  25.4 1.3 %shard_map.70 = f32[4,8,32,128]{3,2,1,0:T(8,128)S(1)} custom-call(bf16[256,4096]{1,0:T(8,128)(2,1)S(1)} %get-tuple-element.19.spread_ref, bf16[32,8,16,128]{3,2,1,0:T(8,128)(2,1)S(1)} %get-tuple-element.16.refs_0_, bf16[96,8,16,128]{3,2,1,0:T(8,128)(2,1)S(1)} %shard_map.68.refs_1_, bf16[64,8,16,128]{3,2,1,0:T(8,128)(2,1)S(1)} %collective-permute-done.4.refs_2_, ...), custom_call_target="tpu_custom_call" | custom-call | tf_op jit(solution)/shard_map/pallas_call | solution.py:154
  26.7 1.3 %shard_map.72 = f32[4,8,32,128]{3,2,1,0:T(8,128)S(1)} custom-call(bf16[256,4096]{1,0:T(8,128)(2,1)S(1)} %get-tuple-element.21.spread_ref, bf16[32,8,16,128]{3,2,1,0:T(8,128)(2,1)S(1)} %get-tuple-element.16.refs_0_, bf16[96,8,16,128]{3,2,1,0:T(8,128)(2,1)S(1)} %shard_map.68.refs_1_, bf16[64,8,16,128]{3,2,1,0:T(8,128)(2,1)S(1)} %collective-permute-done.4.refs_2_, ...), custom_call_target="tpu_custom_call" | custom-call | tf_op jit(solution)/shard_map/pallas_call | solution.py:154
  28.0 0.0 collective-permute-done.6
  28.0 0.1 convert_add_fusion.1
  28.1 0.0 copy-start
  28.1 2.6 %collective-permute-start.7 = (bf16[2,8,32,128]{3,2,1,0:T(8,128)(2,1)S(1)}, bf16[2,8,32,128]{3,2,1,0:T(8,128)(2,1)S(1)}, u32[]{:S(2)}, u32[]{:S(2)}) collective-permute-start(bf16[2,8,32,128]{3,2,1,0:T(8,128)(2,1)S(1)} %fusion.4), channel_id=1, source_target_pairs={{0,4},{1,9},{2,6},{3,11},{4,0},{5,13},{6,2},{7,15},{8,12},{9,1},{1... | collective-permute-start | bytes 393224 | tf_op jit(solution)/shard_map/ppermute | solution.py:21
  30.7 0.0 collective-permute-done.9
  30.7 0.1 convert_add_fusion
  30.8 1.3 %collective-permute-start.10 = (bf16[2,8,32,128]{3,2,1,0:T(8,128)(2,1)S(1)}, bf16[2,8,32,128]{3,2,1,0:T(8,128)(2,1)S(1)}, u32[]{:S(2)}, u32[]{:S(2)}) collective-permute-start(bf16[2,8,32,128]{3,2,1,0:T(8,128)(2,1)S(1)} %fusion.5), channel_id=1, source_target_pairs={{0,4},{1,3},{2,6},{3,1},{4,0},{5,7},{6,2},{7,5},{8,12},{9,11},{10,... | collective-permute-start | bytes 393224 | tf_op jit(solution)/shard_map/ppermute | solution.py:21
  32.1 1.6 %collective-permute-done.7 = bf16[2,8,32,128]{3,2,1,0:T(8,128)(2,1)S(1)} collective-permute-done((bf16[2,8,32,128]{3,2,1,0:T(8,128)(2,1)S(1)}, bf16[2,8,32,128]{3,2,1,0:T(8,128)(2,1)S(1)}, u32[]{:S(2)}, u32[]{:S(2)}) %collective-permute-start.7) | collective-permute-done | bytes 131104 | tf_op jit(solution)/shard_map/ppermute | solution.py:21
  33.8 0.0 copy-start.1
  33.8 1.3 %collective-permute-start.8 = (bf16[1,8,32,128]{3,2,1,0:T(8,128)(2,1)S(1)}, bf16[1,8,32,128]{3,2,1,0:T(8,128)(2,1)S(1)}, u32[]{:S(2)}, u32[]{:S(2)}) collective-permute-start(bf16[1,8,32,128]{3,2,1,0:T(8,128)(2,1)S(1)} %fusion.11), channel_id=1, source_target_pairs={{0,8},{1,3},{2,10},{3,1},{4,12},{5,7},{6,14},{7,5},{8,0},{9,11},{1... | collective-permute-start | bytes 196616 | tf_op jit(solution)/shard_map/ppermute | solution.py:21
  35.1 0.0 collective-permute-done.10
  35.2 3.0 %collective-permute-start.11 = (bf16[1,8,32,128]{3,2,1,0:T(8,128)(2,1)S(1)}, bf16[1,8,32,128]{3,2,1,0:T(8,128)(2,1)S(1)}, u32[]{:S(2)}, u32[]{:S(2)}) collective-permute-start(bf16[1,8,32,128]{3,2,1,0:T(8,128)(2,1)S(1)} %fusion.13), channel_id=1, source_target_pairs={{0,8},{1,9},{2,10},{3,11},{4,12},{5,13},{6,14},{7,15},{8,0},{9,1},... | collective-permute-start | bytes 196616 | tf_op jit(solution)/shard_map/ppermute | solution.py:21
  38.1 0.0 collective-permute-done.8
  38.2 2.6 %collective-permute-done.11 = bf16[1,8,32,128]{3,2,1,0:T(8,128)(2,1)S(1)} collective-permute-done((bf16[1,8,32,128]{3,2,1,0:T(8,128)(2,1)S(1)}, bf16[1,8,32,128]{3,2,1,0:T(8,128)(2,1)S(1)}, u32[]{:S(2)}, u32[]{:S(2)}) %collective-permute-start.11) | collective-permute-done | bytes 65568 | tf_op jit(solution)/shard_map/ppermute | solution.py:21
  40.8 2.7 %collective-permute-start.12 = (bf16[16,32,128]{2,1,0:T(8,128)(2,1)S(1)}, bf16[16,32,128]{2,1,0:T(8,128)(2,1)S(1)}, u32[]{:S(2)}, u32[]{:S(2)}) collective-permute-start(bf16[16,32,128]{2,1,0:T(8,128)(2,1)S(1)} %pad_maximum_fusion.own_ref), channel_id=1, source_target_pairs={{0,1},{1,0},{2,3},{3,2},{4,5},{5,4},{6,7},{7,6},{8,9},{9,8},{10,11... | collective-permute-start | bytes 393224 | tf_op jit(solution)/shard_map/ppermute | solution.py:21
  43.6 3.1 %collective-permute-start.13 = (bf16[16,32,128]{2,1,0:T(8,128)(2,1)S(1)}, bf16[16,32,128]{2,1,0:T(8,128)(2,1)S(1)}, u32[]{:S(2)}, u32[]{:S(2)}) collective-permute-start(bf16[16,32,128]{2,1,0:T(8,128)(2,1)S(1)} %pad_maximum_fusion.own_ref), channel_id=1, source_target_pairs={{1,2},{3,4},{5,6},{7,8},{9,10},{11,12},{13,14},{2,1},{4,3},{6,5},{... | collective-permute-start | bytes 393224 | tf_op jit(solution)/shard_map/ppermute | solution.py:348
  46.6 0.0 copy-done
  46.6 0.6 %shard_map.64.bands_ref = bf16[4352,256]{1,0:T(8,128)(2,1)S(1)} custom-call(f32[33,33]{1,0:T(8,128)S(1)} %copy-done), custom_call_target="tpu_custom_call" | custom-call | tf_op jit(solution)/shard_map/pallas_call | solution.py:297
  47.3 0.0 collective-permute-done.12.beside_ref
  47.3 4.0 %collective-permute-done.13.across_ref = bf16[16,32,128]{2,1,0:T(8,128)(2,1)S(1)} collective-permute-done((bf16[16,32,128]{2,1,0:T(8,128)(2,1)S(1)}, bf16[16,32,128]{2,1,0:T(8,128)(2,1)S(1)}, u32[]{:S(2)}, u32[]{:S(2)}) %collective-permute-start.13) | collective-permute-done | bytes 131104 | tf_op jit(solution)/shard_map/ppermute | solution.py:348
  51.2 0.0 copy-done.1
  51.2 1.5 %shard_map.73 = f32[32,16,128]{2,1,0:T(8,128)} custom-call(bf16[4352,256]{1,0:T(8,128)(2,1)S(1)} %shard_map.64.bands_ref, s32[16,128]{1,0:T(8,128)S(1)} %copy-done.1, bf16[16,32,128]{2,1,0:T(8,128)(2,1)S(1)} %collective-permute-done.12.beside_ref, bf16[16,32,128]{2,1,0:T(8,128)(2,1)S(1)} %collective-permute-done.13.across_ref, ...), custom_call_target="tpu_custom_call" | custom-call | tf_op jit(solution)/shard_map/pallas_call | solution.py:350
  (17 shorter events, 0.2 us)
Async XLA Ops:
  1.9 17.8 %collective-permute-start.5 = (bf16[64,8,16,128]{3,2,1,0:T(8,128)(2,1)S(1)}, bf16[64,8,16,128]{3,2,1,0:T(8,128)(2,1)S(1)}, u32[]{:S(2)}, u32[]{:S(2)}) collective-permute-start(bf16[64,8,16,128]{3,2,1,0:T(8,128)(2,1)S(1)} %get-tuple-element.18), channel_id=1, source_target_pairs={{0,1},{1,0},{2,3},{3,2},{4,5},{5,4},{6,7},{7,6},{8,9},{9,8},{10,11... | collective-permute-start | bytes 6291464 | tf_op jit(solution)/shard_map/ppermute | solution.py:21
  4.3 15.5 %collective-permute-start.4 = (bf16[64,8,16,128]{3,2,1,0:T(8,128)(2,1)S(1)}, bf16[64,8,16,128]{3,2,1,0:T(8,128)(2,1)S(1)}, u32[]{:S(2)}, u32[]{:S(2)}) collective-permute-start(bf16[64,8,16,128]{3,2,1,0:T(8,128)(2,1)S(1)} %get-tuple-element.17), channel_id=1, source_target_pairs={{0,1},{1,0},{2,3},{3,2},{4,5},{5,4},{6,7},{7,6},{8,9},{9,8},{10,11... | collective-permute-start | bytes 6291464 | tf_op jit(solution)/shard_map/ppermute | solution.py:21
  5.9 3.2 %collective-permute-start = (bf16[1,32,128]{2,1,0:T(8,128)(2,1)S(1)}, bf16[1,32,128]{2,1,0:T(8,128)(2,1)S(1)}, u32[]{:S(2)}, u32[]{:S(2)}) collective-permute-start(bf16[1,32,128]{2,1,0:T(8,128)(2,1)S(1)} %shard_map.67), channel_id=1, source_target_pairs={{0,2},{1,3},{2,0},{3,1},{4,6},{5,7},{6,4},{7,5},{8,10},{9,11},{10,... | collective-permute-start | bytes 24584 | tf_op jit(solution)/shard_map/ppermute | solution.py:21
  9.2 2.7 %collective-permute-start.1 = (bf16[2,32,128]{2,1,0:T(8,128)(2,1)S(1)}, bf16[2,32,128]{2,1,0:T(8,128)(2,1)S(1)}, u32[]{:S(2)}, u32[]{:S(2)}) collective-permute-start(bf16[2,32,128]{2,1,0:T(8,128)(2,1)S(1)} %pad_maximum_fusion.3), channel_id=1, source_target_pairs={{0,4},{1,5},{2,6},{3,7},{4,0},{5,1},{6,2},{7,3},{8,12},{9,13},{10,... | collective-permute-start | bytes 49160 | tf_op jit(solution)/shard_map/ppermute | solution.py:21
  11.8 3.7 %collective-permute-start.2 = (bf16[4,32,128]{2,1,0:T(8,128)(2,1)S(1)}, bf16[4,32,128]{2,1,0:T(8,128)(2,1)S(1)}, u32[]{:S(2)}, u32[]{:S(2)}) collective-permute-start(bf16[4,32,128]{2,1,0:T(8,128)(2,1)S(1)} %pad_maximum_fusion.2), channel_id=1, source_target_pairs={{0,8},{1,9},{2,10},{3,11},{4,12},{5,13},{6,14},{7,15},{8,0},{9,1},... | collective-permute-start | bytes 98312 | tf_op jit(solution)/shard_map/ppermute | solution.py:21
  15.5 4.2 %collective-permute-start.3 = (bf16[8,32,128]{2,1,0:T(8,128)(2,1)S(1)}, bf16[8,32,128]{2,1,0:T(8,128)(2,1)S(1)}, u32[]{:S(2)}, u32[]{:S(2)}) collective-permute-start(bf16[8,32,128]{2,1,0:T(8,128)(2,1)S(1)} %pad_maximum_fusion.1), channel_id=1, source_target_pairs={{0,1},{1,0},{2,3},{3,2},{4,5},{5,4},{6,7},{7,6},{8,9},{9,8},{10,11... | collective-permute-start | bytes 196616 | tf_op jit(solution)/shard_map/ppermute | solution.py:21
  21.7 6.2 %collective-permute-start.6 = (bf16[4,8,32,128]{3,2,1,0:T(8,128)(2,1)S(1)}, bf16[4,8,32,128]{3,2,1,0:T(8,128)(2,1)S(1)}, u32[]{:S(2)}, u32[]{:S(2)}) collective-permute-start(bf16[4,8,32,128]{3,2,1,0:T(8,128)(2,1)S(1)} %get-tuple-element.20), channel_id=1, source_target_pairs={{0,2},{1,5},{2,0},{3,7},{4,6},{5,1},{6,4},{7,3},{8,10},{9,13},{10,... | collective-permute-start | bytes 786440 | tf_op jit(solution)/shard_map/ppermute | solution.py:21
  24.0 6.7 %collective-permute-start.9 = (bf16[4,8,32,128]{3,2,1,0:T(8,128)(2,1)S(1)}, bf16[4,8,32,128]{3,2,1,0:T(8,128)(2,1)S(1)}, u32[]{:S(2)}, u32[]{:S(2)}) collective-permute-start(bf16[4,8,32,128]{3,2,1,0:T(8,128)(2,1)S(1)} %get-tuple-element.22), channel_id=1, source_target_pairs={{0,2},{1,5},{2,0},{3,7},{4,6},{5,1},{6,4},{7,3},{8,10},{9,13},{10,... | collective-permute-start | bytes 786440 | tf_op jit(solution)/shard_map/ppermute | solution.py:21
  28.1 18.6 %copy-start = (f32[33,33]{1,0:T(8,128)S(1)}, f32[33,33]{1,0:T(8,128)}, u32[]{:S(2)}) copy-start(f32[33,33]{1,0:T(8,128)} %kernel_ref.1) | copy-start | bytes 13072
  28.1 5.7 %collective-permute-start.7 = (bf16[2,8,32,128]{3,2,1,0:T(8,128)(2,1)S(1)}, bf16[2,8,32,128]{3,2,1,0:T(8,128)(2,1)S(1)}, u32[]{:S(2)}, u32[]{:S(2)}) collective-permute-start(bf16[2,8,32,128]{3,2,1,0:T(8,128)(2,1)S(1)} %fusion.4), channel_id=1, source_target_pairs={{0,4},{1,9},{2,6},{3,11},{4,0},{5,13},{6,2},{7,15},{8,12},{9,1},{1... | collective-permute-start | bytes 393224 | tf_op jit(solution)/shard_map/ppermute | solution.py:21
  30.8 4.3 %collective-permute-start.10 = (bf16[2,8,32,128]{3,2,1,0:T(8,128)(2,1)S(1)}, bf16[2,8,32,128]{3,2,1,0:T(8,128)(2,1)S(1)}, u32[]{:S(2)}, u32[]{:S(2)}) collective-permute-start(bf16[2,8,32,128]{3,2,1,0:T(8,128)(2,1)S(1)} %fusion.5), channel_id=1, source_target_pairs={{0,4},{1,3},{2,6},{3,1},{4,0},{5,7},{6,2},{7,5},{8,12},{9,11},{10,... | collective-permute-start | bytes 393224 | tf_op jit(solution)/shard_map/ppermute | solution.py:21
  33.8 17.5 %copy-start.1 = (s32[16,128]{1,0:T(8,128)S(1)}, s32[16,128]{1,0:T(8,128)}, u32[]{:S(2)}) copy-start(s32[16,128]{1,0:T(8,128)} %mask_ref.1) | copy-start | bytes 24580
  33.8 4.3 %collective-permute-start.8 = (bf16[1,8,32,128]{3,2,1,0:T(8,128)(2,1)S(1)}, bf16[1,8,32,128]{3,2,1,0:T(8,128)(2,1)S(1)}, u32[]{:S(2)}, u32[]{:S(2)}) collective-permute-start(bf16[1,8,32,128]{3,2,1,0:T(8,128)(2,1)S(1)} %fusion.11), channel_id=1, source_target_pairs={{0,8},{1,3},{2,10},{3,1},{4,12},{5,7},{6,14},{7,5},{8,0},{9,11},{1... | collective-permute-start | bytes 196616 | tf_op jit(solution)/shard_map/ppermute | solution.py:21
  35.2 5.6 %collective-permute-start.11 = (bf16[1,8,32,128]{3,2,1,0:T(8,128)(2,1)S(1)}, bf16[1,8,32,128]{3,2,1,0:T(8,128)(2,1)S(1)}, u32[]{:S(2)}, u32[]{:S(2)}) collective-permute-start(bf16[1,8,32,128]{3,2,1,0:T(8,128)(2,1)S(1)} %fusion.13), channel_id=1, source_target_pairs={{0,8},{1,9},{2,10},{3,11},{4,12},{5,13},{6,14},{7,15},{8,0},{9,1},... | collective-permute-start | bytes 196616 | tf_op jit(solution)/shard_map/ppermute | solution.py:21
  40.8 6.4 %collective-permute-start.12 = (bf16[16,32,128]{2,1,0:T(8,128)(2,1)S(1)}, bf16[16,32,128]{2,1,0:T(8,128)(2,1)S(1)}, u32[]{:S(2)}, u32[]{:S(2)}) collective-permute-start(bf16[16,32,128]{2,1,0:T(8,128)(2,1)S(1)} %pad_maximum_fusion.own_ref), channel_id=1, source_target_pairs={{0,1},{1,0},{2,3},{3,2},{4,5},{5,4},{6,7},{7,6},{8,9},{9,8},{10,11... | collective-permute-start | bytes 393224 | tf_op jit(solution)/shard_map/ppermute | solution.py:21
  43.6 7.7 %collective-permute-start.13 = (bf16[16,32,128]{2,1,0:T(8,128)(2,1)S(1)}, bf16[16,32,128]{2,1,0:T(8,128)(2,1)S(1)}, u32[]{:S(2)}, u32[]{:S(2)}) collective-permute-start(bf16[16,32,128]{2,1,0:T(8,128)(2,1)S(1)} %pad_maximum_fusion.own_ref), channel_id=1, source_target_pairs={{1,2},{3,4},{5,6},{7,8},{9,10},{11,12},{13,14},{2,1},{4,3},{6,5},{... | collective-permute-start | bytes 393224 | tf_op jit(solution)/shard_map/ppermute | solution.py:348

commit v7 on v6

--- a/solution.py
+++ b/solution.py
@@ -94,27 +94,38 @@
     load(green_ref, own_ref, semaphore, first, lax.axis_index("space") & 1).wait()
 
 
-def fill_spread(rows, start, chosen_ref, repeat_ref, slip_ref, spread_ref):
-    owners, realizations, _ = slip_ref.shape
+def widen(chosen_ref, repeat_ref, slip_ref, wide_ref):
     group, depth = repeat_ref.shape
-    slip = jnp.concatenate([slip_ref[owner] for owner in range(owners)], axis=1)
+    slip = jnp.concatenate([slip_ref[owner] for owner in range(slip_ref.shape[0])], axis=1)
     picked = jnp.dot(slip, chosen_ref[...], preferred_element_type=jnp.float32)
     picked = picked.astype(jnp.bfloat16)
-    row_of = lax.broadcasted_iota(jnp.int32, (realizations, depth), 1) % rows
     for side in range(2):
-        wide = jnp.dot(
+        wide_ref[:, side * depth : (side + 1) * depth] = jnp.dot(
             picked[:, side * group : (side + 1) * group],
             repeat_ref[...],
             preferred_element_type=jnp.float32,
         )
-        for row in range(spread_ref.shape[0] // realizations):
-            spread_ref[
-                row * realizations : (row + 1) * realizations, side * depth : (side + 1) * depth
-            ] = jnp.where(row_of == start + row, wide, 0.0).astype(jnp.bfloat16)
-
-
-def away_kernel(places, stream, rows, start, chosen_ref, repeat_ref, slip_ref, *refs):
-    fill_spread(rows, start, chosen_ref, repeat_ref, slip_ref, refs[-1])
+
+
+def fill_spread(rows, start, wide_ref, spread_ref):
+    realizations, depth = wide_ref.shape
+    wide = wide_ref[...]
+    row_of = lax.broadcasted_iota(jnp.int32, (realizations, depth), 1) % rows
+    for row in range(spread_ref.shape[0] // realizations):
+        spread_ref[row * realizations : (row + 1) * realizations, :] = jnp.where(
+            row_of == start + row, wide, 0.0
+        ).astype(jnp.bfloat16)
+
+
+def first_kernel(places, rows, chosen_ref, repeat_ref, slip_ref, *refs):
+    parts, (out_ref, spread_ref, wide_ref) = refs[:-3], refs[-3:]
+    widen(chosen_ref, repeat_ref, slip_ref, wide_ref)
+    fill_spread(rows, 0, wide_ref, spread_ref)
+    uplift_kernel(places, 0, spread_ref, *parts, out_ref)
+
+
+def next_kernel(places, stream, rows, start, wide_ref, *refs):
+    fill_spread(rows, start, wide_ref, refs[-1])
     uplift_kernel(places, stream, refs[-1], *refs[:-1])
 
 
@@ -304,18 +315,31 @@
 
     lines = rows // STREAMS
 
+    wide = []
+
     def away_blocks(stream):
-        size = lines * realizations
+        sides = 2 * group * rows
+        shapes = (
+            jax.ShapeDtypeStruct((count // 4, lines, realizations, width), jnp.bfloat16),
+            jax.ShapeDtypeStruct((lines * realizations, sides), jnp.bfloat16),
+        )
+        if stream == 0:
+            sent, spread, table = pl.pallas_call(
+                functools.partial(first_kernel, places[1::2], rows),
+                out_shape=(*shapes, jax.ShapeDtypeStruct((realizations, sides), jnp.float32)),
+                in_specs=[VMEM] * (3 + len(parts)),
+                out_specs=(VMEM, VMEM, VMEM),
+                compiler_params=PARAMS,
+            )(chosen, repeat, slip, *parts)
+            wide.append(table)
+            return sent, spread
         return pl.pallas_call(
-            functools.partial(away_kernel, places[1::2], stream, rows, stream * lines),
-            out_shape=(
-                jax.ShapeDtypeStruct((count // 4, lines, realizations, width), jnp.bfloat16),
-                jax.ShapeDtypeStruct((size, 2 * group * rows), jnp.bfloat16),
-            ),
-            in_specs=[VMEM] * (3 + len(parts)),
+            functools.partial(next_kernel, places[1::2], stream, rows, stream * lines),
+            out_shape=shapes,
+            in_specs=[VMEM] * (1 + len(parts)),
             out_specs=(VMEM, VMEM),
             compiler_params=PARAMS,
-        )(chosen, repeat, slip, *parts)
+        )(wide[0], *parts)
 
     places = list(range(count // 2))
     streams = range(STREAMS)

time: 53 us -> 52.5 us (level)
  the two profiles are of different devices: /device:TPU:11 before, /device:TPU:9 now
where the time goes in v7:
time: 52.5 us; the launch traced here: 52.3 us
  starting transfers between devices  23.9 us (46%)
  Pallas kernels  14.9 us (28%)
  waiting for transfers between devices  12.9 us (25%)
    ppermute x13, starting transfers between devices, swap(): lax.ppermute(block, 'space', [(i, i ^ bits[i & 1]) for i in range(count)])  20.9 us
    ppermute x13, waiting for transfers between devices, swap(): lax.ppermute(block, 'space', [(i, i ^ bits[i & 1]) for i in range(count)])  8.92 us
    ppermute x1, waiting for transfers between devices, body(): across = lax.ppermute(seafloor, 'space', crossing)  4 us
    ppermute x1, starting transfers between devices, body(): across = lax.ppermute(seafloor, 'space', crossing)  3.04 us
    pallas_call x2, Pallas kernels, uplift_blocks(): pl.pallas_call(functools.partial(uplift_kernel, places, stream), out_shap...  2.58 us
    pallas_call x1, Pallas kernels, away_blocks(): pl.pallas_call(functools.partial(first_kernel, places[1::2], rows), out_s...  1.91 us
    pallas_call x1, Pallas kernels, body(): pl.pallas_call(rest_kernel, out_shape=part(group - group // 4), in_specs=...  1.9 us
    pallas_call x1, Pallas kernels, body(): pl.pallas_call(functools.partial(repeat_kernel, rows), out_shape=(part(gr...  1.88 us
  transfers between devices with their start and end apart: 14, of which 8 were waited for; matrix products, arithmetic and copies ran while one was open for 1% of the time, Pallas kernels for 18%

profile of v7, /device:TPU:9, one launch (start us, length us, event | category | flops | bytes accessed | tf_op | source)
XLA Modules:
  0.0 52.3 jit_solution(12230221590341543109)
XLA Ops:
  0.0 1.9 %shard_map.66 = (bf16[64,8,16,128]{3,2,1,0:T(8,128)(2,1)S(1)}, bf16[32,8,16,128]{3,2,1,0:T(8,128)(2,1)S(1)}, bf16[128,2048]{1,0:T(8,128)(2,1)S(1)}) custom-call(bf16[128,8,2,16,128]{4,3,2,1,0:T(8,128)(2,1)} %bitcast.48), custom_call_target="tpu_custom_call" | custom-call | tf_op jit(solution)/shard_map/pallas_call | solution.py:286
  1.9 0.7 %collective-permute-start.5 = (bf16[64,8,16,128]{3,2,1,0:T(8,128)(2,1)S(1)}, bf16[64,8,16,128]{3,2,1,0:T(8,128)(2,1)S(1)}, u32[]{:S(2)}, u32[]{:S(2)}) collective-permute-start(bf16[64,8,16,128]{3,2,1,0:T(8,128)(2,1)S(1)} %get-tuple-element.19), channel_id=1, source_target_pairs={{0,1},{1,0},{2,3},{3,2},{4,5},{5,4},{6,7},{7,6},{8,9},{9,8},{10,11... | collective-permute-start | bytes 6291464 | tf_op jit(solution)/shard_map/ppermute | solution.py:21
  2.6 1.6 %shard_map.65 = (bf16[64,8,16,128]{3,2,1,0:T(8,128)(2,1)S(1)}, bf16[2048,256]{1,0:T(8,128)(2,1)S(1)}) custom-call(s32[16,128]{1,0:T(8,128)} %bitcast.55, bf16[128,8,2,16,128]{4,3,2,1,0:T(8,128)(2,1)} %bitcast.49), custom_call_target="tpu_custom_call" | custom-call | tf_op jit(solution)/shard_map/pallas_call | solution.py:271
  4.3 0.1 collective-permute-start.4
  4.3 1.6 %shard_map.67 = bf16[1,32,128]{2,1,0:T(8,128)(2,1)S(1)} custom-call(bf16[32,4096]{1,0:T(8,128)(2,1)} %coefficients_hbm.1, bf16[4096,128]{1,0:T(8,128)(2,1)} %modes_hbm.1), custom_call_target="tpu_custom_call" | custom-call | tf_op jit(solution)/shard_map/pallas_call | solution.py:248
  5.9 1.3 %collective-permute-start = (bf16[1,32,128]{2,1,0:T(8,128)(2,1)S(1)}, bf16[1,32,128]{2,1,0:T(8,128)(2,1)S(1)}, u32[]{:S(2)}, u32[]{:S(2)}) collective-permute-start(bf16[1,32,128]{2,1,0:T(8,128)(2,1)S(1)} %shard_map.67), channel_id=1, source_target_pairs={{0,2},{1,3},{2,0},{3,1},{4,6},{5,7},{6,4},{7,5},{8,10},{9,11},{10,... | collective-permute-start | bytes 24584 | tf_op jit(solution)/shard_map/ppermute | solution.py:21
  7.2 1.9 %shard_map.68.refs_1_ = bf16[96,8,16,128]{3,2,1,0:T(8,128)(2,1)S(1)} custom-call(bf16[128,8,2,16,128]{4,3,2,1,0:T(8,128)(2,1)} %bitcast.50), custom_call_target="tpu_custom_call" | custom-call | tf_op jit(solution)/shard_map/pallas_call | solution.py:299
  9.1 0.0 collective-permute-done
  9.2 0.2 collective-permute-start.1
  9.4 2.4 %collective-permute-done.1 = bf16[2,32,128]{2,1,0:T(8,128)(2,1)S(1)} collective-permute-done((bf16[2,32,128]{2,1,0:T(8,128)(2,1)S(1)}, bf16[2,32,128]{2,1,0:T(8,128)(2,1)S(1)}, u32[]{:S(2)}, u32[]{:S(2)}) %collective-permute-start.1) | collective-permute-done | bytes 16416 | tf_op jit(solution)/shard_map/ppermute | solution.py:21
  11.8 2.3 %collective-permute-start.2 = (bf16[4,32,128]{2,1,0:T(8,128)(2,1)S(1)}, bf16[4,32,128]{2,1,0:T(8,128)(2,1)S(1)}, u32[]{:S(2)}, u32[]{:S(2)}) collective-permute-start(bf16[4,32,128]{2,1,0:T(8,128)(2,1)S(1)} %pad_maximum_fusion.2), channel_id=1, source_target_pairs={{0,8},{1,9},{2,10},{3,11},{4,12},{5,13},{6,14},{7,15},{8,0},{9,1},... | collective-permute-start | bytes 98312 | tf_op jit(solution)/shard_map/ppermute | solution.py:21
  14.2 1.3 %collective-permute-done.2 = bf16[4,32,128]{2,1,0:T(8,128)(2,1)S(1)} collective-permute-done((bf16[4,32,128]{2,1,0:T(8,128)(2,1)S(1)}, bf16[4,32,128]{2,1,0:T(8,128)(2,1)S(1)}, u32[]{:S(2)}, u32[]{:S(2)}) %collective-permute-start.2) | collective-permute-done | bytes 32800 | tf_op jit(solution)/shard_map/ppermute | solution.py:21
  15.5 3.3 %collective-permute-start.3 = (bf16[8,32,128]{2,1,0:T(8,128)(2,1)S(1)}, bf16[8,32,128]{2,1,0:T(8,128)(2,1)S(1)}, u32[]{:S(2)}, u32[]{:S(2)}) collective-permute-start(bf16[8,32,128]{2,1,0:T(8,128)(2,1)S(1)} %pad_maximum_fusion.1), channel_id=1, source_target_pairs={{0,1},{1,0},{2,3},{3,2},{4,5},{5,4},{6,7},{7,6},{8,9},{9,8},{10,11... | collective-permute-start | bytes 196616 | tf_op jit(solution)/shard_map/ppermute | solution.py:21
  18.8 0.9 %collective-permute-done.3 = bf16[8,32,128]{2,1,0:T(8,128)(2,1)S(1)} collective-permute-done((bf16[8,32,128]{2,1,0:T(8,128)(2,1)S(1)}, bf16[8,32,128]{2,1,0:T(8,128)(2,1)S(1)}, u32[]{:S(2)}, u32[]{:S(2)}) %collective-permute-start.3) | collective-permute-done | bytes 65568 | tf_op jit(solution)/shard_map/ppermute | solution.py:21
  19.7 0.0 collective-permute-done.5.refs_3_
  19.7 0.0 collective-permute-done.4.refs_2_
  19.7 1.9 %shard_map.69 = (bf16[4,8,32,128]{3,2,1,0:T(8,128)(2,1)S(1)}, bf16[256,4096]{1,0:T(8,128)(2,1)S(1)}, f32[32,4096]{1,0:T(8,128)S(1)}) custom-call(bf16[2048,256]{1,0:T(8,128)(2,1)S(1)} %get-tuple-element.15.chosen_ref, bf16[128,2048]{1,0:T(8,128)(2,1)S(1)} %get-tuple-element.16.repeat_ref, ...), custom_call_target="tpu_custom_call" | custom-call | tf_op jit(solution)/shard_map/pallas_call | solution.py:327
  21.6 0.1 collective-permute-start.6
  21.7 1.3 %shard_map.71 = (bf16[4,8,32,128]{3,2,1,0:T(8,128)(2,1)S(1)}, bf16[256,4096]{1,0:T(8,128)(2,1)S(1)}) custom-call(f32[32,4096]{1,0:T(8,128)S(1)} %get-tuple-element.22.wide_ref, bf16[32,8,16,128]{3,2,1,0:T(8,128)(2,1)S(1)} %get-tuple-element.17.refs_0_, bf16[96,8,16,128]{3,2,1,0:T(8,128)(2,1)S(1)} %shard_map.68.refs_1_, ...), custom_call_target="tpu_custom_call" | custom-call | tf_op jit(solution)/shard_map/pallas_call | solution.py:336
  23.0 1.5 %collective-permute-start.9 = (bf16[4,8,32,128]{3,2,1,0:T(8,128)(2,1)S(1)}, bf16[4,8,32,128]{3,2,1,0:T(8,128)(2,1)S(1)}, u32[]{:S(2)}, u32[]{:S(2)}) collective-permute-start(bf16[4,8,32,128]{3,2,1,0:T(8,128)(2,1)S(1)} %get-tuple-element.24), channel_id=1, source_target_pairs={{0,2},{1,5},{2,0},{3,7},{4,6},{5,1},{6,4},{7,3},{8,10},{9,13},{10,... | collective-permute-start | bytes 786440 | tf_op jit(solution)/shard_map/ppermute | solution.py:21
  24.5 1.3 %shard_map.70 = f32[4,8,32,128]{3,2,1,0:T(8,128)S(1)} custom-call(bf16[256,4096]{1,0:T(8,128)(2,1)S(1)} %get-tuple-element.20.spread_ref, bf16[32,8,16,128]{3,2,1,0:T(8,128)(2,1)S(1)} %get-tuple-element.17.refs_0_, bf16[96,8,16,128]{3,2,1,0:T(8,128)(2,1)S(1)} %shard_map.68.refs_1_, bf16[64,8,16,128]{3,2,1,0:T(8,128)(2,1)S(1)} %collective-permute-done.4.refs_2_, ...), custom_call_target="tpu_custom_call" | custom-call | tf_op jit(solution)/shard_map/pallas_call | solution.py:165
  25.8 1.3 %shard_map.72 = f32[4,8,32,128]{3,2,1,0:T(8,128)S(1)} custom-call(bf16[256,4096]{1,0:T(8,128)(2,1)S(1)} %get-tuple-element.23.spread_ref, bf16[32,8,16,128]{3,2,1,0:T(8,128)(2,1)S(1)} %get-tuple-element.17.refs_0_, bf16[96,8,16,128]{3,2,1,0:T(8,128)(2,1)S(1)} %shard_map.68.refs_1_, bf16[64,8,16,128]{3,2,1,0:T(8,128)(2,1)S(1)} %collective-permute-done.4.refs_2_, ...), custom_call_target="tpu_custom_call" | custom-call | tf_op jit(solution)/shard_map/pallas_call | solution.py:165
  27.1 0.1 collective-permute-done.6
  27.2 0.1 convert_add_fusion.1
  27.3 0.0 copy-start
  27.3 2.6 %collective-permute-start.7 = (bf16[2,8,32,128]{3,2,1,0:T(8,128)(2,1)S(1)}, bf16[2,8,32,128]{3,2,1,0:T(8,128)(2,1)S(1)}, u32[]{:S(2)}, u32[]{:S(2)}) collective-permute-start(bf16[2,8,32,128]{3,2,1,0:T(8,128)(2,1)S(1)} %fusion.4), channel_id=1, source_target_pairs={{0,4},{1,9},{2,6},{3,11},{4,0},{5,13},{6,2},{7,15},{8,12},{9,1},{1... | collective-permute-start | bytes 393224 | tf_op jit(solution)/shard_map/ppermute | solution.py:21
  30.0 0.1 collective-permute-done.9
  30.0 0.1 convert_add_fusion
  30.1 1.3 %collective-permute-start.10 = (bf16[2,8,32,128]{3,2,1,0:T(8,128)(2,1)S(1)}, bf16[2,8,32,128]{3,2,1,0:T(8,128)(2,1)S(1)}, u32[]{:S(2)}, u32[]{:S(2)}) collective-permute-start(bf16[2,8,32,128]{3,2,1,0:T(8,128)(2,1)S(1)} %fusion.5), channel_id=1, source_target_pairs={{0,4},{1,3},{2,6},{3,1},{4,0},{5,7},{6,2},{7,5},{8,12},{9,11},{10,... | collective-permute-start | bytes 393224 | tf_op jit(solution)/shard_map/ppermute | solution.py:21
  31.4 1.5 %collective-permute-done.7 = bf16[2,8,32,128]{3,2,1,0:T(8,128)(2,1)S(1)} collective-permute-done((bf16[2,8,32,128]{3,2,1,0:T(8,128)(2,1)S(1)}, bf16[2,8,32,128]{3,2,1,0:T(8,128)(2,1)S(1)}, u32[]{:S(2)}, u32[]{:S(2)}) %collective-permute-start.7) | collective-permute-done | bytes 131104 | tf_op jit(solution)/shard_map/ppermute | solution.py:21
  33.0 0.0 copy-start.1
  33.1 1.3 %collective-permute-start.8 = (bf16[1,8,32,128]{3,2,1,0:T(8,128)(2,1)S(1)}, bf16[1,8,32,128]{3,2,1,0:T(8,128)(2,1)S(1)}, u32[]{:S(2)}, u32[]{:S(2)}) collective-permute-start(bf16[1,8,32,128]{3,2,1,0:T(8,128)(2,1)S(1)} %fusion.11), channel_id=1, source_target_pairs={{0,8},{1,3},{2,10},{3,1},{4,12},{5,7},{6,14},{7,5},{8,0},{9,11},{1... | collective-permute-start | bytes 196616 | tf_op jit(solution)/shard_map/ppermute | solution.py:21
  34.4 0.0 collective-permute-done.10
  34.4 3.0 %collective-permute-start.11 = (bf16[1,8,32,128]{3,2,1,0:T(8,128)(2,1)S(1)}, bf16[1,8,32,128]{3,2,1,0:T(8,128)(2,1)S(1)}, u32[]{:S(2)}, u32[]{:S(2)}) collective-permute-start(bf16[1,8,32,128]{3,2,1,0:T(8,128)(2,1)S(1)} %fusion.13), channel_id=1, source_target_pairs={{0,8},{1,9},{2,10},{3,11},{4,12},{5,13},{6,14},{7,15},{8,0},{9,1},... | collective-permute-start | bytes 196616 | tf_op jit(solution)/shard_map/ppermute | solution.py:21
  37.4 0.0 collective-permute-done.8
  37.4 2.5 %collective-permute-done.11 = bf16[1,8,32,128]{3,2,1,0:T(8,128)(2,1)S(1)} collective-permute-done((bf16[1,8,32,128]{3,2,1,0:T(8,128)(2,1)S(1)}, bf16[1,8,32,128]{3,2,1,0:T(8,128)(2,1)S(1)}, u32[]{:S(2)}, u32[]{:S(2)}) %collective-permute-start.11) | collective-permute-done | bytes 65568 | tf_op jit(solution)/shard_map/ppermute | solution.py:21
  40.0 3.1 %collective-permute-start.12 = (bf16[16,32,128]{2,1,0:T(8,128)(2,1)S(1)}, bf16[16,32,128]{2,1,0:T(8,128)(2,1)S(1)}, u32[]{:S(2)}, u32[]{:S(2)}) collective-permute-start(bf16[16,32,128]{2,1,0:T(8,128)(2,1)S(1)} %pad_maximum_fusion.own_ref), channel_id=1, source_target_pairs={{0,1},{1,0},{2,3},{3,2},{4,5},{5,4},{6,7},{7,6},{8,9},{9,8},{10,11... | collective-permute-start | bytes 393224 | tf_op jit(solution)/shard_map/ppermute | solution.py:21
  43.1 3.0 %collective-permute-start.13 = (bf16[16,32,128]{2,1,0:T(8,128)(2,1)S(1)}, bf16[16,32,128]{2,1,0:T(8,128)(2,1)S(1)}, u32[]{:S(2)}, u32[]{:S(2)}) collective-permute-start(bf16[16,32,128]{2,1,0:T(8,128)(2,1)S(1)} %pad_maximum_fusion.own_ref), channel_id=1, source_target_pairs={{1,2},{3,4},{5,6},{7,8},{9,10},{11,12},{13,14},{2,1},{4,3},{6,5},{... | collective-permute-start | bytes 393224 | tf_op jit(solution)/shard_map/ppermute | solution.py:372
  46.2 0.0 copy-done
  46.2 0.6 %shard_map.64.bands_ref = bf16[4352,256]{1,0:T(8,128)(2,1)S(1)} custom-call(f32[33,33]{1,0:T(8,128)S(1)} %copy-done), custom_call_target="tpu_custom_call" | custom-call | tf_op jit(solution)/shard_map/pallas_call | solution.py:308
  46.8 0.0 collective-permute-done.12.beside_ref
  46.8 4.0 %collective-permute-done.13.across_ref = bf16[16,32,128]{2,1,0:T(8,128)(2,1)S(1)} collective-permute-done((bf16[16,32,128]{2,1,0:T(8,128)(2,1)S(1)}, bf16[16,32,128]{2,1,0:T(8,128)(2,1)S(1)}, u32[]{:S(2)}, u32[]{:S(2)}) %collective-permute-start.13) | collective-permute-done | bytes 131104 | tf_op jit(solution)/shard_map/ppermute | solution.py:372
  50.8 0.0 copy-done.1
  50.8 1.5 %shard_map.73 = f32[32,16,128]{2,1,0:T(8,128)} custom-call(bf16[4352,256]{1,0:T(8,128)(2,1)S(1)} %shard_map.64.bands_ref, s32[16,128]{1,0:T(8,128)S(1)} %copy-done.1, bf16[16,32,128]{2,1,0:T(8,128)(2,1)S(1)} %collective-permute-done.12.beside_ref, bf16[16,32,128]{2,1,0:T(8,128)(2,1)S(1)} %collective-permute-done.13.across_ref, ...), custom_call_target="tpu_custom_call" | custom-call | tf_op jit(solution)/shard_map/pallas_call | solution.py:374
  (17 shorter events, 0.2 us)
Async XLA Ops:
  1.9 17.8 %collective-permute-start.5 = (bf16[64,8,16,128]{3,2,1,0:T(8,128)(2,1)S(1)}, bf16[64,8,16,128]{3,2,1,0:T(8,128)(2,1)S(1)}, u32[]{:S(2)}, u32[]{:S(2)}) collective-permute-start(bf16[64,8,16,128]{3,2,1,0:T(8,128)(2,1)S(1)} %get-tuple-element.19), channel_id=1, source_target_pairs={{0,1},{1,0},{2,3},{3,2},{4,5},{5,4},{6,7},{7,6},{8,9},{9,8},{10,11... | collective-permute-start | bytes 6291464 | tf_op jit(solution)/shard_map/ppermute | solution.py:21
  4.3 15.5 %collective-permute-start.4 = (bf16[64,8,16,128]{3,2,1,0:T(8,128)(2,1)S(1)}, bf16[64,8,16,128]{3,2,1,0:T(8,128)(2,1)S(1)}, u32[]{:S(2)}, u32[]{:S(2)}) collective-permute-start(bf16[64,8,16,128]{3,2,1,0:T(8,128)(2,1)S(1)} %get-tuple-element.18), channel_id=1, source_target_pairs={{0,1},{1,0},{2,3},{3,2},{4,5},{5,4},{6,7},{7,6},{8,9},{9,8},{10,11... | collective-permute-start | bytes 6291464 | tf_op jit(solution)/shard_map/ppermute | solution.py:21
  5.9 3.2 %collective-permute-start = (bf16[1,32,128]{2,1,0:T(8,128)(2,1)S(1)}, bf16[1,32,128]{2,1,0:T(8,128)(2,1)S(1)}, u32[]{:S(2)}, u32[]{:S(2)}) collective-permute-start(bf16[1,32,128]{2,1,0:T(8,128)(2,1)S(1)} %shard_map.67), channel_id=1, source_target_pairs={{0,2},{1,3},{2,0},{3,1},{4,6},{5,7},{6,4},{7,5},{8,10},{9,11},{10,... | collective-permute-start | bytes 24584 | tf_op jit(solution)/shard_map/ppermute | solution.py:21
  9.2 2.7 %collective-permute-start.1 = (bf16[2,32,128]{2,1,0:T(8,128)(2,1)S(1)}, bf16[2,32,128]{2,1,0:T(8,128)(2,1)S(1)}, u32[]{:S(2)}, u32[]{:S(2)}) collective-permute-start(bf16[2,32,128]{2,1,0:T(8,128)(2,1)S(1)} %pad_maximum_fusion.3), channel_id=1, source_target_pairs={{0,4},{1,5},{2,6},{3,7},{4,0},{5,1},{6,2},{7,3},{8,12},{9,13},{10,... | collective-permute-start | bytes 49160 | tf_op jit(solution)/shard_map/ppermute | solution.py:21
  11.8 3.7 %collective-permute-start.2 = (bf16[4,32,128]{2,1,0:T(8,128)(2,1)S(1)}, bf16[4,32,128]{2,1,0:T(8,128)(2,1)S(1)}, u32[]{:S(2)}, u32[]{:S(2)}) collective-permute-start(bf16[4,32,128]{2,1,0:T(8,128)(2,1)S(1)} %pad_maximum_fusion.2), channel_id=1, source_target_pairs={{0,8},{1,9},{2,10},{3,11},{4,12},{5,13},{6,14},{7,15},{8,0},{9,1},... | collective-permute-start | bytes 98312 | tf_op jit(solution)/shard_map/ppermute | solution.py:21
  15.5 4.2 %collective-permute-start.3 = (bf16[8,32,128]{2,1,0:T(8,128)(2,1)S(1)}, bf16[8,32,128]{2,1,0:T(8,128)(2,1)S(1)}, u32[]{:S(2)}, u32[]{:S(2)}) collective-permute-start(bf16[8,32,128]{2,1,0:T(8,128)(2,1)S(1)} %pad_maximum_fusion.1), channel_id=1, source_target_pairs={{0,1},{1,0},{2,3},{3,2},{4,5},{5,4},{6,7},{7,6},{8,9},{9,8},{10,11... | collective-permute-start | bytes 196616 | tf_op jit(solution)/shard_map/ppermute | solution.py:21
  21.6 5.6 %collective-permute-start.6 = (bf16[4,8,32,128]{3,2,1,0:T(8,128)(2,1)S(1)}, bf16[4,8,32,128]{3,2,1,0:T(8,128)(2,1)S(1)}, u32[]{:S(2)}, u32[]{:S(2)}) collective-permute-start(bf16[4,8,32,128]{3,2,1,0:T(8,128)(2,1)S(1)} %get-tuple-element.21), channel_id=1, source_target_pairs={{0,2},{1,5},{2,0},{3,7},{4,6},{5,1},{6,4},{7,3},{8,10},{9,13},{10,... | collective-permute-start | bytes 786440 | tf_op jit(solution)/shard_map/ppermute | solution.py:21
  23.0 7.0 %collective-permute-start.9 = (bf16[4,8,32,128]{3,2,1,0:T(8,128)(2,1)S(1)}, bf16[4,8,32,128]{3,2,1,0:T(8,128)(2,1)S(1)}, u32[]{:S(2)}, u32[]{:S(2)}) collective-permute-start(bf16[4,8,32,128]{3,2,1,0:T(8,128)(2,1)S(1)} %get-tuple-element.24), channel_id=1, source_target_pairs={{0,2},{1,5},{2,0},{3,7},{4,6},{5,1},{6,4},{7,3},{8,10},{9,13},{10,... | collective-permute-start | bytes 786440 | tf_op jit(solution)/shard_map/ppermute | solution.py:21
  27.3 18.9 %copy-start = (f32[33,33]{1,0:T(8,128)S(1)}, f32[33,33]{1,0:T(8,128)}, u32[]{:S(2)}) copy-start(f32[33,33]{1,0:T(8,128)} %kernel_ref.1) | copy-start | bytes 13072
  27.3 5.6 %collective-permute-start.7 = (bf16[2,8,32,128]{3,2,1,0:T(8,128)(2,1)S(1)}, bf16[2,8,32,128]{3,2,1,0:T(8,128)(2,1)S(1)}, u32[]{:S(2)}, u32[]{:S(2)}) collective-permute-start(bf16[2,8,32,128]{3,2,1,0:T(8,128)(2,1)S(1)} %fusion.4), channel_id=1, source_target_pairs={{0,4},{1,9},{2,6},{3,11},{4,0},{5,13},{6,2},{7,15},{8,12},{9,1},{1... | collective-permute-start | bytes 393224 | tf_op jit(solution)/shard_map/ppermute | solution.py:21
  30.1 4.2 %collective-permute-start.10 = (bf16[2,8,32,128]{3,2,1,0:T(8,128)(2,1)S(1)}, bf16[2,8,32,128]{3,2,1,0:T(8,128)(2,1)S(1)}, u32[]{:S(2)}, u32[]{:S(2)}) collective-permute-start(bf16[2,8,32,128]{3,2,1,0:T(8,128)(2,1)S(1)} %fusion.5), channel_id=1, source_target_pairs={{0,4},{1,3},{2,6},{3,1},{4,0},{5,7},{6,2},{7,5},{8,12},{9,11},{10,... | collective-permute-start | bytes 393224 | tf_op jit(solution)/shard_map/ppermute | solution.py:21
  33.0 17.8 %copy-start.1 = (s32[16,128]{1,0:T(8,128)S(1)}, s32[16,128]{1,0:T(8,128)}, u32[]{:S(2)}) copy-start(s32[16,128]{1,0:T(8,128)} %mask_ref.1) | copy-start | bytes 24580
  33.1 4.3 %collective-permute-start.8 = (bf16[1,8,32,128]{3,2,1,0:T(8,128)(2,1)S(1)}, bf16[1,8,32,128]{3,2,1,0:T(8,128)(2,1)S(1)}, u32[]{:S(2)}, u32[]{:S(2)}) collective-permute-start(bf16[1,8,32,128]{3,2,1,0:T(8,128)(2,1)S(1)} %fusion.11), channel_id=1, source_target_pairs={{0,8},{1,3},{2,10},{3,1},{4,12},{5,7},{6,14},{7,5},{8,0},{9,11},{1... | collective-permute-start | bytes 196616 | tf_op jit(solution)/shard_map/ppermute | solution.py:21
  34.4 5.5 %collective-permute-start.11 = (bf16[1,8,32,128]{3,2,1,0:T(8,128)(2,1)S(1)}, bf16[1,8,32,128]{3,2,1,0:T(8,128)(2,1)S(1)}, u32[]{:S(2)}, u32[]{:S(2)}) collective-permute-start(bf16[1,8,32,128]{3,2,1,0:T(8,128)(2,1)S(1)} %fusion.13), channel_id=1, source_target_pairs={{0,8},{1,9},{2,10},{3,11},{4,12},{5,13},{6,14},{7,15},{8,0},{9,1},... | collective-permute-start | bytes 196616 | tf_op jit(solution)/shard_map/ppermute | solution.py:21
  40.0 6.8 %collective-permute-start.12 = (bf16[16,32,128]{2,1,0:T(8,128)(2,1)S(1)}, bf16[16,32,128]{2,1,0:T(8,128)(2,1)S(1)}, u32[]{:S(2)}, u32[]{:S(2)}) collective-permute-start(bf16[16,32,128]{2,1,0:T(8,128)(2,1)S(1)} %pad_maximum_fusion.own_ref), channel_id=1, source_target_pairs={{0,1},{1,0},{2,3},{3,2},{4,5},{5,4},{6,7},{7,6},{8,9},{9,8},{10,11... | collective-permute-start | bytes 393224 | tf_op jit(solution)/shard_map/ppermute | solution.py:21
  43.1 7.7 %collective-permute-start.13 = (bf16[16,32,128]{2,1,0:T(8,128)(2,1)S(1)}, bf16[16,32,128]{2,1,0:T(8,128)(2,1)S(1)}, u32[]{:S(2)}, u32[]{:S(2)}) collective-permute-start(bf16[16,32,128]{2,1,0:T(8,128)(2,1)S(1)} %pad_maximum_fusion.own_ref), channel_id=1, source_target_pairs={{1,2},{3,4},{5,6},{7,8},{9,10},{11,12},{13,14},{2,1},{4,3},{6,5},{... | collective-permute-start | bytes 393224 | tf_op jit(solution)/shard_map/ppermute | solution.py:372

commit v8 on v7

--- a/solution.py
+++ b/solution.py
@@ -313,12 +313,12 @@
         compiler_params=PARAMS,
     )(kernel)
 
-    lines = rows // STREAMS
-
+    cuts = [0, rows * 7 // 16, rows]
     wide = []
 
     def away_blocks(stream):
         sides = 2 * group * rows
+        lines = cuts[stream + 1] - cuts[stream]
         shapes = (
             jax.ShapeDtypeStruct((count // 4, lines, realizations, width), jnp.bfloat16),
             jax.ShapeDtypeStruct((lines * realizations, sides), jnp.bfloat16),
@@ -334,7 +334,7 @@
             wide.append(table)
             return sent, spread
         return pl.pallas_call(
-            functools.partial(next_kernel, places[1::2], stream, rows, stream * lines),
+            functools.partial(next_kernel, places[1::2], stream, rows, cuts[stream]),
             out_shape=shapes,
             in_specs=[VMEM] * (1 + len(parts)),
             out_specs=(VMEM, VMEM),

time: 52.5 us -> 52.6 us (level)
  the two profiles are of different devices: /device:TPU:9 before, /device:TPU:27 now
where the time goes in v8:
time: 52.6 us; the launch traced here: 52.3 us
  waiting for transfers between devices  21.6 us (41%)
  starting transfers between devices  15.3 us (29%)
  Pallas kernels  14.9 us (28%)
    ppermute x13, waiting for transfers between devices, swap(): lax.ppermute(block, 'space', [(i, i ^ bits[i & 1]) for i in range(count)])  17 us
    ppermute x13, starting transfers between devices, swap(): lax.ppermute(block, 'space', [(i, i ^ bits[i & 1]) for i in range(count)])  12.8 us
    ppermute x1, waiting for transfers between devices, body(): across = lax.ppermute(seafloor, 'space', crossing)  4.54 us
    pallas_call x2, Pallas kernels, uplift_blocks(): pl.pallas_call(functools.partial(uplift_kernel, places, stream), out_shap...  2.58 us
    ppermute x1, starting transfers between devices, body(): across = lax.ppermute(seafloor, 'space', crossing)  2.5 us
    pallas_call x1, Pallas kernels, body(): pl.pallas_call(rest_kernel, out_shape=part(group - group // 4), in_specs=...  1.9 us
    pallas_call x1, Pallas kernels, body(): pl.pallas_call(functools.partial(repeat_kernel, rows), out_shape=(part(gr...  1.88 us
    pallas_call x1, Pallas kernels, away_blocks(): pl.pallas_call(functools.partial(first_kernel, places[1::2], rows), out_s...  1.78 us
  transfers between devices with their start and end apart: 14, of which 8 were waited for; matrix products, arithmetic and copies ran while one was open for 1% of the time, Pallas kernels for 19%

profile of v8, /device:TPU:27, one launch (start us, length us, event | category | flops | bytes accessed | tf_op | source)
XLA Modules:
  0.0 52.3 jit_solution(15795560197439837919)
XLA Ops:
  0.0 1.9 %shard_map.66 = (bf16[64,8,16,128]{3,2,1,0:T(8,128)(2,1)S(1)}, bf16[32,8,16,128]{3,2,1,0:T(8,128)(2,1)S(1)}, bf16[128,2048]{1,0:T(8,128)(2,1)S(1)}) custom-call(bf16[128,8,2,16,128]{4,3,2,1,0:T(8,128)(2,1)} %bitcast.48), custom_call_target="tpu_custom_call" | custom-call | tf_op jit(solution)/shard_map/pallas_call | solution.py:286
  1.9 0.7 %collective-permute-start.5 = (bf16[64,8,16,128]{3,2,1,0:T(8,128)(2,1)S(1)}, bf16[64,8,16,128]{3,2,1,0:T(8,128)(2,1)S(1)}, u32[]{:S(2)}, u32[]{:S(2)}) collective-permute-start(bf16[64,8,16,128]{3,2,1,0:T(8,128)(2,1)S(1)} %get-tuple-element.19), channel_id=1, source_target_pairs={{0,1},{1,0},{2,3},{3,2},{4,5},{5,4},{6,7},{7,6},{8,9},{9,8},{10,11... | collective-permute-start | bytes 6291464 | tf_op jit(solution)/shard_map/ppermute | solution.py:21
  2.6 1.6 %shard_map.65 = (bf16[64,8,16,128]{3,2,1,0:T(8,128)(2,1)S(1)}, bf16[2048,256]{1,0:T(8,128)(2,1)S(1)}) custom-call(s32[16,128]{1,0:T(8,128)} %bitcast.55, bf16[128,8,2,16,128]{4,3,2,1,0:T(8,128)(2,1)} %bitcast.49), custom_call_target="tpu_custom_call" | custom-call | tf_op jit(solution)/shard_map/pallas_call | solution.py:271
  4.3 0.1 collective-permute-start.4
  4.3 1.6 %shard_map.67 = bf16[1,32,128]{2,1,0:T(8,128)(2,1)S(1)} custom-call(bf16[32,4096]{1,0:T(8,128)(2,1)} %coefficients_hbm.1, bf16[4096,128]{1,0:T(8,128)(2,1)} %modes_hbm.1), custom_call_target="tpu_custom_call" | custom-call | tf_op jit(solution)/shard_map/pallas_call | solution.py:248
  5.9 1.3 %collective-permute-start = (bf16[1,32,128]{2,1,0:T(8,128)(2,1)S(1)}, bf16[1,32,128]{2,1,0:T(8,128)(2,1)S(1)}, u32[]{:S(2)}, u32[]{:S(2)}) collective-permute-start(bf16[1,32,128]{2,1,0:T(8,128)(2,1)S(1)} %shard_map.67), channel_id=1, source_target_pairs={{0,2},{1,3},{2,0},{3,1},{4,6},{5,7},{6,4},{7,5},{8,10},{9,11},{10,... | collective-permute-start | bytes 24584 | tf_op jit(solution)/shard_map/ppermute | solution.py:21
  7.2 1.9 %shard_map.68.refs_1_ = bf16[96,8,16,128]{3,2,1,0:T(8,128)(2,1)S(1)} custom-call(bf16[128,8,2,16,128]{4,3,2,1,0:T(8,128)(2,1)} %bitcast.50), custom_call_target="tpu_custom_call" | custom-call | tf_op jit(solution)/shard_map/pallas_call | solution.py:299
  9.1 0.0 collective-permute-done
  9.2 0.2 collective-permute-start.1
  9.4 2.4 %collective-permute-done.1 = bf16[2,32,128]{2,1,0:T(8,128)(2,1)S(1)} collective-permute-done((bf16[2,32,128]{2,1,0:T(8,128)(2,1)S(1)}, bf16[2,32,128]{2,1,0:T(8,128)(2,1)S(1)}, u32[]{:S(2)}, u32[]{:S(2)}) %collective-permute-start.1) | collective-permute-done | bytes 16416 | tf_op jit(solution)/shard_map/ppermute | solution.py:21
  11.8 0.1 collective-permute-start.2
  11.9 3.8 %collective-permute-done.2 = bf16[4,32,128]{2,1,0:T(8,128)(2,1)S(1)} collective-permute-done((bf16[4,32,128]{2,1,0:T(8,128)(2,1)S(1)}, bf16[4,32,128]{2,1,0:T(8,128)(2,1)S(1)}, u32[]{:S(2)}, u32[]{:S(2)}) %collective-permute-start.2) | collective-permute-done | bytes 32800 | tf_op jit(solution)/shard_map/ppermute | solution.py:21
  15.7 3.3 %collective-permute-start.3 = (bf16[8,32,128]{2,1,0:T(8,128)(2,1)S(1)}, bf16[8,32,128]{2,1,0:T(8,128)(2,1)S(1)}, u32[]{:S(2)}, u32[]{:S(2)}) collective-permute-start(bf16[8,32,128]{2,1,0:T(8,128)(2,1)S(1)} %pad_maximum_fusion.1), channel_id=1, source_target_pairs={{0,1},{1,0},{2,3},{3,2},{4,5},{5,4},{6,7},{7,6},{8,9},{9,8},{10,11... | collective-permute-start | bytes 196616 | tf_op jit(solution)/shard_map/ppermute | solution.py:21
  19.0 0.9 %collective-permute-done.3 = bf16[8,32,128]{2,1,0:T(8,128)(2,1)S(1)} collective-permute-done((bf16[8,32,128]{2,1,0:T(8,128)(2,1)S(1)}, bf16[8,32,128]{2,1,0:T(8,128)(2,1)S(1)}, u32[]{:S(2)}, u32[]{:S(2)}) %collective-permute-start.3) | collective-permute-done | bytes 65568 | tf_op jit(solution)/shard_map/ppermute | solution.py:21
  19.9 0.0 collective-permute-done.5.refs_3_
  19.9 0.0 collective-permute-done.4.refs_2_
  20.0 1.8 %shard_map.69 = (bf16[4,7,32,128]{3,2,1,0:T(8,128)(2,1)S(1)}, bf16[224,4096]{1,0:T(8,128)(2,1)S(1)}, f32[32,4096]{1,0:T(8,128)S(1)}) custom-call(bf16[2048,256]{1,0:T(8,128)(2,1)S(1)} %get-tuple-element.15.chosen_ref, bf16[128,2048]{1,0:T(8,128)(2,1)S(1)} %get-tuple-element.16.repeat_ref, ...), custom_call_target="tpu_custom_call" | custom-call | tf_op jit(solution)/shard_map/pallas_call | solution.py:327
  21.7 0.1 collective-permute-start.6
  21.8 1.4 %shard_map.71 = (bf16[4,9,32,128]{3,2,1,0:T(8,128)(2,1)S(1)}, bf16[288,4096]{1,0:T(8,128)(2,1)S(1)}) custom-call(f32[32,4096]{1,0:T(8,128)S(1)} %get-tuple-element.22.wide_ref, bf16[32,8,16,128]{3,2,1,0:T(8,128)(2,1)S(1)} %get-tuple-element.17.refs_0_, bf16[96,8,16,128]{3,2,1,0:T(8,128)(2,1)S(1)} %shard_map.68.refs_1_, ...), custom_call_target="tpu_custom_call" | custom-call | tf_op jit(solution)/shard_map/pallas_call | solution.py:336
  23.2 1.5 %collective-permute-start.9 = (bf16[4,9,32,128]{3,2,1,0:T(8,128)(2,1)S(1)}, bf16[4,9,32,128]{3,2,1,0:T(8,128)(2,1)S(1)}, u32[]{:S(2)}, u32[]{:S(2)}) collective-permute-start(bf16[4,9,32,128]{3,2,1,0:T(8,128)(2,1)S(1)} %get-tuple-element.24), channel_id=1, source_target_pairs={{0,2},{1,5},{2,0},{3,7},{4,6},{5,1},{6,4},{7,3},{8,10},{9,13},{10,... | collective-permute-start | bytes 884744 | tf_op jit(solution)/shard_map/ppermute | solution.py:21
  24.8 1.2 %shard_map.70 = f32[4,7,32,128]{3,2,1,0:T(8,128)S(1)} custom-call(bf16[224,4096]{1,0:T(8,128)(2,1)S(1)} %get-tuple-element.20.spread_ref, bf16[32,8,16,128]{3,2,1,0:T(8,128)(2,1)S(1)} %get-tuple-element.17.refs_0_, bf16[96,8,16,128]{3,2,1,0:T(8,128)(2,1)S(1)} %shard_map.68.refs_1_, bf16[64,8,16,128]{3,2,1,0:T(8,128)(2,1)S(1)} %collective-permute-done.4.refs_2_, ...), custom_call_target="tpu_custom_call" | custom-call | tf_op jit(solution)/shard_map/pallas_call | solution.py:165
  25.9 1.4 %shard_map.72 = f32[4,9,32,128]{3,2,1,0:T(8,128)S(1)} custom-call(bf16[288,4096]{1,0:T(8,128)(2,1)S(1)} %get-tuple-element.23.spread_ref, bf16[32,8,16,128]{3,2,1,0:T(8,128)(2,1)S(1)} %get-tuple-element.17.refs_0_, bf16[96,8,16,128]{3,2,1,0:T(8,128)(2,1)S(1)} %shard_map.68.refs_1_, bf16[64,8,16,128]{3,2,1,0:T(8,128)(2,1)S(1)} %collective-permute-done.4.refs_2_, ...), custom_call_target="tpu_custom_call" | custom-call | tf_op jit(solution)/shard_map/pallas_call | solution.py:165
  27.4 0.0 collective-permute-done.6
  27.4 0.1 convert_add_fusion.1
  27.5 0.0 copy-start
  27.5 0.1 collective-permute-start.7
  27.5 2.6 %collective-permute-done.9 = bf16[4,9,32,128]{3,2,1,0:T(8,128)(2,1)S(1)} collective-permute-done((bf16[4,9,32,128]{3,2,1,0:T(8,128)(2,1)S(1)}, bf16[4,9,32,128]{3,2,1,0:T(8,128)(2,1)S(1)}, u32[]{:S(2)}, u32[]{:S(2)}) %collective-permute-start.9) | collective-permute-done | bytes 294944 | tf_op jit(solution)/shard_map/ppermute | solution.py:21
  30.1 0.1 convert_add_fusion
  30.2 1.3 %collective-permute-start.10 = (bf16[2,9,32,128]{3,2,1,0:T(8,128)(2,1)S(1)}, bf16[2,9,32,128]{3,2,1,0:T(8,128)(2,1)S(1)}, u32[]{:S(2)}, u32[]{:S(2)}) collective-permute-start(bf16[2,9,32,128]{3,2,1,0:T(8,128)(2,1)S(1)} %fusion.4), channel_id=1, source_target_pairs={{0,4},{1,3},{2,6},{3,1},{4,0},{5,7},{6,2},{7,5},{8,12},{9,11},{10,... | collective-permute-start | bytes 442376 | tf_op jit(solution)/shard_map/ppermute | solution.py:21
  31.6 1.6 %collective-permute-done.7 = bf16[2,7,32,128]{3,2,1,0:T(8,128)(2,1)S(1)} collective-permute-done((bf16[2,7,32,128]{3,2,1,0:T(8,128)(2,1)S(1)}, bf16[2,7,32,128]{3,2,1,0:T(8,128)(2,1)S(1)}, u32[]{:S(2)}, u32[]{:S(2)}) %collective-permute-start.7) | collective-permute-done | bytes 114720 | tf_op jit(solution)/shard_map/ppermute | solution.py:21
  33.2 0.0 copy-start.1
  33.2 1.3 %collective-permute-start.8 = (bf16[1,7,32,128]{3,2,1,0:T(8,128)(2,1)S(1)}, bf16[1,7,32,128]{3,2,1,0:T(8,128)(2,1)S(1)}, u32[]{:S(2)}, u32[]{:S(2)}) collective-permute-start(bf16[1,7,32,128]{3,2,1,0:T(8,128)(2,1)S(1)} %fusion.13), channel_id=1, source_target_pairs={{0,8},{1,3},{2,10},{3,1},{4,12},{5,7},{6,14},{7,5},{8,0},{9,11},{1... | collective-permute-start | bytes 172040 | tf_op jit(solution)/shard_map/ppermute | solution.py:21
  34.5 0.0 collective-permute-done.10
  34.5 0.1 collective-permute-start.11
  34.6 2.0 %collective-permute-done.8 = bf16[1,7,32,128]{3,2,1,0:T(8,128)(2,1)S(1)} collective-permute-done((bf16[1,7,32,128]{3,2,1,0:T(8,128)(2,1)S(1)}, bf16[1,7,32,128]{3,2,1,0:T(8,128)(2,1)S(1)}, u32[]{:S(2)}, u32[]{:S(2)}) %collective-permute-start.8) | collective-permute-done | bytes 57376 | tf_op jit(solution)/shard_map/ppermute | solution.py:21
  36.6 3.8 %collective-permute-done.11 = bf16[1,9,32,128]{3,2,1,0:T(8,128)(2,1)S(1)} collective-permute-done((bf16[1,9,32,128]{3,2,1,0:T(8,128)(2,1)S(1)}, bf16[1,9,32,128]{3,2,1,0:T(8,128)(2,1)S(1)}, u32[]{:S(2)}, u32[]{:S(2)}) %collective-permute-start.11) | collective-permute-done | bytes 73760 | tf_op jit(solution)/shard_map/ppermute | solution.py:21
  40.4 2.7 %collective-permute-start.12 = (bf16[16,32,128]{2,1,0:T(8,128)(2,1)S(1)}, bf16[16,32,128]{2,1,0:T(8,128)(2,1)S(1)}, u32[]{:S(2)}, u32[]{:S(2)}) collective-permute-start(bf16[16,32,128]{2,1,0:T(8,128)(2,1)S(1)} %pad_maximum_fusion.own_ref), channel_id=1, source_target_pairs={{0,1},{1,0},{2,3},{3,2},{4,5},{5,4},{6,7},{7,6},{8,9},{9,8},{10,11... | collective-permute-start | bytes 393224 | tf_op jit(solution)/shard_map/ppermute | solution.py:21
  43.1 2.5 %collective-permute-start.13 = (bf16[16,32,128]{2,1,0:T(8,128)(2,1)S(1)}, bf16[16,32,128]{2,1,0:T(8,128)(2,1)S(1)}, u32[]{:S(2)}, u32[]{:S(2)}) collective-permute-start(bf16[16,32,128]{2,1,0:T(8,128)(2,1)S(1)} %pad_maximum_fusion.own_ref), channel_id=1, source_target_pairs={{1,2},{3,4},{5,6},{7,8},{9,10},{11,12},{13,14},{2,1},{4,3},{6,5},{... | collective-permute-start | bytes 393224 | tf_op jit(solution)/shard_map/ppermute | solution.py:372
  45.7 0.0 copy-done
  45.7 0.6 %shard_map.64.bands_ref = bf16[4352,256]{1,0:T(8,128)(2,1)S(1)} custom-call(f32[33,33]{1,0:T(8,128)S(1)} %copy-done), custom_call_target="tpu_custom_call" | custom-call | tf_op jit(solution)/shard_map/pallas_call | solution.py:308
  46.3 0.0 collective-permute-done.12.beside_ref
  46.3 4.5 %collective-permute-done.13.across_ref = bf16[16,32,128]{2,1,0:T(8,128)(2,1)S(1)} collective-permute-done((bf16[16,32,128]{2,1,0:T(8,128)(2,1)S(1)}, bf16[16,32,128]{2,1,0:T(8,128)(2,1)S(1)}, u32[]{:S(2)}, u32[]{:S(2)}) %collective-permute-start.13) | collective-permute-done | bytes 131104 | tf_op jit(solution)/shard_map/ppermute | solution.py:372
  50.8 0.0 copy-done.1
  50.8 1.5 %shard_map.73 = f32[32,16,128]{2,1,0:T(8,128)} custom-call(bf16[4352,256]{1,0:T(8,128)(2,1)S(1)} %shard_map.64.bands_ref, s32[16,128]{1,0:T(8,128)S(1)} %copy-done.1, bf16[16,32,128]{2,1,0:T(8,128)(2,1)S(1)} %collective-permute-done.12.beside_ref, bf16[16,32,128]{2,1,0:T(8,128)(2,1)S(1)} %collective-permute-done.13.across_ref, ...), custom_call_target="tpu_custom_call" | custom-call | tf_op jit(solution)/shard_map/pallas_call | solution.py:374
  (17 shorter events, 0.2 us)
Async XLA Ops:
  1.9 18.1 %collective-permute-start.5 = (bf16[64,8,16,128]{3,2,1,0:T(8,128)(2,1)S(1)}, bf16[64,8,16,128]{3,2,1,0:T(8,128)(2,1)S(1)}, u32[]{:S(2)}, u32[]{:S(2)}) collective-permute-start(bf16[64,8,16,128]{3,2,1,0:T(8,128)(2,1)S(1)} %get-tuple-element.19), channel_id=1, source_target_pairs={{0,1},{1,0},{2,3},{3,2},{4,5},{5,4},{6,7},{7,6},{8,9},{9,8},{10,11... | collective-permute-start | bytes 6291464 | tf_op jit(solution)/shard_map/ppermute | solution.py:21
  4.3 15.7 %collective-permute-start.4 = (bf16[64,8,16,128]{3,2,1,0:T(8,128)(2,1)S(1)}, bf16[64,8,16,128]{3,2,1,0:T(8,128)(2,1)S(1)}, u32[]{:S(2)}, u32[]{:S(2)}) collective-permute-start(bf16[64,8,16,128]{3,2,1,0:T(8,128)(2,1)S(1)} %get-tuple-element.18), channel_id=1, source_target_pairs={{0,1},{1,0},{2,3},{3,2},{4,5},{5,4},{6,7},{7,6},{8,9},{9,8},{10,11... | collective-permute-start | bytes 6291464 | tf_op jit(solution)/shard_map/ppermute | solution.py:21
  5.9 3.2 %collective-permute-start = (bf16[1,32,128]{2,1,0:T(8,128)(2,1)S(1)}, bf16[1,32,128]{2,1,0:T(8,128)(2,1)S(1)}, u32[]{:S(2)}, u32[]{:S(2)}) collective-permute-start(bf16[1,32,128]{2,1,0:T(8,128)(2,1)S(1)} %shard_map.67), channel_id=1, source_target_pairs={{0,2},{1,3},{2,0},{3,1},{4,6},{5,7},{6,4},{7,5},{8,10},{9,11},{10,... | collective-permute-start | bytes 24584 | tf_op jit(solution)/shard_map/ppermute | solution.py:21
  9.2 2.7 %collective-permute-start.1 = (bf16[2,32,128]{2,1,0:T(8,128)(2,1)S(1)}, bf16[2,32,128]{2,1,0:T(8,128)(2,1)S(1)}, u32[]{:S(2)}, u32[]{:S(2)}) collective-permute-start(bf16[2,32,128]{2,1,0:T(8,128)(2,1)S(1)} %pad_maximum_fusion.3), channel_id=1, source_target_pairs={{0,4},{1,5},{2,6},{3,7},{4,0},{5,1},{6,2},{7,3},{8,12},{9,13},{10,... | collective-permute-start | bytes 49160 | tf_op jit(solution)/shard_map/ppermute | solution.py:21
  11.8 3.9 %collective-permute-start.2 = (bf16[4,32,128]{2,1,0:T(8,128)(2,1)S(1)}, bf16[4,32,128]{2,1,0:T(8,128)(2,1)S(1)}, u32[]{:S(2)}, u32[]{:S(2)}) collective-permute-start(bf16[4,32,128]{2,1,0:T(8,128)(2,1)S(1)} %pad_maximum_fusion.2), channel_id=1, source_target_pairs={{0,8},{1,9},{2,10},{3,11},{4,12},{5,13},{6,14},{7,15},{8,0},{9,1},... | collective-permute-start | bytes 98312 | tf_op jit(solution)/shard_map/ppermute | solution.py:21
  15.7 4.2 %collective-permute-start.3 = (bf16[8,32,128]{2,1,0:T(8,128)(2,1)S(1)}, bf16[8,32,128]{2,1,0:T(8,128)(2,1)S(1)}, u32[]{:S(2)}, u32[]{:S(2)}) collective-permute-start(bf16[8,32,128]{2,1,0:T(8,128)(2,1)S(1)} %pad_maximum_fusion.1), channel_id=1, source_target_pairs={{0,1},{1,0},{2,3},{3,2},{4,5},{5,4},{6,7},{7,6},{8,9},{9,8},{10,11... | collective-permute-start | bytes 196616 | tf_op jit(solution)/shard_map/ppermute | solution.py:21
  21.7 5.6 %collective-permute-start.6 = (bf16[4,7,32,128]{3,2,1,0:T(8,128)(2,1)S(1)}, bf16[4,7,32,128]{3,2,1,0:T(8,128)(2,1)S(1)}, u32[]{:S(2)}, u32[]{:S(2)}) collective-permute-start(bf16[4,7,32,128]{3,2,1,0:T(8,128)(2,1)S(1)} %get-tuple-element.21), channel_id=1, source_target_pairs={{0,2},{1,5},{2,0},{3,7},{4,6},{5,1},{6,4},{7,3},{8,10},{9,13},{10,... | collective-permute-start | bytes 688136 | tf_op jit(solution)/shard_map/ppermute | solution.py:21
  23.2 6.9 %collective-permute-start.9 = (bf16[4,9,32,128]{3,2,1,0:T(8,128)(2,1)S(1)}, bf16[4,9,32,128]{3,2,1,0:T(8,128)(2,1)S(1)}, u32[]{:S(2)}, u32[]{:S(2)}) collective-permute-start(bf16[4,9,32,128]{3,2,1,0:T(8,128)(2,1)S(1)} %get-tuple-element.24), channel_id=1, source_target_pairs={{0,2},{1,5},{2,0},{3,7},{4,6},{5,1},{6,4},{7,3},{8,10},{9,13},{10,... | collective-permute-start | bytes 884744 | tf_op jit(solution)/shard_map/ppermute | solution.py:21
  27.5 18.2 %copy-start = (f32[33,33]{1,0:T(8,128)S(1)}, f32[33,33]{1,0:T(8,128)}, u32[]{:S(2)}) copy-start(f32[33,33]{1,0:T(8,128)} %kernel_ref.1) | copy-start | bytes 13072
  27.5 5.7 %collective-permute-start.7 = (bf16[2,7,32,128]{3,2,1,0:T(8,128)(2,1)S(1)}, bf16[2,7,32,128]{3,2,1,0:T(8,128)(2,1)S(1)}, u32[]{:S(2)}, u32[]{:S(2)}) collective-permute-start(bf16[2,7,32,128]{3,2,1,0:T(8,128)(2,1)S(1)} %fusion.7), channel_id=1, source_target_pairs={{0,4},{1,9},{2,6},{3,11},{4,0},{5,13},{6,2},{7,15},{8,12},{9,1},{1... | collective-permute-start | bytes 344072 | tf_op jit(solution)/shard_map/ppermute | solution.py:21
  30.2 4.2 %collective-permute-start.10 = (bf16[2,9,32,128]{3,2,1,0:T(8,128)(2,1)S(1)}, bf16[2,9,32,128]{3,2,1,0:T(8,128)(2,1)S(1)}, u32[]{:S(2)}, u32[]{:S(2)}) collective-permute-start(bf16[2,9,32,128]{3,2,1,0:T(8,128)(2,1)S(1)} %fusion.4), channel_id=1, source_target_pairs={{0,4},{1,3},{2,6},{3,1},{4,0},{5,7},{6,2},{7,5},{8,12},{9,11},{10,... | collective-permute-start | bytes 442376 | tf_op jit(solution)/shard_map/ppermute | solution.py:21
  33.2 17.7 %copy-start.1 = (s32[16,128]{1,0:T(8,128)S(1)}, s32[16,128]{1,0:T(8,128)}, u32[]{:S(2)}) copy-start(s32[16,128]{1,0:T(8,128)} %mask_ref.1) | copy-start | bytes 24580
  33.2 3.4 %collective-permute-start.8 = (bf16[1,7,32,128]{3,2,1,0:T(8,128)(2,1)S(1)}, bf16[1,7,32,128]{3,2,1,0:T(8,128)(2,1)S(1)}, u32[]{:S(2)}, u32[]{:S(2)}) collective-permute-start(bf16[1,7,32,128]{3,2,1,0:T(8,128)(2,1)S(1)} %fusion.13), channel_id=1, source_target_pairs={{0,8},{1,3},{2,10},{3,1},{4,12},{5,7},{6,14},{7,5},{8,0},{9,11},{1... | collective-permute-start | bytes 172040 | tf_op jit(solution)/shard_map/ppermute | solution.py:21
  34.5 5.8 %collective-permute-start.11 = (bf16[1,9,32,128]{3,2,1,0:T(8,128)(2,1)S(1)}, bf16[1,9,32,128]{3,2,1,0:T(8,128)(2,1)S(1)}, u32[]{:S(2)}, u32[]{:S(2)}) collective-permute-start(bf16[1,9,32,128]{3,2,1,0:T(8,128)(2,1)S(1)} %fusion.11), channel_id=1, source_target_pairs={{0,8},{1,9},{2,10},{3,11},{4,12},{5,13},{6,14},{7,15},{8,0},{9,1},... | collective-permute-start | bytes 221192 | tf_op jit(solution)/shard_map/ppermute | solution.py:21
  40.4 5.9 %collective-permute-start.12 = (bf16[16,32,128]{2,1,0:T(8,128)(2,1)S(1)}, bf16[16,32,128]{2,1,0:T(8,128)(2,1)S(1)}, u32[]{:S(2)}, u32[]{:S(2)}) collective-permute-start(bf16[16,32,128]{2,1,0:T(8,128)(2,1)S(1)} %pad_maximum_fusion.own_ref), channel_id=1, source_target_pairs={{0,1},{1,0},{2,3},{3,2},{4,5},{5,4},{6,7},{7,6},{8,9},{9,8},{10,11... | collective-permute-start | bytes 393224 | tf_op jit(solution)/shard_map/ppermute | solution.py:21
  43.1 7.7 %collective-permute-start.13 = (bf16[16,32,128]{2,1,0:T(8,128)(2,1)S(1)}, bf16[16,32,128]{2,1,0:T(8,128)(2,1)S(1)}, u32[]{:S(2)}, u32[]{:S(2)}) collective-permute-start(bf16[16,32,128]{2,1,0:T(8,128)(2,1)S(1)} %pad_maximum_fusion.own_ref), channel_id=1, source_target_pairs={{1,2},{3,4},{5,6},{7,8},{9,10},{11,12},{13,14},{2,1},{4,3},{6,5},{... | collective-permute-start | bytes 393224 | tf_op jit(solution)/shard_map/ppermute | solution.py:372

commit v9 on v8

--- a/solution.py
+++ b/solution.py
@@ -94,10 +94,18 @@
     load(green_ref, own_ref, semaphore, first, lax.axis_index("space") & 1).wait()
 
 
-def widen(chosen_ref, repeat_ref, slip_ref, wide_ref):
+def pick(slip_ref, chosen):
+    slip = jnp.concatenate([slip_ref[owner] for owner in range(slip_ref.shape[0])], axis=1)
+    return jnp.dot(slip, chosen, preferred_element_type=jnp.float32)
+
+
+def early_kernel(chosen_ref, slip_ref, early_ref):
+    early_ref[...] = pick(slip_ref, chosen_ref[: chosen_ref.shape[0] // 2, :])
+
+
+def widen(chosen_ref, repeat_ref, slip_ref, early_ref, wide_ref):
     group, depth = repeat_ref.shape
-    slip = jnp.concatenate([slip_ref[owner] for owner in range(slip_ref.shape[0])], axis=1)
-    picked = jnp.dot(slip, chosen_ref[...], preferred_element_type=jnp.float32)
+    picked = early_ref[...] + pick(slip_ref, chosen_ref[chosen_ref.shape[0] // 2 :, :])
     picked = picked.astype(jnp.bfloat16)
     for side in range(2):
         wide_ref[:, side * depth : (side + 1) * depth] = jnp.dot(
@@ -117,9 +125,9 @@
         ).astype(jnp.bfloat16)
 
 
-def first_kernel(places, rows, chosen_ref, repeat_ref, slip_ref, *refs):
+def first_kernel(places, rows, chosen_ref, repeat_ref, slip_ref, early_ref, *refs):
     parts, (out_ref, spread_ref, wide_ref) = refs[:-3], refs[-3:]
-    widen(chosen_ref, repeat_ref, slip_ref, wide_ref)
+    widen(chosen_ref, repeat_ref, slip_ref, early_ref, wide_ref)
     fill_spread(rows, 0, wide_ref, spread_ref)
     uplift_kernel(places, 0, spread_ref, *parts, out_ref)
 
@@ -260,9 +268,10 @@
         pltpu.with_memory_space_constraint(coefficients, pltpu.HBM),
         pltpu.with_memory_space_constraint(kl_modes, pltpu.HBM),
     )
-    for level in (*range(1, levels), 0):
+    for level in range(1, levels):
         arrived = swap(slip, 1 << level)
         slip = jnp.concatenate([slip, arrived], axis=0)
+    last_slip = swap(slip, 1)
 
     def part(depth):
         return jax.ShapeDtypeStruct((depth, count // 2, rows, width), green.dtype)
@@ -314,6 +323,13 @@
     )(kernel)
 
     cuts = [0, rows * 7 // 16, rows]
+    early = pl.pallas_call(
+        early_kernel,
+        out_shape=jax.ShapeDtypeStruct((realizations, 2 * group), jnp.float32),
+        in_specs=[VMEM] * 2,
+        out_specs=VMEM,
+        compiler_params=PARAMS,
+    )(chosen, slip)
     wide = []
 
     def away_blocks(stream):
@@ -327,10 +343,10 @@
             sent, spread, table = pl.pallas_call(
                 functools.partial(first_kernel, places[1::2], rows),
                 out_shape=(*shapes, jax.ShapeDtypeStruct((realizations, sides), jnp.float32)),
-                in_specs=[VMEM] * (3 + len(parts)),
+                in_specs=[VMEM] * (4 + len(parts)),
                 out_specs=(VMEM, VMEM, VMEM),
                 compiler_params=PARAMS,
-            )(chosen, repeat, slip, *parts)
+            )(chosen, repeat, last_slip, early, *parts)
             wide.append(table)
             return sent, spread
         return pl.pallas_call(

time: 52.6 us -> 53.2 us (1.011)
  the two profiles are of different devices: /device:TPU:27 before, /device:TPU:25 now
where the time goes in v9:
time: 53.2 us; the launch traced here: 53 us
  waiting for transfers between devices  21.4 us (40%)
  starting transfers between devices  16.1 us (30%)
  Pallas kernels  14.9 us (28%)
    ppermute x13, waiting for transfers between devices, swap(): lax.ppermute(block, 'space', [(i, i ^ bits[i & 1]) for i in range(count)])  17.2 us
    ppermute x13, starting transfers between devices, swap(): lax.ppermute(block, 'space', [(i, i ^ bits[i & 1]) for i in range(count)])  13.4 us
    ppermute x1, waiting for transfers between devices, body(): across = lax.ppermute(seafloor, 'space', crossing)  4.27 us
    ppermute x1, starting transfers between devices, body(): across = lax.ppermute(seafloor, 'space', crossing)  2.78 us
    pallas_call x2, Pallas kernels, uplift_blocks(): pl.pallas_call(functools.partial(uplift_kernel, places, stream), out_shap...  2.58 us
    pallas_call x1, Pallas kernels, body(): pl.pallas_call(rest_kernel, out_shape=part(group - group // 4), in_specs=...  1.9 us
    pallas_call x1, Pallas kernels, body(): pl.pallas_call(functools.partial(repeat_kernel, rows), out_shape=(part(gr...  1.88 us
    pallas_call x1, Pallas kernels, body(): pl.pallas_call(functools.partial(choose_kernel, columns, levels), out_sha...  1.62 us
  transfers between devices with their start and end apart: 14, of which 8 were waited for; matrix products, arithmetic and copies ran while one was open for 1% of the time, Pallas kernels for 19%

profile of v9, /device:TPU:25, one launch (start us, length us, event | category | flops | bytes accessed | tf_op | source)
XLA Modules:
  0.0 53.0 jit_solution(237160044909248164)
XLA Ops:
  0.0 1.9 %shard_map.66 = (bf16[64,8,16,128]{3,2,1,0:T(8,128)(2,1)S(1)}, bf16[32,8,16,128]{3,2,1,0:T(8,128)(2,1)S(1)}, bf16[128,2048]{1,0:T(8,128)(2,1)S(1)}) custom-call(bf16[128,8,2,16,128]{4,3,2,1,0:T(8,128)(2,1)} %bitcast.48), custom_call_target="tpu_custom_call" | custom-call | tf_op jit(solution)/shard_map/pallas_call | solution.py:295
  1.9 0.7 %collective-permute-start.5 = (bf16[64,8,16,128]{3,2,1,0:T(8,128)(2,1)S(1)}, bf16[64,8,16,128]{3,2,1,0:T(8,128)(2,1)S(1)}, u32[]{:S(2)}, u32[]{:S(2)}) collective-permute-start(bf16[64,8,16,128]{3,2,1,0:T(8,128)(2,1)S(1)} %get-tuple-element.19), channel_id=1, source_target_pairs={{0,1},{1,0},{2,3},{3,2},{4,5},{5,4},{6,7},{7,6},{8,9},{9,8},{10,11... | collective-permute-start | bytes 6291464 | tf_op jit(solution)/shard_map/ppermute | solution.py:21
  2.6 1.6 %shard_map.65 = (bf16[64,8,16,128]{3,2,1,0:T(8,128)(2,1)S(1)}, bf16[2048,256]{1,0:T(8,128)(2,1)S(1)}) custom-call(s32[16,128]{1,0:T(8,128)} %bitcast.55, bf16[128,8,2,16,128]{4,3,2,1,0:T(8,128)(2,1)} %bitcast.49), custom_call_target="tpu_custom_call" | custom-call | tf_op jit(solution)/shard_map/pallas_call | solution.py:280
  4.3 0.1 collective-permute-start.4
  4.3 1.6 %shard_map.67 = bf16[1,32,128]{2,1,0:T(8,128)(2,1)S(1)} custom-call(bf16[32,4096]{1,0:T(8,128)(2,1)} %coefficients_hbm.1, bf16[4096,128]{1,0:T(8,128)(2,1)} %modes_hbm.1), custom_call_target="tpu_custom_call" | custom-call | tf_op jit(solution)/shard_map/pallas_call | solution.py:256
  5.9 1.3 %collective-permute-start = (bf16[1,32,128]{2,1,0:T(8,128)(2,1)S(1)}, bf16[1,32,128]{2,1,0:T(8,128)(2,1)S(1)}, u32[]{:S(2)}, u32[]{:S(2)}) collective-permute-start(bf16[1,32,128]{2,1,0:T(8,128)(2,1)S(1)} %shard_map.67), channel_id=1, source_target_pairs={{0,2},{1,3},{2,0},{3,1},{4,6},{5,7},{6,4},{7,5},{8,10},{9,11},{10,... | collective-permute-start | bytes 24584 | tf_op jit(solution)/shard_map/ppermute | solution.py:21
  7.2 1.3 %collective-permute-done = bf16[1,32,128]{2,1,0:T(8,128)(2,1)S(1)} collective-permute-done((bf16[1,32,128]{2,1,0:T(8,128)(2,1)S(1)}, bf16[1,32,128]{2,1,0:T(8,128)(2,1)S(1)}, u32[]{:S(2)}, u32[]{:S(2)}) %collective-permute-start) | collective-permute-done | bytes 8224 | tf_op jit(solution)/shard_map/ppermute | solution.py:21
  8.5 0.2 collective-permute-start.1
  8.7 2.4 %collective-permute-done.1 = bf16[2,32,128]{2,1,0:T(8,128)(2,1)S(1)} collective-permute-done((bf16[2,32,128]{2,1,0:T(8,128)(2,1)S(1)}, bf16[2,32,128]{2,1,0:T(8,128)(2,1)S(1)}, u32[]{:S(2)}, u32[]{:S(2)}) %collective-permute-start.1) | collective-permute-done | bytes 16416 | tf_op jit(solution)/shard_map/ppermute | solution.py:21
  11.1 0.1 collective-permute-start.2
  11.2 3.8 %collective-permute-done.2 = bf16[4,32,128]{2,1,0:T(8,128)(2,1)S(1)} collective-permute-done((bf16[4,32,128]{2,1,0:T(8,128)(2,1)S(1)}, bf16[4,32,128]{2,1,0:T(8,128)(2,1)S(1)}, u32[]{:S(2)}, u32[]{:S(2)}) %collective-permute-start.2) | collective-permute-done | bytes 32800 | tf_op jit(solution)/shard_map/ppermute | solution.py:21
  15.0 4.0 %collective-permute-start.3 = (bf16[8,32,128]{2,1,0:T(8,128)(2,1)S(1)}, bf16[8,32,128]{2,1,0:T(8,128)(2,1)S(1)}, u32[]{:S(2)}, u32[]{:S(2)}) collective-permute-start(bf16[8,32,128]{2,1,0:T(8,128)(2,1)S(1)} %pad_maximum_fusion.1.slip_ref), channel_id=1, source_target_pairs={{0,1},{1,0},{2,3},{3,2},{4,5},{5,4},{6,7},{7,6},{8,9},{9,8},{10,11... | collective-permute-start | bytes 196616 | tf_op jit(solution)/shard_map/ppermute | solution.py:21
  19.0 1.9 %shard_map.69.refs_1_ = bf16[96,8,16,128]{3,2,1,0:T(8,128)(2,1)S(1)} custom-call(bf16[128,8,2,16,128]{4,3,2,1,0:T(8,128)(2,1)} %bitcast.50), custom_call_target="tpu_custom_call" | custom-call | tf_op jit(solution)/shard_map/pallas_call | solution.py:308
  20.9 0.2 shard_map.68.early_ref
  21.1 0.0 collective-permute-done.3.slip_ref
  21.1 0.0 collective-permute-done.5.refs_3_
  21.1 0.0 collective-permute-done.4.refs_2_
  21.2 1.6 %shard_map.70 = (bf16[4,7,32,128]{3,2,1,0:T(8,128)(2,1)S(1)}, bf16[224,4096]{1,0:T(8,128)(2,1)S(1)}, f32[32,4096]{1,0:T(8,128)S(1)}) custom-call(bf16[2048,256]{1,0:T(8,128)(2,1)S(1)} %get-tuple-element.15.chosen_ref, bf16[128,2048]{1,0:T(8,128)(2,1)S(1)} %get-tuple-element.16.repeat_ref, bf16[8,32,128]{2,1,0:T(8,128)(2,1)S(1)} %collective-permute-done.3.slip_ref, ...), custom_call_target="tpu_custom_call" | custom-call | tf_op jit(solution)/shard_map/pallas_call | solution.py:343
  22.8 0.1 collective-permute-start.6
  22.8 1.4 %shard_map.72 = (bf16[4,9,32,128]{3,2,1,0:T(8,128)(2,1)S(1)}, bf16[288,4096]{1,0:T(8,128)(2,1)S(1)}) custom-call(f32[32,4096]{1,0:T(8,128)S(1)} %get-tuple-element.22.wide_ref, bf16[32,8,16,128]{3,2,1,0:T(8,128)(2,1)S(1)} %get-tuple-element.17.refs_0_, bf16[96,8,16,128]{3,2,1,0:T(8,128)(2,1)S(1)} %shard_map.69.refs_1_, ...), custom_call_target="tpu_custom_call" | custom-call | tf_op jit(solution)/shard_map/pallas_call | solution.py:352
  24.2 1.5 %collective-permute-start.9 = (bf16[4,9,32,128]{3,2,1,0:T(8,128)(2,1)S(1)}, bf16[4,9,32,128]{3,2,1,0:T(8,128)(2,1)S(1)}, u32[]{:S(2)}, u32[]{:S(2)}) collective-permute-start(bf16[4,9,32,128]{3,2,1,0:T(8,128)(2,1)S(1)} %get-tuple-element.24), channel_id=1, source_target_pairs={{0,2},{1,5},{2,0},{3,7},{4,6},{5,1},{6,4},{7,3},{8,10},{9,13},{10,... | collective-permute-start | bytes 884744 | tf_op jit(solution)/shard_map/ppermute | solution.py:21
  25.8 1.2 %shard_map.71 = f32[4,7,32,128]{3,2,1,0:T(8,128)S(1)} custom-call(bf16[224,4096]{1,0:T(8,128)(2,1)S(1)} %get-tuple-element.20.spread_ref, bf16[32,8,16,128]{3,2,1,0:T(8,128)(2,1)S(1)} %get-tuple-element.17.refs_0_, bf16[96,8,16,128]{3,2,1,0:T(8,128)(2,1)S(1)} %shard_map.69.refs_1_, bf16[64,8,16,128]{3,2,1,0:T(8,128)(2,1)S(1)} %collective-permute-done.4.refs_2_, ...), custom_call_target="tpu_custom_call" | custom-call | tf_op jit(solution)/shard_map/pallas_call | solution.py:173
  26.9 1.4 %shard_map.73 = f32[4,9,32,128]{3,2,1,0:T(8,128)S(1)} custom-call(bf16[288,4096]{1,0:T(8,128)(2,1)S(1)} %get-tuple-element.23.spread_ref, bf16[32,8,16,128]{3,2,1,0:T(8,128)(2,1)S(1)} %get-tuple-element.17.refs_0_, bf16[96,8,16,128]{3,2,1,0:T(8,128)(2,1)S(1)} %shard_map.69.refs_1_, bf16[64,8,16,128]{3,2,1,0:T(8,128)(2,1)S(1)} %collective-permute-done.4.refs_2_, ...), custom_call_target="tpu_custom_call" | custom-call | tf_op jit(solution)/shard_map/pallas_call | solution.py:173
  28.4 0.0 collective-permute-done.6
  28.4 0.1 convert_add_fusion.1
  28.5 0.0 copy-start
  28.5 0.1 collective-permute-start.7
  28.6 2.6 %collective-permute-done.9 = bf16[4,9,32,128]{3,2,1,0:T(8,128)(2,1)S(1)} collective-permute-done((bf16[4,9,32,128]{3,2,1,0:T(8,128)(2,1)S(1)}, bf16[4,9,32,128]{3,2,1,0:T(8,128)(2,1)S(1)}, u32[]{:S(2)}, u32[]{:S(2)}) %collective-permute-start.9) | collective-permute-done | bytes 294944 | tf_op jit(solution)/shard_map/ppermute | solution.py:21
  31.1 0.1 convert_add_fusion
  31.3 1.3 %collective-permute-start.10 = (bf16[2,9,32,128]{3,2,1,0:T(8,128)(2,1)S(1)}, bf16[2,9,32,128]{3,2,1,0:T(8,128)(2,1)S(1)}, u32[]{:S(2)}, u32[]{:S(2)}) collective-permute-start(bf16[2,9,32,128]{3,2,1,0:T(8,128)(2,1)S(1)} %fusion.4), channel_id=1, source_target_pairs={{0,4},{1,3},{2,6},{3,1},{4,0},{5,7},{6,2},{7,5},{8,12},{9,11},{10,... | collective-permute-start | bytes 442376 | tf_op jit(solution)/shard_map/ppermute | solution.py:21
  32.6 1.7 %collective-permute-done.7 = bf16[2,7,32,128]{3,2,1,0:T(8,128)(2,1)S(1)} collective-permute-done((bf16[2,7,32,128]{3,2,1,0:T(8,128)(2,1)S(1)}, bf16[2,7,32,128]{3,2,1,0:T(8,128)(2,1)S(1)}, u32[]{:S(2)}, u32[]{:S(2)}) %collective-permute-start.7) | collective-permute-done | bytes 114720 | tf_op jit(solution)/shard_map/ppermute | solution.py:21
  34.3 0.0 copy-start.1
  34.3 1.3 %collective-permute-start.8 = (bf16[1,7,32,128]{3,2,1,0:T(8,128)(2,1)S(1)}, bf16[1,7,32,128]{3,2,1,0:T(8,128)(2,1)S(1)}, u32[]{:S(2)}, u32[]{:S(2)}) collective-permute-start(bf16[1,7,32,128]{3,2,1,0:T(8,128)(2,1)S(1)} %fusion.13), channel_id=1, source_target_pairs={{0,8},{1,3},{2,10},{3,1},{4,12},{5,7},{6,14},{7,5},{8,0},{9,11},{1... | collective-permute-start | bytes 172040 | tf_op jit(solution)/shard_map/ppermute | solution.py:21
  35.6 0.0 collective-permute-done.10
  35.7 0.1 collective-permute-start.11
  35.8 1.7 %collective-permute-done.8 = bf16[1,7,32,128]{3,2,1,0:T(8,128)(2,1)S(1)} collective-permute-done((bf16[1,7,32,128]{3,2,1,0:T(8,128)(2,1)S(1)}, bf16[1,7,32,128]{3,2,1,0:T(8,128)(2,1)S(1)}, u32[]{:S(2)}, u32[]{:S(2)}) %collective-permute-start.8) | collective-permute-done | bytes 57376 | tf_op jit(solution)/shard_map/ppermute | solution.py:21
  37.5 3.7 %collective-permute-done.11 = bf16[1,9,32,128]{3,2,1,0:T(8,128)(2,1)S(1)} collective-permute-done((bf16[1,9,32,128]{3,2,1,0:T(8,128)(2,1)S(1)}, bf16[1,9,32,128]{3,2,1,0:T(8,128)(2,1)S(1)}, u32[]{:S(2)}, u32[]{:S(2)}) %collective-permute-start.11) | collective-permute-done | bytes 73760 | tf_op jit(solution)/shard_map/ppermute | solution.py:21
  41.2 2.6 %collective-permute-start.12 = (bf16[16,32,128]{2,1,0:T(8,128)(2,1)S(1)}, bf16[16,32,128]{2,1,0:T(8,128)(2,1)S(1)}, u32[]{:S(2)}, u32[]{:S(2)}) collective-permute-start(bf16[16,32,128]{2,1,0:T(8,128)(2,1)S(1)} %pad_maximum_fusion.own_ref), channel_id=1, source_target_pairs={{0,1},{1,0},{2,3},{3,2},{4,5},{5,4},{6,7},{7,6},{8,9},{9,8},{10,11... | collective-permute-start | bytes 393224 | tf_op jit(solution)/shard_map/ppermute | solution.py:21
  43.8 2.8 %collective-permute-start.13 = (bf16[16,32,128]{2,1,0:T(8,128)(2,1)S(1)}, bf16[16,32,128]{2,1,0:T(8,128)(2,1)S(1)}, u32[]{:S(2)}, u32[]{:S(2)}) collective-permute-start(bf16[16,32,128]{2,1,0:T(8,128)(2,1)S(1)} %pad_maximum_fusion.own_ref), channel_id=1, source_target_pairs={{1,2},{3,4},{5,6},{7,8},{9,10},{11,12},{13,14},{2,1},{4,3},{6,5},{... | collective-permute-start | bytes 393224 | tf_op jit(solution)/shard_map/ppermute | solution.py:388
  46.6 0.0 copy-done
  46.6 0.6 %shard_map.64.bands_ref = bf16[4352,256]{1,0:T(8,128)(2,1)S(1)} custom-call(f32[33,33]{1,0:T(8,128)S(1)} %copy-done), custom_call_target="tpu_custom_call" | custom-call | tf_op jit(solution)/shard_map/pallas_call | solution.py:317
  47.2 0.0 collective-permute-done.12.beside_ref
  47.2 4.3 %collective-permute-done.13.across_ref = bf16[16,32,128]{2,1,0:T(8,128)(2,1)S(1)} collective-permute-done((bf16[16,32,128]{2,1,0:T(8,128)(2,1)S(1)}, bf16[16,32,128]{2,1,0:T(8,128)(2,1)S(1)}, u32[]{:S(2)}, u32[]{:S(2)}) %collective-permute-start.13) | collective-permute-done | bytes 131104 | tf_op jit(solution)/shard_map/ppermute | solution.py:388
  51.5 0.0 copy-done.1
  51.5 1.5 %shard_map.74 = f32[32,16,128]{2,1,0:T(8,128)} custom-call(bf16[4352,256]{1,0:T(8,128)(2,1)S(1)} %shard_map.64.bands_ref, s32[16,128]{1,0:T(8,128)S(1)} %copy-done.1, bf16[16,32,128]{2,1,0:T(8,128)(2,1)S(1)} %collective-permute-done.12.beside_ref, bf16[16,32,128]{2,1,0:T(8,128)(2,1)S(1)} %collective-permute-done.13.across_ref, ...), custom_call_target="tpu_custom_call" | custom-call | tf_op jit(solution)/shard_map/pallas_call | solution.py:390
  (12 shorter events, 0.2 us)
Async XLA Ops:
  1.9 19.2 %collective-permute-start.5 = (bf16[64,8,16,128]{3,2,1,0:T(8,128)(2,1)S(1)}, bf16[64,8,16,128]{3,2,1,0:T(8,128)(2,1)S(1)}, u32[]{:S(2)}, u32[]{:S(2)}) collective-permute-start(bf16[64,8,16,128]{3,2,1,0:T(8,128)(2,1)S(1)} %get-tuple-element.19), channel_id=1, source_target_pairs={{0,1},{1,0},{2,3},{3,2},{4,5},{5,4},{6,7},{7,6},{8,9},{9,8},{10,11... | collective-permute-start | bytes 6291464 | tf_op jit(solution)/shard_map/ppermute | solution.py:21
  4.3 16.9 %collective-permute-start.4 = (bf16[64,8,16,128]{3,2,1,0:T(8,128)(2,1)S(1)}, bf16[64,8,16,128]{3,2,1,0:T(8,128)(2,1)S(1)}, u32[]{:S(2)}, u32[]{:S(2)}) collective-permute-start(bf16[64,8,16,128]{3,2,1,0:T(8,128)(2,1)S(1)} %get-tuple-element.18), channel_id=1, source_target_pairs={{0,1},{1,0},{2,3},{3,2},{4,5},{5,4},{6,7},{7,6},{8,9},{9,8},{10,11... | collective-permute-start | bytes 6291464 | tf_op jit(solution)/shard_map/ppermute | solution.py:21
  5.9 2.6 %collective-permute-start = (bf16[1,32,128]{2,1,0:T(8,128)(2,1)S(1)}, bf16[1,32,128]{2,1,0:T(8,128)(2,1)S(1)}, u32[]{:S(2)}, u32[]{:S(2)}) collective-permute-start(bf16[1,32,128]{2,1,0:T(8,128)(2,1)S(1)} %shard_map.67), channel_id=1, source_target_pairs={{0,2},{1,3},{2,0},{3,1},{4,6},{5,7},{6,4},{7,5},{8,10},{9,11},{10,... | collective-permute-start | bytes 24584 | tf_op jit(solution)/shard_map/ppermute | solution.py:21
  8.5 2.6 %collective-permute-start.1 = (bf16[2,32,128]{2,1,0:T(8,128)(2,1)S(1)}, bf16[2,32,128]{2,1,0:T(8,128)(2,1)S(1)}, u32[]{:S(2)}, u32[]{:S(2)}) collective-permute-start(bf16[2,32,128]{2,1,0:T(8,128)(2,1)S(1)} %pad_maximum_fusion.3), channel_id=1, source_target_pairs={{0,4},{1,5},{2,6},{3,7},{4,0},{5,1},{6,2},{7,3},{8,12},{9,13},{10,... | collective-permute-start | bytes 49160 | tf_op jit(solution)/shard_map/ppermute | solution.py:21
  11.1 3.9 %collective-permute-start.2 = (bf16[4,32,128]{2,1,0:T(8,128)(2,1)S(1)}, bf16[4,32,128]{2,1,0:T(8,128)(2,1)S(1)}, u32[]{:S(2)}, u32[]{:S(2)}) collective-permute-start(bf16[4,32,128]{2,1,0:T(8,128)(2,1)S(1)} %pad_maximum_fusion.2), channel_id=1, source_target_pairs={{0,8},{1,9},{2,10},{3,11},{4,12},{5,13},{6,14},{7,15},{8,0},{9,1},... | collective-permute-start | bytes 98312 | tf_op jit(solution)/shard_map/ppermute | solution.py:21
  15.0 6.1 %collective-permute-start.3 = (bf16[8,32,128]{2,1,0:T(8,128)(2,1)S(1)}, bf16[8,32,128]{2,1,0:T(8,128)(2,1)S(1)}, u32[]{:S(2)}, u32[]{:S(2)}) collective-permute-start(bf16[8,32,128]{2,1,0:T(8,128)(2,1)S(1)} %pad_maximum_fusion.1.slip_ref), channel_id=1, source_target_pairs={{0,1},{1,0},{2,3},{3,2},{4,5},{5,4},{6,7},{7,6},{8,9},{9,8},{10,11... | collective-permute-start | bytes 196616 | tf_op jit(solution)/shard_map/ppermute | solution.py:21
  22.8 5.6 %collective-permute-start.6 = (bf16[4,7,32,128]{3,2,1,0:T(8,128)(2,1)S(1)}, bf16[4,7,32,128]{3,2,1,0:T(8,128)(2,1)S(1)}, u32[]{:S(2)}, u32[]{:S(2)}) collective-permute-start(bf16[4,7,32,128]{3,2,1,0:T(8,128)(2,1)S(1)} %get-tuple-element.21), channel_id=1, source_target_pairs={{0,2},{1,5},{2,0},{3,7},{4,6},{5,1},{6,4},{7,3},{8,10},{9,13},{10,... | collective-permute-start | bytes 688136 | tf_op jit(solution)/shard_map/ppermute | solution.py:21
  24.2 6.9 %collective-permute-start.9 = (bf16[4,9,32,128]{3,2,1,0:T(8,128)(2,1)S(1)}, bf16[4,9,32,128]{3,2,1,0:T(8,128)(2,1)S(1)}, u32[]{:S(2)}, u32[]{:S(2)}) collective-permute-start(bf16[4,9,32,128]{3,2,1,0:T(8,128)(2,1)S(1)} %get-tuple-element.24), channel_id=1, source_target_pairs={{0,2},{1,5},{2,0},{3,7},{4,6},{5,1},{6,4},{7,3},{8,10},{9,13},{10,... | collective-permute-start | bytes 884744 | tf_op jit(solution)/shard_map/ppermute | solution.py:21
  28.5 18.1 %copy-start = (f32[33,33]{1,0:T(8,128)S(1)}, f32[33,33]{1,0:T(8,128)}, u32[]{:S(2)}) copy-start(f32[33,33]{1,0:T(8,128)} %kernel_ref.1) | copy-start | bytes 13072
  28.5 5.7 %collective-permute-start.7 = (bf16[2,7,32,128]{3,2,1,0:T(8,128)(2,1)S(1)}, bf16[2,7,32,128]{3,2,1,0:T(8,128)(2,1)S(1)}, u32[]{:S(2)}, u32[]{:S(2)}) collective-permute-start(bf16[2,7,32,128]{3,2,1,0:T(8,128)(2,1)S(1)} %fusion.7), channel_id=1, source_target_pairs={{0,4},{1,9},{2,6},{3,11},{4,0},{5,13},{6,2},{7,15},{8,12},{9,1},{1... | collective-permute-start | bytes 344072 | tf_op jit(solution)/shard_map/ppermute | solution.py:21
  31.3 4.4 %collective-permute-start.10 = (bf16[2,9,32,128]{3,2,1,0:T(8,128)(2,1)S(1)}, bf16[2,9,32,128]{3,2,1,0:T(8,128)(2,1)S(1)}, u32[]{:S(2)}, u32[]{:S(2)}) collective-permute-start(bf16[2,9,32,128]{3,2,1,0:T(8,128)(2,1)S(1)} %fusion.4), channel_id=1, source_target_pairs={{0,4},{1,3},{2,6},{3,1},{4,0},{5,7},{6,2},{7,5},{8,12},{9,11},{10,... | collective-permute-start | bytes 442376 | tf_op jit(solution)/shard_map/ppermute | solution.py:21
  34.3 17.3 %copy-start.1 = (s32[16,128]{1,0:T(8,128)S(1)}, s32[16,128]{1,0:T(8,128)}, u32[]{:S(2)}) copy-start(s32[16,128]{1,0:T(8,128)} %mask_ref.1) | copy-start | bytes 24580
  34.3 3.2 %collective-permute-start.8 = (bf16[1,7,32,128]{3,2,1,0:T(8,128)(2,1)S(1)}, bf16[1,7,32,128]{3,2,1,0:T(8,128)(2,1)S(1)}, u32[]{:S(2)}, u32[]{:S(2)}) collective-permute-start(bf16[1,7,32,128]{3,2,1,0:T(8,128)(2,1)S(1)} %fusion.13), channel_id=1, source_target_pairs={{0,8},{1,3},{2,10},{3,1},{4,12},{5,7},{6,14},{7,5},{8,0},{9,11},{1... | collective-permute-start | bytes 172040 | tf_op jit(solution)/shard_map/ppermute | solution.py:21
  35.7 5.5 %collective-permute-start.11 = (bf16[1,9,32,128]{3,2,1,0:T(8,128)(2,1)S(1)}, bf16[1,9,32,128]{3,2,1,0:T(8,128)(2,1)S(1)}, u32[]{:S(2)}, u32[]{:S(2)}) collective-permute-start(bf16[1,9,32,128]{3,2,1,0:T(8,128)(2,1)S(1)} %fusion.11), channel_id=1, source_target_pairs={{0,8},{1,9},{2,10},{3,11},{4,12},{5,13},{6,14},{7,15},{8,0},{9,1},... | collective-permute-start | bytes 221192 | tf_op jit(solution)/shard_map/ppermute | solution.py:21
  41.2 6.0 %collective-permute-start.12 = (bf16[16,32,128]{2,1,0:T(8,128)(2,1)S(1)}, bf16[16,32,128]{2,1,0:T(8,128)(2,1)S(1)}, u32[]{:S(2)}, u32[]{:S(2)}) collective-permute-start(bf16[16,32,128]{2,1,0:T(8,128)(2,1)S(1)} %pad_maximum_fusion.own_ref), channel_id=1, source_target_pairs={{0,1},{1,0},{2,3},{3,2},{4,5},{5,4},{6,7},{7,6},{8,9},{9,8},{10,11... | collective-permute-start | bytes 393224 | tf_op jit(solution)/shard_map/ppermute | solution.py:21
  43.8 7.7 %collective-permute-start.13 = (bf16[16,32,128]{2,1,0:T(8,128)(2,1)S(1)}, bf16[16,32,128]{2,1,0:T(8,128)(2,1)S(1)}, u32[]{:S(2)}, u32[]{:S(2)}) collective-permute-start(bf16[16,32,128]{2,1,0:T(8,128)(2,1)S(1)} %pad_maximum_fusion.own_ref), channel_id=1, source_target_pairs={{1,2},{3,4},{5,6},{7,8},{9,10},{11,12},{13,14},{2,1},{4,3},{6,5},{... | collective-permute-start | bytes 393224 | tf_op jit(solution)/shard_map/ppermute | solution.py:388
